TPU v7x, 32 devices: a whole 2x2x4 slice. The times are simulated.
32 devices in a mesh: rep: 4 (over y, x), fsdp: 8 (over z, core).
Axes of the slice: x: 2, y: 2, z: 4, core: 2. Of those that a mesh axis runs over, the one named last changes fastest.
Arguments:
- tokens: bfloat16 [8192, 2048], P(('rep', 'fsdp')), may hold values from -6 to 6
- layer_input: bfloat16 [8192, 256], P(('rep', 'fsdp')), may hold values from -6 to 6
- cotangent: bfloat16 [8192, 2048], P(('rep', 'fsdp')), may hold values from -6 to 6
- norm_gains: float32 [6, 2048], P(None, 'fsdp'), may hold values from 0.1 to 1.9
- qk_gains: float32 [2, 256], P(None, 'fsdp'), may hold values from 0.25 to 0.5
- w_qkv: float32 [2048, 3072], P('fsdp'), may hold values from -0.125 to 0.125
- w_out: float32 [2048, 2048], P('fsdp'), may hold values from -0.125 to 0.125
- laurel_left: float32 [2048, 64], P('fsdp'), may hold values from -0.125 to 0.125
- laurel_right: float32 [64, 2048], P('fsdp'), may hold values from -0.75 to 0.75
- w_gate_up: float32 [8192, 2, 2048], P('fsdp'), may hold values from -0.125 to 0.125
- w_down: float32 [8192, 2048], P('fsdp'), may hold values from -0.0625 to 0.0625
- pli_gate: float32 [2048, 256], P('fsdp'), may hold values from -0.125 to 0.125
- pli_proj: float32 [256, 2048], P('fsdp'), may hold values from -0.375 to 0.375
Outputs:
- mixed: bfloat16 [8192, 2048], P(('rep', 'fsdp'))
- grad_tokens: float32 [8192, 2048], P(('rep', 'fsdp'))
- grad_layer_input: float32 [8192, 256], P(('rep', 'fsdp'))
- grad_norm_gains: float32 [6, 2048], P(None, 'fsdp')
- grad_qk_gains: float32 [2, 256], P(None, 'fsdp')
- grad_w_qkv: float32 [2048, 3072], P('fsdp')
- grad_w_out: float32 [2048, 2048], P('fsdp')
- grad_laurel_left: float32 [2048, 64], P('fsdp')
- grad_laurel_right: float32 [64, 2048], P('fsdp')
- grad_w_gate_up: float32 [8192, 2, 2048], P('fsdp')
- grad_w_down: float32 [8192, 2048], P('fsdp')
- grad_pli_gate: float32 [2048, 256], P('fsdp')
- grad_pli_proj: float32 [256, 2048], P('fsdp')
All inputs are finite; a program needn't handle non-finite values.
Results may differ from a plain program's by a relative error of at most 0.028.
Values may be sent and summed in bfloat16 or wider, within the bound.
No kernel may reach another device: no remote copies, remote signals or barrier semaphores. Data moves between devices by JAX's collectives and lax.ppermute only.
A program may use at most 512 MiB of HBM per device.

v0:
```python
import jax
import jax.numpy as jnp
from jax import lax
from jax.sharding import PartitionSpec as P

H = 8
KVH = 2
HD = 256
CONT_LEN = 256
PROMPT_DEVS = 4


EPSILON = 1e-06
THETA_BASE = 1000000.0
HALF_ROOT = 0.7071067811865476
NEG_FILL = -1e30


def rms_norm(tensor):
    return tensor * lax.rsqrt(jnp.mean(tensor * tensor, axis=-1, keepdims=True) + EPSILON)


def rotary(tensor, places):
    halfway = tensor.shape[-1] // 2
    frequency = THETA_BASE ** (-(jnp.arange(halfway, dtype=jnp.float32) * 2.0 / tensor.shape[-1]))
    angles = places.astype(jnp.float32)[:, None, None] * frequency
    cosine = jnp.cos(angles)
    sine_part = jnp.sin(angles)
    first_half = tensor[..., :halfway]
    second_half = tensor[..., halfway:]
    return jnp.concatenate(
        [
            first_half * cosine - second_half * sine_part,
            second_half * cosine + first_half * sine_part,
        ],
        axis=-1,
    )


def gelu_mix(gate_up):
    return jax.nn.gelu(gate_up[:, 0], approximate=True) * gate_up[:, 1]


def outer_sum(left_mat, right_mat):
    return lax.dot_general(
        left_mat, right_mat, (((0,), (0,)), ((), ())), preferred_element_type=jnp.float32
    )


def back_dot(gradient, weight):
    return lax.dot_general(
        gradient, weight, (((1,), (1,)), ((), ())), preferred_element_type=jnp.float32
    )


def allowed_keys(first_row, block_rows, key_count, device, rows_dev):
    prompt_len = key_count - rows_dev
    query_local = first_row + jnp.arange(block_rows, dtype=jnp.int32)
    key_index = jnp.arange(key_count, dtype=jnp.int32)
    in_prompt = device < PROMPT_DEVS
    query_global = device * rows_dev + query_local
    own_index = key_index - prompt_len
    prompt_ok = jnp.logical_or(
        jnp.logical_not(in_prompt), key_index[None, :] <= query_global[:, None]
    )
    same_piece = own_index[None, :] // CONT_LEN == query_local[:, None] // CONT_LEN
    own_ok = jnp.logical_and(
        jnp.logical_not(in_prompt),
        jnp.logical_and(same_piece, own_index[None, :] <= query_local[:, None]),
    )
    return jnp.where(key_index[None, :] < prompt_len, prompt_ok, own_ok)


def block_layout(queries):
    rows_dev = queries.shape[0]
    block_rows = min(rows_dev, 512)
    blocks = rows_dev // block_rows
    starts = jnp.arange(blocks, dtype=jnp.int32) * block_rows
    return (block_rows, blocks, starts)


def masked_scores(query_block, keys_all, first_row, block_rows, device, rows_dev):
    scores = jnp.einsum("qkgd,skd->qkgs", query_block, keys_all, preferred_element_type=jnp.float32)
    allowed = allowed_keys(first_row, block_rows, keys_all.shape[0], device, rows_dev)[
        :, None, None, :
    ]
    return jnp.where(allowed, scores, NEG_FILL)


def attention_forward(queries, keys_all, values_all, device):
    rows_dev = queries.shape[0]
    block_rows, blocks, starts = block_layout(queries)

    def one_block(block_item):
        query_block, first_row = block_item
        scores = masked_scores(query_block, keys_all, first_row, block_rows, device, rows_dev)
        row_peak = jnp.max(scores, axis=-1, keepdims=True)
        row_total = jnp.sum(jnp.exp(scores - row_peak), axis=-1, keepdims=True)
        log_total = row_peak + jnp.log(row_total)
        shares_bf = jnp.exp(scores - log_total).astype(jnp.bfloat16)
        attended = jnp.einsum(
            "qkgs,skd->qkgd", shares_bf, values_all, preferred_element_type=jnp.float32
        )
        return (attended, log_total[..., 0])

    shaped = queries.reshape((blocks, block_rows) + queries.shape[1:])
    attended, log_totals = lax.map(one_block, (shaped, starts))
    return (attended.reshape(queries.shape), log_totals.reshape(queries.shape[:3]))


def attention_backward(queries, keys_all, values_all, grad_attended, log_totals, device):
    rows_dev = queries.shape[0]
    block_rows, blocks, starts = block_layout(queries)

    def one_block(carried, block_item):
        key_grad, value_grad = carried
        query_block, grad_block, total_block, first_row = block_item
        scores = masked_scores(query_block, keys_all, first_row, block_rows, device, rows_dev)
        shares = jnp.exp(scores - total_block[..., None])
        grad_shares = jnp.einsum(
            "qkgd,skd->qkgs", grad_block, values_all, preferred_element_type=jnp.float32
        )
        inner_sum = jnp.sum(shares * grad_shares, axis=-1, keepdims=True)
        grad_scores = (shares * (grad_shares - inner_sum)).astype(jnp.bfloat16)
        grad_query = jnp.einsum(
            "qkgs,skd->qkgd", grad_scores, keys_all, preferred_element_type=jnp.float32
        )
        key_grad = key_grad + jnp.einsum(
            "qkgs,qkgd->skd", grad_scores, query_block, preferred_element_type=jnp.float32
        )
        value_grad = value_grad + jnp.einsum(
            "qkgs,qkgd->skd",
            shares.astype(jnp.bfloat16),
            grad_block,
            preferred_element_type=jnp.float32,
        )
        return ((key_grad, value_grad), grad_query)

    shaped_query = queries.reshape((blocks, block_rows) + queries.shape[1:])
    shaped_grad = grad_attended.reshape((blocks, block_rows) + queries.shape[1:])
    shaped_total = log_totals.reshape((blocks, block_rows) + queries.shape[1:3])
    zero_grad = jnp.zeros(keys_all.shape, jnp.float32)
    (key_grad, value_grad), grad_query = lax.scan(
        one_block, (zero_grad, zero_grad), (shaped_query, shaped_grad, shaped_total, starts)
    )
    return (grad_query.reshape(queries.shape), key_grad, value_grad)


def body(
    tokens,
    layer_input,
    cotangent,
    norm_gains,
    qk_gains,
    w_qkv,
    w_out,
    laurel_left,
    laurel_right,
    w_gate_up,
    w_down,
    pli_gate,
    pli_proj,
):
    device = lax.axis_index("fsdp")
    rows_dev = tokens.shape[0]
    prompt_len = PROMPT_DEVS * rows_dev
    groups = H // KVH
    gathered = (
        lax.all_gather(norm_gains.astype(jnp.bfloat16), "fsdp", axis=1, tiled=True),
        lax.all_gather(qk_gains.astype(jnp.bfloat16), "fsdp", axis=1, tiled=True),
        lax.all_gather(w_qkv.astype(jnp.bfloat16), "fsdp", axis=0, tiled=True),
        lax.all_gather(w_out.astype(jnp.bfloat16), "fsdp", axis=0, tiled=True),
        lax.all_gather(laurel_left.astype(jnp.bfloat16), "fsdp", axis=0, tiled=True),
        lax.all_gather(laurel_right.astype(jnp.bfloat16), "fsdp", axis=0, tiled=True),
        lax.all_gather(pli_gate.astype(jnp.bfloat16), "fsdp", axis=0, tiled=True),
        lax.all_gather(pli_proj.astype(jnp.bfloat16), "fsdp", axis=0, tiled=True),
    )
    gains = gathered[0].astype(jnp.float32)
    qk_gain = gathered[1].astype(jnp.float32)
    inputs = tokens.astype(jnp.float32)
    extra_input = layer_input.astype(jnp.float32)

    def input_norm(tensor, gain_rows):
        return rms_norm(tensor) * gain_rows[0]

    normed, input_pull = jax.vjp(input_norm, inputs, gains)
    normed_bf = normed.astype(jnp.bfloat16)
    projected = jnp.dot(normed_bf, gathered[2], preferred_element_type=jnp.float32)
    local_rows = jnp.arange(rows_dev, dtype=jnp.int32)
    places = jnp.where(
        device < PROMPT_DEVS, device * rows_dev + local_rows, prompt_len + local_rows % CONT_LEN
    )

    def head_prep(projected, gain_pair):
        query_part = projected[:, : H * HD].reshape(rows_dev, H, HD)
        key_part = projected[:, H * HD : (H + KVH) * HD].reshape(rows_dev, KVH, HD)
        value_part = projected[:, (H + KVH) * HD :].reshape(rows_dev, KVH, HD)
        queries = rotary(rms_norm(query_part) * gain_pair[0], places).reshape(
            rows_dev, KVH, groups, HD
        )
        return (queries, rotary(rms_norm(key_part) * gain_pair[1], places), rms_norm(value_part))

    (queries, keys_own, values_own), prep_pull = jax.vjp(head_prep, projected, qk_gain)
    queries_bf = queries.astype(jnp.bfloat16)
    keys_bf = keys_own.astype(jnp.bfloat16)
    values_bf = values_own.astype(jnp.bfloat16)
    gathered_kv = (
        lax.all_gather(keys_bf, "fsdp", axis=0, tiled=True),
        lax.all_gather(values_bf, "fsdp", axis=0, tiled=True),
    )
    keys_all = jnp.concatenate([gathered_kv[0][:prompt_len], keys_bf], axis=0)
    values_all = jnp.concatenate([gathered_kv[1][:prompt_len], values_bf], axis=0)
    attended, log_totals = attention_forward(queries_bf, keys_all, values_all, device)
    attended_bf = attended.reshape(rows_dev, H * HD).astype(jnp.bfloat16)
    attn_proj = jnp.dot(attended_bf, gathered[3], preferred_element_type=jnp.float32)
    laurel_mid = jnp.dot(normed_bf, gathered[4], preferred_element_type=jnp.float32).astype(
        jnp.bfloat16
    )
    laurel_out = jnp.dot(laurel_mid, gathered[5], preferred_element_type=jnp.float32)

    def middle(inputs, normed, attn_proj, laurel_out, gain_rows):
        first_sum = inputs + rms_norm(attn_proj) * gain_rows[1]
        laurel_sum = normed + rms_norm(laurel_out) * gain_rows[2]
        stream = (first_sum + laurel_sum) * HALF_ROOT
        return (stream, rms_norm(stream) * gain_rows[3])

    (stream, ffn_in), middle_pull = jax.vjp(middle, inputs, normed, attn_proj, laurel_out, gains)
    ffn_in_bf = ffn_in.astype(jnp.bfloat16)
    wide_weights = (
        lax.all_gather(w_gate_up.astype(jnp.bfloat16), "fsdp", axis=0, tiled=True),
        lax.all_gather(w_down.astype(jnp.bfloat16), "fsdp", axis=0, tiled=True),
    )
    gate_up = jnp.einsum(
        "td,fkd->tkf", ffn_in_bf, wide_weights[0], preferred_element_type=jnp.float32
    )
    hidden, hidden_pull = jax.vjp(gelu_mix, gate_up)
    hidden_bf = hidden.astype(jnp.bfloat16)
    ffn_out = jnp.dot(hidden_bf, wide_weights[1], preferred_element_type=jnp.float32)

    def tail_norm(stream, ffn_out, gain_rows):
        return stream + rms_norm(ffn_out) * gain_rows[4]

    after_ffn, tail_pull = jax.vjp(tail_norm, stream, ffn_out, gains)
    after_bf = after_ffn.astype(jnp.bfloat16)
    pli_pre = jnp.dot(after_bf, gathered[6], preferred_element_type=jnp.float32)

    def pli_mix(pli_pre, extra_input):
        return jax.nn.gelu(pli_pre, approximate=True) * extra_input

    pli_mid, pli_pull = jax.vjp(pli_mix, pli_pre, extra_input)
    pli_mid_bf = pli_mid.astype(jnp.bfloat16)
    pli_out = jnp.dot(pli_mid_bf, gathered[7], preferred_element_type=jnp.float32)

    def final_norm(after_ffn, pli_out, gain_rows):
        return after_ffn + rms_norm(pli_out) * gain_rows[5]

    result, final_pull = jax.vjp(final_norm, after_ffn, pli_out, gains)
    back_weights = (
        lax.all_gather(w_qkv.astype(jnp.bfloat16), "fsdp", axis=0, tiled=True),
        lax.all_gather(w_out.astype(jnp.bfloat16), "fsdp", axis=0, tiled=True),
        lax.all_gather(laurel_left.astype(jnp.bfloat16), "fsdp", axis=0, tiled=True),
        lax.all_gather(laurel_right.astype(jnp.bfloat16), "fsdp", axis=0, tiled=True),
        lax.all_gather(pli_gate.astype(jnp.bfloat16), "fsdp", axis=0, tiled=True),
        lax.all_gather(pli_proj.astype(jnp.bfloat16), "fsdp", axis=0, tiled=True),
    )
    grad_after, grad_pli_out, gain_final = final_pull(cotangent.astype(jnp.float32))
    grad_pli_out_bf = grad_pli_out.astype(jnp.bfloat16)
    grad_pproj = outer_sum(pli_mid_bf, grad_pli_out_bf)
    grad_pli_mid = back_dot(grad_pli_out_bf, back_weights[5])
    grad_pli_pre, grad_extra = pli_pull(grad_pli_mid)
    grad_pli_pre_bf = grad_pli_pre.astype(jnp.bfloat16)
    grad_pgate = outer_sum(after_bf, grad_pli_pre_bf)
    grad_after = grad_after + back_dot(grad_pli_pre_bf, back_weights[4])
    grad_stream, grad_ffn_out, gain_tail = tail_pull(grad_after)
    grad_ffn_bf = grad_ffn_out.astype(jnp.bfloat16)
    wide_back = (
        lax.all_gather(w_gate_up.astype(jnp.bfloat16), "fsdp", axis=0, tiled=True),
        lax.all_gather(w_down.astype(jnp.bfloat16), "fsdp", axis=0, tiled=True),
    )
    grad_hidden = back_dot(grad_ffn_bf, wide_back[1])
    (grad_gate_up,) = hidden_pull(grad_hidden)
    grad_gu_bf = grad_gate_up.astype(jnp.bfloat16)
    grad_ffn_in = jnp.einsum(
        "tkf,fkd->td", grad_gu_bf, wide_back[0], preferred_element_type=jnp.float32
    )
    slab = grad_gu_bf
    grad_gate_up_w = lax.psum_scatter(
        jnp.einsum("tkf,td->fkd", slab, ffn_in_bf, preferred_element_type=jnp.float32).astype(
            jnp.bfloat16
        ),
        "fsdp",
        scatter_dimension=0,
        tiled=True,
    )
    slab = hidden_bf
    grad_down_w = lax.psum_scatter(
        outer_sum(slab, grad_ffn_bf).astype(jnp.bfloat16), "fsdp", scatter_dimension=0, tiled=True
    )
    grad_inputs, grad_normed, grad_attn_proj, grad_laurel_out, gain_middle = middle_pull(
        (grad_stream, grad_ffn_in)
    )
    grad_attn_bf = grad_attn_proj.astype(jnp.bfloat16)
    grad_out_w = outer_sum(attended_bf, grad_attn_bf)
    grad_attended = (
        back_dot(grad_attn_bf, back_weights[1])
        .astype(jnp.bfloat16)
        .reshape(rows_dev, KVH, groups, HD)
    )
    grad_laurel_bf = grad_laurel_out.astype(jnp.bfloat16)
    grad_right_w = outer_sum(laurel_mid, grad_laurel_bf)
    grad_mid_bf = back_dot(grad_laurel_bf, back_weights[3]).astype(jnp.bfloat16)
    grad_left_w = outer_sum(normed_bf, grad_mid_bf)
    grad_normed = grad_normed + back_dot(grad_mid_bf, back_weights[2])
    grad_queries, key_grad, value_grad = attention_backward(
        queries_bf, keys_all, values_all, grad_attended, log_totals, device
    )
    prompt_keys, prompt_values = (
        lax.psum(key_grad[:prompt_len].astype(jnp.bfloat16), "fsdp").astype(jnp.float32),
        lax.psum(value_grad[:prompt_len].astype(jnp.bfloat16), "fsdp").astype(jnp.float32),
    )
    owner_start = jnp.minimum(device, PROMPT_DEVS - 1) * rows_dev
    in_prompt = device < PROMPT_DEVS
    key_sum = jnp.where(
        in_prompt,
        lax.dynamic_slice_in_dim(prompt_keys, owner_start, rows_dev, 0),
        key_grad[prompt_len:],
    )
    value_sum = jnp.where(
        in_prompt,
        lax.dynamic_slice_in_dim(prompt_values, owner_start, rows_dev, 0),
        value_grad[prompt_len:],
    )
    grad_projected, grad_qk_gain = prep_pull((grad_queries, key_sum, value_sum))
    grad_proj_bf = grad_projected.astype(jnp.bfloat16)
    grad_qkv_w = outer_sum(normed_bf, grad_proj_bf)
    grad_normed = grad_normed + back_dot(grad_proj_bf, back_weights[0])
    grad_first, gain_input = input_pull(grad_normed)
    grad_tokens = grad_inputs + grad_first
    gain_total = gain_final + gain_tail + gain_middle + gain_input
    shards = (
        lax.psum_scatter(
            gain_total.astype(jnp.bfloat16), "fsdp", scatter_dimension=1, tiled=True
        ).astype(jnp.float32),
        lax.psum_scatter(
            grad_qk_gain.astype(jnp.bfloat16), "fsdp", scatter_dimension=1, tiled=True
        ).astype(jnp.float32),
        lax.psum_scatter(
            grad_qkv_w.astype(jnp.bfloat16), "fsdp", scatter_dimension=0, tiled=True
        ).astype(jnp.float32),
        lax.psum_scatter(
            grad_out_w.astype(jnp.bfloat16), "fsdp", scatter_dimension=0, tiled=True
        ).astype(jnp.float32),
        lax.psum_scatter(
            grad_left_w.astype(jnp.bfloat16), "fsdp", scatter_dimension=0, tiled=True
        ).astype(jnp.float32),
        lax.psum_scatter(
            grad_right_w.astype(jnp.bfloat16), "fsdp", scatter_dimension=0, tiled=True
        ).astype(jnp.float32),
        lax.psum_scatter(
            grad_pgate.astype(jnp.bfloat16), "fsdp", scatter_dimension=0, tiled=True
        ).astype(jnp.float32),
        lax.psum_scatter(
            grad_pproj.astype(jnp.bfloat16), "fsdp", scatter_dimension=0, tiled=True
        ).astype(jnp.float32),
    )
    summed = (
        lax.psum(shards[0].astype(jnp.bfloat16), "rep").astype(jnp.float32),
        lax.psum(shards[1].astype(jnp.bfloat16), "rep").astype(jnp.float32),
        lax.psum(shards[2].astype(jnp.bfloat16), "rep").astype(jnp.float32),
        lax.psum(shards[3].astype(jnp.bfloat16), "rep").astype(jnp.float32),
        lax.psum(shards[4].astype(jnp.bfloat16), "rep").astype(jnp.float32),
        lax.psum(shards[5].astype(jnp.bfloat16), "rep").astype(jnp.float32),
        lax.psum(grad_gate_up_w, "rep").astype(jnp.float32),
        lax.psum(grad_down_w, "rep").astype(jnp.float32),
        lax.psum(shards[6].astype(jnp.bfloat16), "rep").astype(jnp.float32),
        lax.psum(shards[7].astype(jnp.bfloat16), "rep").astype(jnp.float32),
    )
    return (
        result.astype(jnp.bfloat16),
        grad_tokens,
        grad_extra,
        summed[0],
        summed[1],
        summed[2],
        summed[3],
        summed[4],
        summed[5],
        summed[6],
        summed[7],
        summed[8],
        summed[9],
    )


def solution(mesh):
    placed = (
        P(("rep", "fsdp"), None),
        P(("rep", "fsdp"), None),
        P(("rep", "fsdp"), None),
        P(None, "fsdp"),
        P(None, "fsdp"),
        P("fsdp", None),
        P("fsdp", None),
        P("fsdp", None),
        P("fsdp", None),
        P("fsdp", None, None),
        P("fsdp", None),
        P("fsdp", None),
        P("fsdp", None),
    )
    return jax.shard_map(
        body,
        mesh=mesh,
        in_specs=placed,
        out_specs=(
            P(("rep", "fsdp"), None),
            P(("rep", "fsdp"), None),
            P(("rep", "fsdp"), None),
            P(None, "fsdp"),
            P(None, "fsdp"),
            P("fsdp", None),
            P("fsdp", None),
            P("fsdp", None),
            P("fsdp", None),
            P("fsdp", None, None),
            P("fsdp", None),
            P("fsdp", None),
            P("fsdp", None),
        ),
        check_vma=False,
    )
```

profile of v0, /device:TPU:0, one launch (start us, length us, event | category | flops | bytes accessed | tf_op | source)
XLA Modules:
  0.0 3124.4 jit_solution(3149129742641646129)
XLA Ops:
  10.7 13.4 all-gather
  24.2 14.3 all_gather.44
  40.5 89.9 %all-gather.10.cloned.1.call-done = bf16[2048,3072]{1,0:T(8,128)(2,1)} async-done(((bf16[256,3072]{1,0:T(8,128)(2,1)}), bf16[2048,3072]{1,0:T(8,128)(2,1)}) %all-gather.10.cloned.1.call-update) | async-done | bytes 12582928 | tf_op jit(solution)/shard_map/all_gather | solution.py:171
  145.1 17.4 copy.245
  172.4 15.1 all_gather.51
  187.4 15.3 all_gather.50
  223.8 6.9 convolution_convert_fusion.8
  230.8 54.8 %all-gather.16.cloned.1.call-done = bf16[2048,2048]{1,0:T(8,128)(2,1)} async-done(((bf16[256,2048]{1,0:T(8,128)(2,1)}), bf16[2048,2048]{1,0:T(8,128)(2,1)}) %all-gather.16.cloned.1.call-update) | async-done | bytes 8388624 | tf_op jit(solution)/shard_map/all_gather | solution.py:172
  292.8 557.3 %all-gather.18.cloned.1.call-done = bf16[8192,2,2048]{2,0,1:T(8,128)(2,1)} async-done(((bf16[1024,2,2048]{2,0,1:T(8,128)(2,1)}), bf16[8192,2,2048]{2,0,1:T(8,128)(2,1)}) %all-gather.18.cloned.1.call-update) | async-done | bytes 67108880 | tf_op jit(solution)/shard_map/all_gather | solution.py:230
  850.1 36.1 %convolution_bitcast_fusion = f32[256,2,8192]{2,0,1:T(8,128)} fusion(bf16[8192,2,2048]{2,0,1:T(8,128)(2,1)} %all-gather.18.cloned.1.call-done, f32[256,2048]{1,0:T(8,128)S(1)} %get-tuple-element.174, f32[2048]{0:T(1024)S(1)} %bitcast.226, f32[256]{0:T(256)S(1)} %get-tuple-element.206), kind=kOutput, calls=%fused_computation.4 | convolution fusion | flops 17181442048 | bytes 85992448 | tf_op jit(solution)/shard_map/td,fkd->tkf/dot_general | solution.py:233
  886.2 9.3 multiply_convert_fusion
  895.5 242.9 %all-gather.20.cloned.1.call-done = bf16[8192,2048]{1,0:T(8,128)(2,1)} async-done(((bf16[1024,2048]{1,0:T(8,128)(2,1)}), bf16[8192,2048]{1,0:T(8,128)(2,1)}) %all-gather.20.cloned.1.call-update) | async-done | bytes 33554448 | tf_op jit(solution)/shard_map/all_gather | solution.py:231
  1138.4 16.7 multiply_reduce_fusion.11
  1162.7 21.6 all-gather.24.cloned.1.call-done
  1195.4 25.9 multiply_bitcast_fusion
  1221.4 32.1 %multiply_reduce_fusion.3 = (f32[2048]{0:T(1024)}, f32[256]{0:T(256)S(1)}, f32[256,2048]{1,0:T(8,128)}) fusion(f32[256,2048]{1,0:T(8,128)S(1)} %copy-done.10, f32[256]{0:T(256)S(1)} %get-tuple-element.206, f32[2048]{0:T(1024)S(1)} %bitcast.227, bf16[8192,2,2048]{2,0,1:T(8,128)(2,1)} %all-gather.18.cloned.1.call-done, ...), kind=kOutput, calls=%fused_computation.79 | convolution fusion | flops 17191925760 | bytes 88098816 | tf_op jit(solution)/shard_map/tkf,fkd->td/dot_general | solution.py:283
  1268.4 7.9 convolution_bitcast_fusion.1
  1304.1 54.8 %all-reduce.24.cloned.1.call-done = (bf16[1024,2,256]{2,0,1:T(8,128)(2,1)}, bf16[1024,2,256]{2,0,1:T(8,128)(2,1)}) async-done(((bf16[1024,2,256]{2,0,1:T(8,128)(2,1)}, bf16[1024,2,256]{2,0,1:T(8,128)(2,1)}), (bf16[1024,2,256]{2,0,1:T(8,128)(2,1)}, bf16[1024,2,256]{2,0,1:T(8,128)(2,1)})) %all-reduce.24.cloned.1.call-update) | async-done | bytes 2097168 | tf_op jit(solution)/shard_map/psum | solution.py:318
  1376.8 10.2 fusion.85
  1404.2 8.2 convolution_convert_fusion.1
  1413.7 16.1 convolution_convert_fusion
  1431.5 34.8 %convert_bitcast_fusion = bf16[8192,2,2048]{0,2,1:T(8,128)(2,1)} fusion(f32[256,1,8192]{2,0,1:T(8,128)} %get-tuple-element.176, f32[256,1,8192]{2,0,1:T(8,128)} %get-tuple-element.175, f32[256,2048]{1,0:T(8,128)S(1)} %copy-done.11, f32[2048]{0:T(1024)S(1)} %bitcast.229, f32[256]{0:T(256)S(1)} %copy-done.77), kind=kOutput, calls=%fused_computation | convolution fusion | flops 17223385088 | bytes 85992448 | tf_op jit(solution)/shard_map/tkf,td->fkd/dot_general | solution.py:288
  1467.6 19.2 reduce-scatter.13.cloned.1.call-done
  1486.9 32.5 %reduce-scatter.27.cloned.1.call-done = bf16[256,256]{1,0:T(8,128)(2,1)} async-done(((bf16[2048,256]{1,0:T(8,128)(2,1)}), bf16[256,256]{1,0:T(8,128)(2,1)}) %reduce-scatter.27.cloned.1.call-update) | async-done | bytes 131088 | tf_op jit(solution)/shard_map/reduce_scatter | solution.py:359
  1519.4 32.8 %reduce-scatter.29.cloned.1.call-done = bf16[32,2048]{1,0:T(8,128)(2,1)} async-done(((bf16[256,2048]{1,0:T(8,128)(2,1)}), bf16[32,2048]{1,0:T(8,128)(2,1)}) %reduce-scatter.29.cloned.1.call-update) | async-done | bytes 131088 | tf_op jit(solution)/shard_map/reduce_scatter | solution.py:362
  1552.2 90.2 %reduce-scatter.17.cloned.1.call-done = bf16[256,2048]{1,0:T(8,128)(2,1)} async-done(((bf16[2048,2048]{1,0:T(8,128)(2,1)}), bf16[256,2048]{1,0:T(8,128)(2,1)}) %reduce-scatter.17.cloned.1.call-update) | async-done | bytes 1048592 | tf_op jit(solution)/shard_map/reduce_scatter | solution.py:350
  1642.5 130.3 %reduce-scatter.15.cloned.1.call-done = bf16[256,3072]{1,0:T(8,128)(2,1)} async-done(((bf16[2048,3072]{1,0:T(8,128)(2,1)}), bf16[256,3072]{1,0:T(8,128)(2,1)}) %reduce-scatter.15.cloned.1.call-update) | async-done | bytes 1572880 | tf_op jit(solution)/shard_map/reduce_scatter | solution.py:347
  1772.8 326.2 %reduce-scatter.25.cloned.1.call-done = bf16[1024,2048]{1,0:T(8,128)(2,1)} async-done(((bf16[8192,2048]{1,0:T(8,128)(2,1)}), bf16[1024,2048]{1,0:T(8,128)(2,1)}) %reduce-scatter.25.cloned.1.call-update) | async-done | bytes 4194320 | tf_op jit(solution)/shard_map/reduce_scatter | solution.py:296
  2099.0 641.0 %reduce-scatter.23.cloned.1.call-done = bf16[1024,2,2048]{0,2,1:T(8,128)(2,1)} async-done(((bf16[8192,2,2048]{0,2,1:T(8,128)(2,1)}), bf16[1024,2,2048]{0,2,1:T(8,128)(2,1)}) %reduce-scatter.23.cloned.1.call-update) | async-done | bytes 8388624 | tf_op jit(solution)/shard_map/reduce_scatter | solution.py:287
  2745.2 37.8 %all-reduce.26.cloned.1.call-done = (bf16[6,256]{1,0:T(8,128)(2,1)}, bf16[2,32]{1,0:T(2,128)(2,1)}, bf16[256,64]{0,1:T(8,128)(2,1)}, bf16[8,2048]{1,0:T(8,128)(2,1)}) async-done(((bf16[6,256]{1,0:T(8,128)(2,1)}, bf16[2,32]{1,0:T(2,128)(2,1)}, bf16[256,64]{0,1:T(8,128)(2,1)}, bf16[8,2048]{1,0:T(8,128)(2,1)}), (bf16[6,256]{1,0:T(8,128)(2,1)}, bf16[2,32]{1,0:T(2,128)(2,1)}, bf16[256,64]{0,1:T(8,128)(2,1)}, ...) | async-done | bytes 68752 | tf_op jit(solution)/shard_map/psum | solution.py:367
  2788.3 291.7 %all-reduce.28.cloned.1.call-done = (bf16[1024,2,2048]{0,2,1:T(8,128)(2,1)}, bf16[256,3072]{1,0:T(8,128)(2,1)}, bf16[256,2048]{1,0:T(8,128)(2,1)}, bf16[1024,204...) async-done(((bf16[1024,2,2048]{0,2,1:T(8,128)(2,1)}, bf16[256,3072]{1,0:T(8,128)(2,1)}, bf16[256,2048]{1,0:T(8,128)(2,1)}, ...) | async-done | bytes 15466512 | tf_op jit(solution)/shard_map/psum | solution.py:373
  3088.2 22.3 copy.203
  (434 shorter events, 183.0 us)
Async XLA Ops:
  7.2 123.2 %all-gather.10.cloned.1.call-start = ((), (), s32[]{:S(2)}) async-start(), calls=%async_computation.10 | async-start | bytes 14155776 | tf_op jit(solution)/shard_map/all_gather | solution.py:171
  10.6 203.8 %all-gather.14.cloned.1.call-start = ((), (), s32[]{:S(2)}) async-start(), calls=%async_computation.12 | async-start | bytes 2359296 | tf_op jit(solution)/shard_map/all_gather | solution.py:208
  39.3 163.4 %copy-start.92 = (f32[256]{0:T(256)}, f32[256]{0:T(256)S(1)}, u32[]{:S(2)}) copy-start(f32[256]{0:T(256)S(1)} %fusion.71) | copy-start | bytes 3076
  39.9 99.6 %copy-start.109 = (f32[1,256]{1,0:T(1,128)}, f32[1,256]{1,0:T(1,128)S(1)}, u32[]{:S(2)}) copy-start(f32[1,256]{1,0:T(1,128)S(1)} %get-tuple-element.201) | copy-start | bytes 3076
  40.4 99.2 %copy-start.44 = (f32[256,128]{1,0:T(8,128)}, f32[256,128]{1,0:T(8,128)S(1)}, u32[]{:S(2)}) copy-start(f32[256,128]{1,0:T(8,128)S(1)} %get-tuple-element.203) | copy-start | bytes 393220
  40.4 99.2 %copy-start.47 = (f32[256,128]{1,0:T(8,128)}, f32[256,128]{1,0:T(8,128)S(1)}, u32[]{:S(2)}) copy-start(f32[256,128]{1,0:T(8,128)S(1)} %get-tuple-element.204) | copy-start | bytes 393220
  40.5 131.3 %copy-start.86 = (f32[1,2048]{1,0:T(1,128)}, f32[1,2048]{1,0:T(1,128)S(1)}, u32[]{:S(2)}) copy-start(f32[1,2048]{1,0:T(1,128)S(1)} %get-tuple-element.199) | copy-start | bytes 24580
  40.5 251.0 %copy-start.74 = (f32[1,2048]{1,0:T(1,128)}, f32[1,2048]{1,0:T(1,128)S(1)}, u32[]{:S(2)}) copy-start(f32[1,2048]{1,0:T(1,128)S(1)} %get-tuple-element.200) | copy-start | bytes 24580
  140.5 81.9 %all-gather.12.cloned.1.call-start = ((), (), s32[]{:S(2)}) async-start(), calls=%async_computation.11 | async-start | bytes 2359296 | tf_op jit(solution)/shard_map/all_gather | solution.py:209
  142.3 143.2 %all-gather.16.cloned.1.call-start = ((), (), s32[]{:S(2)}) async-start(), calls=%async_computation.13 | async-start | bytes 9437184 | tf_op jit(solution)/shard_map/all_gather | solution.py:172
  145.1 705.0 %all-gather.18.cloned.1.call-start = ((), (), s32[]{:S(2)}) async-start(), calls=%async_computation.14 | async-start | bytes 75497472 | tf_op jit(solution)/shard_map/all_gather | solution.py:230
  162.6 975.9 %all-gather.20.cloned.1.call-start = ((), (), s32[]{:S(2)}) async-start(), calls=%async_computation.15 | async-start | bytes 37748736 | tf_op jit(solution)/shard_map/all_gather | solution.py:231
  168.7 991.7 %all-gather.22.cloned.1.call-start = ((), (), s32[]{:S(2)}) async-start(), calls=%async_computation.16 | async-start | bytes 1179648 | tf_op jit(solution)/shard_map/all_gather | solution.py:175
  170.3 1014.0 %all-gather.24.cloned.1.call-start = ((), (), s32[]{:S(2)}) async-start(), calls=%async_computation.17 | async-start | bytes 1179648 | tf_op jit(solution)/shard_map/all_gather | solution.py:176
  171.0 1187.9 %all-reduce.24.cloned.1.call-start = ((), (), s32[]{:S(2)}) async-start(), calls=%async_computation.28 | async-start | bytes 4194304 | tf_op jit(solution)/shard_map/psum | solution.py:318
  230.8 60.7 %copy-start.29 = (bf16[2,256,256,4]{2,1,3,0:T(8,128)(2,1)}, bf16[2,256,256,4]{2,1,3,0:T(8,128)(2,1)S(1)}, u32[]{:S(2)}) copy-start(bf16[2,256,256,4]{2,1,3,0:T(8,128)(2,1)S(1)} %convolution_convert_fusion.8) | copy-start | bytes 3145732
  292.8 593.4 %copy-start.8 = (f32[256,2048]{1,0:T(8,128)}, f32[256,2048]{1,0:T(8,128)S(1)}, u32[]{:S(2)}) copy-start(f32[256,2048]{1,0:T(8,128)S(1)} %get-tuple-element.174) | copy-start | bytes 6291460
  292.8 928.5 %copy-start.76 = (f32[256]{0:T(256)}, f32[256]{0:T(256)S(1)}, u32[]{:S(2)}) copy-start(f32[256]{0:T(256)S(1)} %get-tuple-element.206) | copy-start | bytes 3076
  1294.4 171.9 %reduce-scatter.31.cloned.1.call-start = ((), (), s32[]{:S(2)}) async-start(), calls=%async_computation.27 | async-start | bytes 73728
  1300.0 58.9 %copy-start.24 = (f32[256,512]{1,0:T(8,128)S(1)}, f32[256,512]{1,0:T(8,128)}, u32[]{:S(2)}) copy-start(f32[256,512]{1,0:T(8,128)} %copy-done.23) | copy-start | bytes 1572868
  1301.2 59.0 %copy-start.107 = (f32[256,2]{0,1:T(2,128)S(1)}, f32[256,2]{0,1:T(2,128)}, u32[]{:S(2)}) copy-start(f32[256,2]{0,1:T(2,128)} %copy-done.106) | copy-start | bytes 6148
  1364.4 103.2 %reduce-scatter.21.cloned.1.call-start = ((), (), s32[]{:S(2)}) async-start(), calls=%async_computation.22 | async-start | bytes 294912 | tf_op jit(solution)/shard_map/reduce_scatter | solution.py:356
  1365.4 102.3 %reduce-scatter.19.cloned.1.call-start = ((), (), s32[]{:S(2)}) async-start(), calls=%async_computation.21 | async-start | bytes 294912 | tf_op jit(solution)/shard_map/reduce_scatter | solution.py:353
  1373.4 113.5 %reduce-scatter.13.cloned.1.call-start = ((), (), s32[]{:S(2)}) async-start(), calls=%async_computation.18 | async-start | bytes 36864 | tf_op jit(solution)/shard_map/reduce_scatter | solution.py:341
  1392.4 127.0 %reduce-scatter.27.cloned.1.call-start = ((), (), s32[]{:S(2)}) async-start(), calls=%async_computation.25 | async-start | bytes 1179648 | tf_op jit(solution)/shard_map/reduce_scatter | solution.py:359
  1394.0 158.3 %reduce-scatter.29.cloned.1.call-start = ((), (), s32[]{:S(2)}) async-start(), calls=%async_computation.26 | async-start | bytes 1179648 | tf_op jit(solution)/shard_map/reduce_scatter | solution.py:362
  1397.0 245.5 %reduce-scatter.17.cloned.1.call-start = ((), (), s32[]{:S(2)}) async-start(), calls=%async_computation.20 | async-start | bytes 9437184 | tf_op jit(solution)/shard_map/reduce_scatter | solution.py:350
  1402.7 370.2 %reduce-scatter.15.cloned.1.call-start = ((), (), s32[]{:S(2)}) async-start(), calls=%async_computation.19 | async-start | bytes 14155776 | tf_op jit(solution)/shard_map/reduce_scatter | solution.py:347
  1412.5 686.5 %reduce-scatter.25.cloned.1.call-start = ((), (), s32[]{:S(2)}) async-start(), calls=%async_computation.24 | async-start | bytes 37748736 | tf_op jit(solution)/shard_map/reduce_scatter | solution.py:296
  1429.9 1310.1 %reduce-scatter.23.cloned.1.call-start = ((), (), s32[]{:S(2)}) async-start(), calls=%async_computation.23 | async-start | bytes 75497472 | tf_op jit(solution)/shard_map/reduce_scatter | solution.py:287
  1466.3 1316.7 %all-reduce.26.cloned.1.call-start = ((), (), s32[]{:S(2)}) async-start(), calls=%async_computation.29 | async-start | bytes 140288 | tf_op jit(solution)/shard_map/psum | solution.py:367
  1486.9 1593.1 %all-reduce.28.cloned.1.call-start = ((), (), s32[]{:S(2)}) async-start(), calls=%async_computation.30 | async-start | bytes 30932992 | tf_op jit(solution)/shard_map/psum | solution.py:373
  (118 other events, 630.5 us)
Sparse Core Ops, SparseCore 0:
  10.7 119.5 all-gather.9
  140.7 27.3 all-gather.13
  170.3 31.6 all-gather.11
  204.0 81.5 all-gather.15
  287.6 562.5 all-gather.17
  851.6 286.7 all-gather.19
  1140.0 20.2 all-gather.21
  1162.5 21.7 all-gather.23
  1294.5 64.3 all-reduce.23
  1364.6 29.7 reduce-scatter.30
  1396.7 28.4 reduce-scatter.20
  1427.3 28.4 reduce-scatter.18
  1458.7 28.0 reduce-scatter.12
  1489.0 30.3 reduce-scatter.26
  1521.5 30.6 reduce-scatter.28
  1554.4 88.0 reduce-scatter.16
  1645.2 127.5 reduce-scatter.14
  1775.0 323.8 reduce-scatter.24
  2101.5 638.4 reduce-scatter.22
  2743.6 39.3 all-reduce.25
  2788.3 291.6 all-reduce.27
where the time goes:
time: 3130 us; the launch traced here: 3120 us
  waiting for transfers between devices  2630 us (84%)
  matrix products  254 us (8%)
  other arithmetic  85.8 us (3%)
  local copies, waits for them, and re-layouts  82.5 us (3%)
  blocking collectives  58 us (2%)
    reduce_scatter x1, waiting for transfers between devices, body(): lax.psum_scatter(jnp.einsum('tkf,td->fkd', slab, ffn_in_bf, preferred_ele...  641 us
    all_gather x1, waiting for transfers between devices, body(): lax.all_gather(w_gate_up.astype(jnp.bfloat16), 'fsdp', axis=0, tiled=True)  557 us
    reduce_scatter x1, waiting for transfers between devices, body(): lax.psum_scatter(outer_sum(slab, grad_ffn_bf).astype(jnp.bfloat16), 'fsdp...  326 us
    psum x1, waiting for transfers between devices, body(): lax.psum(grad_gate_up_w, 'rep').astype(jnp.float32)  292 us
    all_gather x1, waiting for transfers between devices, body(): lax.all_gather(w_down.astype(jnp.bfloat16), 'fsdp', axis=0, tiled=True)  243 us
    reduce_scatter x1, waiting for transfers between devices, body(): lax.psum_scatter(grad_qkv_w.astype(jnp.bfloat16), 'fsdp', scatter_dimensi...  130 us
    reduce_scatter x1, waiting for transfers between devices, body(): lax.psum_scatter(grad_out_w.astype(jnp.bfloat16), 'fsdp', scatter_dimensi...  90.2 us
    all_gather x1, waiting for transfers between devices, body(): lax.all_gather(w_qkv.astype(jnp.bfloat16), 'fsdp', axis=0, tiled=True)  89.9 us
  transfers between devices with their start and end apart: 21, of which 16 were waited for; matrix products, arithmetic and copies ran while one was open for 8% of the time, Pallas kernels for 0%

commit v1 on v0

v1 whole, which is shorter than its diff:
```python
import jax
import jax.numpy as jnp
from jax import lax
from jax.sharding import PartitionSpec as P

H = 8
KVH = 2
HD = 256
CONT_LEN = 256
PROMPT_DEVS = 4


EPSILON = 1e-06
THETA_BASE = 1000000.0
HALF_ROOT = 0.7071067811865476
NEG_FILL = -1e30


def rms_norm(tensor):
    return tensor * lax.rsqrt(jnp.mean(tensor * tensor, axis=-1, keepdims=True) + EPSILON)


def rotary(tensor, places):
    halfway = tensor.shape[-1] // 2
    frequency = THETA_BASE ** (-(jnp.arange(halfway, dtype=jnp.float32) * 2.0 / tensor.shape[-1]))
    angles = places.astype(jnp.float32)[:, None, None] * frequency
    cosine = jnp.cos(angles)
    sine_part = jnp.sin(angles)
    first_half = tensor[..., :halfway]
    second_half = tensor[..., halfway:]
    return jnp.concatenate(
        [
            first_half * cosine - second_half * sine_part,
            second_half * cosine + first_half * sine_part,
        ],
        axis=-1,
    )


def gelu_mix(gate_up):
    return jax.nn.gelu(gate_up[:, 0], approximate=True) * gate_up[:, 1]


def outer_sum(left_mat, right_mat):
    return lax.dot_general(
        left_mat, right_mat, (((0,), (0,)), ((), ())), preferred_element_type=jnp.float32
    )


def back_dot(gradient, weight):
    return lax.dot_general(
        gradient, weight, (((1,), (1,)), ((), ())), preferred_element_type=jnp.float32
    )


def allowed_keys(first_row, block_rows, key_count, device, rows_dev):
    prompt_len = key_count - rows_dev
    query_local = first_row + jnp.arange(block_rows, dtype=jnp.int32)
    key_index = jnp.arange(key_count, dtype=jnp.int32)
    in_prompt = device < PROMPT_DEVS
    query_global = device * rows_dev + query_local
    own_index = key_index - prompt_len
    prompt_ok = jnp.logical_or(
        jnp.logical_not(in_prompt), key_index[None, :] <= query_global[:, None]
    )
    same_piece = own_index[None, :] // CONT_LEN == query_local[:, None] // CONT_LEN
    own_ok = jnp.logical_and(
        jnp.logical_not(in_prompt),
        jnp.logical_and(same_piece, own_index[None, :] <= query_local[:, None]),
    )
    return jnp.where(key_index[None, :] < prompt_len, prompt_ok, own_ok)


def block_layout(queries):
    rows_dev = queries.shape[0]
    block_rows = min(rows_dev, 512)
    blocks = rows_dev // block_rows
    starts = jnp.arange(blocks, dtype=jnp.int32) * block_rows
    return (block_rows, blocks, starts)


def masked_scores(query_block, keys_all, first_row, block_rows, device, rows_dev):
    scores = jnp.einsum("qkgd,skd->qkgs", query_block, keys_all, preferred_element_type=jnp.float32)
    allowed = allowed_keys(first_row, block_rows, keys_all.shape[0], device, rows_dev)[
        :, None, None, :
    ]
    return jnp.where(allowed, scores, NEG_FILL)


def attention_forward(queries, keys_all, values_all, device):
    rows_dev = queries.shape[0]
    block_rows, blocks, starts = block_layout(queries)

    def one_block(block_item):
        query_block, first_row = block_item
        scores = masked_scores(query_block, keys_all, first_row, block_rows, device, rows_dev)
        row_peak = jnp.max(scores, axis=-1, keepdims=True)
        row_total = jnp.sum(jnp.exp(scores - row_peak), axis=-1, keepdims=True)
        log_total = row_peak + jnp.log(row_total)
        shares_bf = jnp.exp(scores - log_total).astype(jnp.bfloat16)
        attended = jnp.einsum(
            "qkgs,skd->qkgd", shares_bf, values_all, preferred_element_type=jnp.float32
        )
        return (attended, log_total[..., 0])

    shaped = queries.reshape((blocks, block_rows) + queries.shape[1:])
    attended, log_totals = lax.map(one_block, (shaped, starts))
    return (attended.reshape(queries.shape), log_totals.reshape(queries.shape[:3]))


def attention_backward(queries, keys_all, values_all, grad_attended, log_totals, device):
    rows_dev = queries.shape[0]
    block_rows, blocks, starts = block_layout(queries)

    def one_block(carried, block_item):
        key_grad, value_grad = carried
        query_block, grad_block, total_block, first_row = block_item
        scores = masked_scores(query_block, keys_all, first_row, block_rows, device, rows_dev)
        shares = jnp.exp(scores - total_block[..., None])
        grad_shares = jnp.einsum(
            "qkgd,skd->qkgs", grad_block, values_all, preferred_element_type=jnp.float32
        )
        inner_sum = jnp.sum(shares * grad_shares, axis=-1, keepdims=True)
        grad_scores = (shares * (grad_shares - inner_sum)).astype(jnp.bfloat16)
        grad_query = jnp.einsum(
            "qkgs,skd->qkgd", grad_scores, keys_all, preferred_element_type=jnp.float32
        )
        key_grad = key_grad + jnp.einsum(
            "qkgs,qkgd->skd", grad_scores, query_block, preferred_element_type=jnp.float32
        )
        value_grad = value_grad + jnp.einsum(
            "qkgs,qkgd->skd",
            shares.astype(jnp.bfloat16),
            grad_block,
            preferred_element_type=jnp.float32,
        )
        return ((key_grad, value_grad), grad_query)

    shaped_query = queries.reshape((blocks, block_rows) + queries.shape[1:])
    shaped_grad = grad_attended.reshape((blocks, block_rows) + queries.shape[1:])
    shaped_total = log_totals.reshape((blocks, block_rows) + queries.shape[1:3])
    zero_grad = jnp.zeros(keys_all.shape, jnp.float32)
    (key_grad, value_grad), grad_query = lax.scan(
        one_block, (zero_grad, zero_grad), (shaped_query, shaped_grad, shaped_total, starts)
    )
    return (grad_query.reshape(queries.shape), key_grad, value_grad)


def core_swap(array, count):
    return lax.ppermute(array, "fsdp", [(i, i ^ 1) for i in range(count)])


def chain_shift(array, count, step, senders):
    chips = count // 2
    pairs = [
        (2 * chip + core, 2 * (chip + step) + core)
        for chip in range(chips)
        if 0 <= chip + step < chips and senders(chip)
        for core in range(2)
    ]
    return lax.ppermute(array, "fsdp", pairs)


def chain_gather(array, count, chip):
    chips = count // 2
    right, left = [array], [array]
    for hop in range(1, chips):
        right.append(chain_shift(right[-1], count, 1, lambda i, hop=hop: i >= hop - 1))
        left.append(chain_shift(left[-1], count, -1, lambda i, hop=hop: i <= chips - hop))
    lower = chip < chips // 2
    reach = jnp.maximum(chip, chips - 1 - chip)
    slots = [array]
    for j in range(1, chips):
        far = jnp.where(lower, left[j], right[j])
        if j > chips // 2:
            near = jnp.where(lower, right[chips - j], left[chips - j])
            far = jnp.where(j <= reach, far, near)
        slots.append(far)
    return slots


def chain_reduce(slots, count, chip):
    chips = count // 2
    lower = chip < chips // 2
    going_right, going_left = None, None
    for distance in range(chips - 1, 0, -1):
        near, far = slots[distance], slots[chips - distance]
        up = near if distance * 2 == chips else jnp.where(lower, near, far)
        down = near if distance * 2 == chips else jnp.where(lower, far, near)
        if going_right is not None:
            up = up + going_right.astype(jnp.float32)
            down = down + going_left.astype(jnp.float32)
        going_right = chain_shift(
            up.astype(jnp.bfloat16), count, 1, lambda i, d=distance: i + d <= chips - 1
        )
        going_left = chain_shift(
            down.astype(jnp.bfloat16), count, -1, lambda i, d=distance: i - d >= 0
        )
    return slots[0] + going_right.astype(jnp.float32) + going_left.astype(jnp.float32)


def body(
    tokens,
    layer_input,
    cotangent,
    norm_gains,
    qk_gains,
    w_qkv,
    w_out,
    laurel_left,
    laurel_right,
    w_gate_up,
    w_down,
    pli_gate,
    pli_proj,
):
    count = lax.axis_size("fsdp")
    device = lax.axis_index("fsdp")
    chip = device // 2
    rows_dev = tokens.shape[0]
    prompt_len = PROMPT_DEVS * rows_dev
    groups = H // KVH
    bf = jnp.bfloat16

    small = jnp.concatenate(
        [
            norm_gains.astype(bf).reshape(-1),
            qk_gains.astype(bf).reshape(-1),
            laurel_left.astype(bf).reshape(-1),
            laurel_right.astype(bf).reshape(-1),
            pli_gate.astype(bf).reshape(-1),
            pli_proj.astype(bf).reshape(-1),
        ]
    )
    small_all = lax.all_gather(small, "fsdp", axis=0, tiled=False)
    qkv_all = lax.all_gather(w_qkv.astype(bf), "fsdp", axis=0, tiled=True)
    out_all = lax.all_gather(w_out.astype(bf), "fsdp", axis=0, tiled=True)
    sizes = [a.size for a in (norm_gains, qk_gains, laurel_left, laurel_right, pli_gate, pli_proj)]
    starts = [sum(sizes[:i]) for i in range(len(sizes))]
    parts = [small_all[:, s : s + z] for s, z in zip(starts, sizes)]
    gains = jnp.moveaxis(parts[0].reshape((count,) + norm_gains.shape), 0, 1).reshape(
        norm_gains.shape[0], -1
    ).astype(jnp.float32)
    qk_gain = jnp.moveaxis(parts[1].reshape((count,) + qk_gains.shape), 0, 1).reshape(
        qk_gains.shape[0], -1
    ).astype(jnp.float32)
    left_all = parts[2].reshape(-1, laurel_left.shape[1])
    right_all = parts[3].reshape(-1, laurel_right.shape[1])
    pgate_all = parts[4].reshape(-1, pli_gate.shape[1])
    pproj_all = parts[5].reshape(-1, pli_proj.shape[1])

    w_gate = w_gate_up[:, 0].astype(bf)
    w_up = w_gate_up[:, 1].astype(bf)
    w_down_bf = w_down.astype(bf)

    inputs = tokens.astype(jnp.float32)
    extra_input = layer_input.astype(jnp.float32)

    def input_norm(tensor, gain_rows):
        return rms_norm(tensor) * gain_rows[0]

    normed, input_pull = jax.vjp(input_norm, inputs, gains)
    normed_bf = normed.astype(bf)
    projected = jnp.dot(normed_bf, qkv_all, preferred_element_type=jnp.float32)
    local_rows = jnp.arange(rows_dev, dtype=jnp.int32)
    places = jnp.where(
        device < PROMPT_DEVS, device * rows_dev + local_rows, prompt_len + local_rows % CONT_LEN
    )

    def head_prep(projected, gain_pair):
        query_part = projected[:, : H * HD].reshape(rows_dev, H, HD)
        key_part = projected[:, H * HD : (H + KVH) * HD].reshape(rows_dev, KVH, HD)
        value_part = projected[:, (H + KVH) * HD :].reshape(rows_dev, KVH, HD)
        queries = rotary(rms_norm(query_part) * gain_pair[0], places).reshape(
            rows_dev, KVH, groups, HD
        )
        return (queries, rotary(rms_norm(key_part) * gain_pair[1], places), rms_norm(value_part))

    (queries, keys_own, values_own), prep_pull = jax.vjp(head_prep, projected, qk_gain)
    queries_bf = queries.astype(bf)
    keys_bf = keys_own.astype(bf)
    values_bf = values_own.astype(bf)
    kv_own = jnp.concatenate(
        [keys_bf.reshape(rows_dev, KVH * HD), values_bf.reshape(rows_dev, KVH * HD)], axis=1
    )
    kv_all = lax.all_gather(kv_own, "fsdp", axis=0, tiled=True)
    kv_seen = jnp.concatenate([kv_all[:prompt_len], kv_own], axis=0)
    keys_all = kv_seen[:, : KVH * HD].reshape(-1, KVH, HD)
    values_all = kv_seen[:, KVH * HD :].reshape(-1, KVH, HD)
    attended, log_totals = attention_forward(queries_bf, keys_all, values_all, device)
    attended_bf = attended.reshape(rows_dev, H * HD).astype(bf)
    attn_proj = jnp.dot(attended_bf, out_all, preferred_element_type=jnp.float32)
    laurel_mid = jnp.dot(normed_bf, left_all, preferred_element_type=jnp.float32).astype(bf)
    laurel_out = jnp.dot(laurel_mid, right_all, preferred_element_type=jnp.float32)

    def middle(inputs, normed, attn_proj, laurel_out, gain_rows):
        first_sum = inputs + rms_norm(attn_proj) * gain_rows[1]
        laurel_sum = normed + rms_norm(laurel_out) * gain_rows[2]
        stream = (first_sum + laurel_sum) * HALF_ROOT
        return (stream, rms_norm(stream) * gain_rows[3])

    (stream, ffn_in), middle_pull = jax.vjp(middle, inputs, normed, attn_proj, laurel_out, gains)

    def both_cores(slots):
        return [jnp.concatenate([slot, core_swap(slot, count)], axis=0) for slot in slots]

    def own_rows(partials):
        kept = []
        for partial in partials:
            other = core_swap(partial[rows_dev:].astype(bf), count)
            kept.append(partial[:rows_dev] + other.astype(jnp.float32))
        return kept

    def gelu_pair(gate, up):
        return jax.nn.gelu(gate, approximate=True) * up

    blocks_in = both_cores(chain_gather(ffn_in.astype(bf), count, chip))
    hiddens, hidden_pulls, partials = [], [], []
    for block in blocks_in:
        gate = back_dot(block, w_gate)
        up = back_dot(block, w_up)
        hidden, pull = jax.vjp(gelu_pair, gate, up)
        hidden = hidden.astype(bf)
        hiddens.append(hidden)
        hidden_pulls.append(pull)
        partials.append(jnp.dot(hidden, w_down_bf, preferred_element_type=jnp.float32))
    ffn_out = chain_reduce(own_rows(partials), count, chip)

    def tail_norm(stream, ffn_out, gain_rows):
        return stream + rms_norm(ffn_out) * gain_rows[4]

    after_ffn, tail_pull = jax.vjp(tail_norm, stream, ffn_out, gains)
    after_bf = after_ffn.astype(bf)
    pli_pre = jnp.dot(after_bf, pgate_all, preferred_element_type=jnp.float32)

    def pli_mix(pli_pre, extra_input):
        return jax.nn.gelu(pli_pre, approximate=True) * extra_input

    pli_mid, pli_pull = jax.vjp(pli_mix, pli_pre, extra_input)
    pli_mid_bf = pli_mid.astype(bf)
    pli_out = jnp.dot(pli_mid_bf, pproj_all, preferred_element_type=jnp.float32)

    def final_norm(after_ffn, pli_out, gain_rows):
        return after_ffn + rms_norm(pli_out) * gain_rows[5]

    result, final_pull = jax.vjp(final_norm, after_ffn, pli_out, gains)
    grad_after, grad_pli_out, gain_final = final_pull(cotangent.astype(jnp.float32))
    grad_pli_out_bf = grad_pli_out.astype(bf)
    grad_pproj = outer_sum(pli_mid_bf, grad_pli_out_bf)
    grad_pli_mid = back_dot(grad_pli_out_bf, pproj_all)
    grad_pli_pre, grad_extra = pli_pull(grad_pli_mid)
    grad_pli_pre_bf = grad_pli_pre.astype(bf)
    grad_pgate = outer_sum(after_bf, grad_pli_pre_bf)
    grad_after = grad_after + back_dot(grad_pli_pre_bf, pgate_all)
    grad_stream, grad_ffn_out, gain_tail = tail_pull(grad_after)

    blocks_grad = both_cores(chain_gather(grad_ffn_out.astype(bf), count, chip))
    gates, ups, partials = [], [], []
    for block, pull in zip(blocks_grad, hidden_pulls):
        gate, up = pull(back_dot(block, w_down_bf))
        gate, up = gate.astype(bf), up.astype(bf)
        gates.append(gate)
        ups.append(up)
        partials.append(
            jnp.dot(gate, w_gate, preferred_element_type=jnp.float32)
            + jnp.dot(up, w_up, preferred_element_type=jnp.float32)
        )
    grad_ffn_in = chain_reduce(own_rows(partials), count, chip)
    rows_in = jnp.concatenate(blocks_in, axis=0)
    rows_grad = jnp.concatenate(blocks_grad, axis=0)
    grad_down_w = outer_sum(jnp.concatenate(hiddens, axis=0), rows_grad).astype(bf)
    grad_gate_w = outer_sum(jnp.concatenate(gates, axis=0), rows_in).astype(bf)
    grad_up_w = outer_sum(jnp.concatenate(ups, axis=0), rows_in).astype(bf)
    down_sum = lax.psum(grad_down_w, "rep")
    gate_sum = lax.psum(grad_gate_w, "rep")
    up_sum = lax.psum(grad_up_w, "rep")

    grad_inputs, grad_normed, grad_attn_proj, grad_laurel_out, gain_middle = middle_pull(
        (grad_stream, grad_ffn_in)
    )
    grad_attn_bf = grad_attn_proj.astype(bf)
    grad_out_w = outer_sum(attended_bf, grad_attn_bf)
    grad_attended = (
        back_dot(grad_attn_bf, out_all).astype(bf).reshape(rows_dev, KVH, groups, HD)
    )
    grad_laurel_bf = grad_laurel_out.astype(bf)
    grad_right_w = outer_sum(laurel_mid, grad_laurel_bf)
    grad_mid_bf = back_dot(grad_laurel_bf, right_all).astype(bf)
    grad_left_w = outer_sum(normed_bf, grad_mid_bf)
    grad_normed = grad_normed + back_dot(grad_mid_bf, left_all)
    grad_queries, key_grad, value_grad = attention_backward(
        queries_bf, keys_all, values_all, grad_attended, log_totals, device
    )
    kv_grad = jnp.concatenate(
        [key_grad.reshape(-1, KVH * HD), value_grad.reshape(-1, KVH * HD)], axis=1
    )
    prompt_kv = lax.psum(kv_grad[:prompt_len].astype(bf), "fsdp")
    owner_start = jnp.minimum(device, PROMPT_DEVS - 1) * rows_dev
    kv_sum = jnp.where(
        device < PROMPT_DEVS,
        lax.dynamic_slice_in_dim(prompt_kv, owner_start, rows_dev, 0).astype(jnp.float32),
        kv_grad[prompt_len:],
    )
    key_sum = kv_sum[:, : KVH * HD].reshape(rows_dev, KVH, HD)
    value_sum = kv_sum[:, KVH * HD :].reshape(rows_dev, KVH, HD)
    grad_projected, grad_qk_gain = prep_pull((grad_queries, key_sum, value_sum))
    grad_proj_bf = grad_projected.astype(bf)
    grad_qkv_w = outer_sum(normed_bf, grad_proj_bf)
    grad_normed = grad_normed + back_dot(grad_proj_bf, qkv_all)
    grad_first, gain_input = input_pull(grad_normed)
    grad_tokens = grad_inputs + grad_first
    gain_total = gain_final + gain_tail + gain_middle + gain_input

    def shard_rows(array):
        return array.astype(bf).reshape(count, -1)

    def shard_columns(array):
        return jnp.moveaxis(array.astype(bf).reshape(array.shape[0], count, -1), 1, 0).reshape(
            count, -1
        )

    small_grad = jnp.concatenate(
        [
            shard_columns(gain_total),
            shard_columns(grad_qk_gain),
            shard_rows(grad_left_w),
            shard_rows(grad_right_w),
            shard_rows(grad_pgate),
            shard_rows(grad_pproj),
        ],
        axis=1,
    )
    out_sum = lax.psum(
        lax.psum_scatter(grad_out_w.astype(bf), "fsdp", scatter_dimension=0, tiled=True), "rep"
    )
    small_sum = lax.psum(
        lax.psum_scatter(small_grad, "fsdp", scatter_dimension=0, tiled=False), "rep"
    ).astype(jnp.float32)
    qkv_sum = lax.psum(
        lax.psum_scatter(grad_qkv_w.astype(bf), "fsdp", scatter_dimension=0, tiled=True), "rep"
    )
    pieces = [
        small_sum[s : s + z].reshape(a.shape)
        for s, z, a in zip(
            starts, sizes, (norm_gains, qk_gains, laurel_left, laurel_right, pli_gate, pli_proj)
        )
    ]
    return (
        result.astype(bf),
        grad_tokens,
        grad_extra,
        pieces[0],
        pieces[1],
        qkv_sum.astype(jnp.float32),
        out_sum.astype(jnp.float32),
        pieces[2],
        pieces[3],
        jnp.stack([gate_sum, up_sum], axis=1).astype(jnp.float32),
        down_sum.astype(jnp.float32),
        pieces[4],
        pieces[5],
    )


def solution(mesh):
    placed = (
        P(("rep", "fsdp"), None),
        P(("rep", "fsdp"), None),
        P(("rep", "fsdp"), None),
        P(None, "fsdp"),
        P(None, "fsdp"),
        P("fsdp", None),
        P("fsdp", None),
        P("fsdp", None),
        P("fsdp", None),
        P("fsdp", None, None),
        P("fsdp", None),
        P("fsdp", None),
        P("fsdp", None),
    )
    return jax.shard_map(
        body,
        mesh=mesh,
        in_specs=placed,
        out_specs=(
            P(("rep", "fsdp"), None),
            P(("rep", "fsdp"), None),
            P(("rep", "fsdp"), None),
            P(None, "fsdp"),
            P(None, "fsdp"),
            P("fsdp", None),
            P("fsdp", None),
            P("fsdp", None),
            P("fsdp", None),
            P("fsdp", None, None),
            P("fsdp", None),
            P("fsdp", None),
            P("fsdp", None),
        ),
        check_vma=False,
    )
```

time: 3130 us -> 1730 us (0.55)
  waiting for transfers between devices: 2630 us -> 1110 us
  local copies, waits for them, and re-layouts: 82.5 us -> 202 us
  blocking collectives: 58 us -> 0 us
  starting transfers between devices: 0.87 us -> 52.5 us
  matrix products: 254 us -> 221 us
    reduce_scatter x9 -> x2, waiting for transfers between devices: 1270 us -> 213 us  [the longest x1 130 us: body(): lax.psum_scatter(grad_qkv_w.astype(bf), 'fsdp', scatter_dimension=0, tile...]
    all_gather x8 -> x3, waiting for transfers between devices: 970 us -> 197 us  [the longest x1 112 us: body(): qkv_all = lax.all_gather(w_qkv.astype(bf), 'fsdp', axis=0, tiled=True)]
    ppermute x0 -> x40, waiting for transfers between devices: none -> 282 us  [the longest x24 281 us: chain_shift(): return lax.ppermute(array, 'fsdp', pairs)]
    dot_general x10 -> x18, matrix products: 139 us -> 51.4 us  [the longest x4 13.2 us: body(): jnp.dot(gate, w_gate, preferred_element_type=jnp.float32)]
    unnamed x22 -> x11, waiting for transfers between devices: 0.37 us -> 80.7 us
    all_gather x4 -> x0, blocking collectives: 58 us -> none  [the longest x1 15.3 us: body(): lax.all_gather(laurel_left.astype(jnp.bfloat16), 'fsdp', axis=0, tiled=True)]
    ppermute x0 -> x40, starting transfers between devices: none -> 51.8 us  [the longest x24 50 us: chain_shift(): return lax.ppermute(array, 'fsdp', pairs)]
    psum x3 -> x2, waiting for transfers between devices: 384 us -> 336 us  [the longest x1 291 us: body(): lax.psum(lax.psum_scatter(small_grad, 'fsdp', scatter_dimension=0, tiled=...]
  transfers between devices with their start and end apart: 21 -> 49, of which waited for: 16 -> 29; matrix products, arithmetic and copies ran while one was open for 8% -> 17% of each run, Pallas kernels for 0% -> 0%
where the time goes in v1:
time: 1730 us; the launch traced here: 1710 us
  waiting for transfers between devices  1110 us (64%)
  matrix products  221 us (13%)
  local copies, waits for them, and re-layouts  202 us (12%)
  other arithmetic  112 us (6%)
  starting transfers between devices  52.5 us (3%)
  between operations  17.4 us (1%)
    psum x1, waiting for transfers between devices, body(): lax.psum(lax.psum_scatter(small_grad, 'fsdp', scatter_dimension=0, tiled=...  291 us
    ppermute x24, waiting for transfers between devices, chain_shift(): return lax.ppermute(array, 'fsdp', pairs)  281 us
    reduce_scatter x1, waiting for transfers between devices, body(): lax.psum_scatter(grad_qkv_w.astype(bf), 'fsdp', scatter_dimension=0, tile...  130 us
    all_gather x1, waiting for transfers between devices, body(): qkv_all = lax.all_gather(w_qkv.astype(bf), 'fsdp', axis=0, tiled=True)  112 us
    unnamed x354, local copies, waits for them, and re-layouts  107 us
    reduce_scatter x1, waiting for transfers between devices, body(): lax.psum_scatter(grad_out_w.astype(bf), 'fsdp', scatter_dimension=0, tile...  82.7 us
    dot_general x18, matrix products, back_dot(): lax.dot_general(gradient, weight, (((1,), (1,)), ((), ())), preferred_ele...  82.2 us
    unnamed x11, waiting for transfers between devices  80.7 us
  transfers between devices with their start and end apart: 49, of which 29 were waited for; matrix products, arithmetic and copies ran while one was open for 17% of the time, Pallas kernels for 0%

profile of v1, /device:TPU:0, one launch (start us, length us, event | category | flops | bytes accessed | tf_op | source)
XLA Modules:
  0.0 1714.6 jit_solution(15972415385394576671)
XLA Ops:
  27.2 67.9 %all-reduce.25.cloned.1.call-done = bf16[1323520]{0:T(1024)(128)(2,1)} async-done(((bf16[1323520]{0:T(1024)(128)(2,1)}), bf16[1323520]{0:T(1024)(128)(2,1)}) %all-reduce.25.cloned.1.call-update) | async-done | bytes 2647056
  102.0 111.7 %all-gather.5.cloned.1.call-done = bf16[2048,3072]{1,0:T(8,128)(2,1)} async-done(((bf16[256,3072]{1,0:T(8,128)(2,1)}), bf16[2048,3072]{1,0:T(8,128)(2,1)}) %all-gather.5.cloned.1.call-update) | async-done | bytes 12582928 | tf_op jit(solution)/shard_map/all_gather | solution.py:236
  244.0 29.3 %all-gather.7.cloned.1.call-done = bf16[2048,1024]{1,0:T(8,128)(2,1)} async-done(((bf16[256,1024]{1,0:T(8,128)(2,1)}), bf16[2048,1024]{1,0:T(8,128)(2,1)}) %all-gather.7.cloned.1.call-update) | async-done | bytes 4194320 | tf_op jit(solution)/shard_map/all_gather | solution.py:286
  299.8 56.3 %all-gather.9.cloned.1.call-done = bf16[2048,2048]{1,0:T(8,128)(2,1)} async-done(((bf16[256,2048]{1,0:T(8,128)(2,1)}), bf16[2048,2048]{1,0:T(8,128)(2,1)}) %all-gather.9.cloned.1.call-update) | async-done | bytes 8388624 | tf_op jit(solution)/shard_map/all_gather | solution.py:237
  370.9 19.6 %collective-permute-done.3 = bf16[256,2048]{1,0:T(8,128)(2,1)S(1)} collective-permute-done((bf16[256,2048]{1,0:T(8,128)(2,1)}, bf16[256,2048]{1,0:T(8,128)(2,1)S(1)}, u32[]{:S(2)}, u32[]{:S(2)}) %collective-permute-start.3) | collective-permute-done | bytes 1048608 | tf_op jit(solution)/shard_map/ppermute | solution.py:161
  404.8 17.6 %copy.218 = bf16[1024,2,2048]{2,0,1:T(8,128)(2,1)S(1)} copy(f32[1024,2,2048]{2,1,0:T(2,128)} %param.22) | data formatting | bytes 25165824 | tf_op args[9]
  444.3 14.5 collective-permute-done.7
  488.7 22.8 %collective-permute-done.14 = bf16[256,2048]{1,0:T(8,128)(2,1)S(1)} collective-permute-done((bf16[256,2048]{1,0:T(8,128)(2,1)S(1)}, bf16[256,2048]{1,0:T(8,128)(2,1)S(1)}, u32[]{:S(2)}, u32[]{:S(2)}) %collective-permute-start.14) | collective-permute-done | bytes 1048608 | tf_op jit(solution)/shard_map/ppermute | solution.py:161
  517.4 21.3 %collective-permute-done.15 = bf16[256,2048]{1,0:T(8,128)(2,1)} collective-permute-done((bf16[256,2048]{1,0:T(8,128)(2,1)S(1)}, bf16[256,2048]{1,0:T(8,128)(2,1)}, u32[]{:S(2)}, u32[]{:S(2)}) %collective-permute-start.15) | collective-permute-done | bytes 1048608 | tf_op jit(solution)/shard_map/ppermute | solution.py:161
  572.7 13.0 collective-permute-done.16
  585.7 33.5 %collective-permute-done.19 = bf16[256,2048]{1,0:T(8,128)(2,1)} collective-permute-done((bf16[256,2048]{1,0:T(8,128)(2,1)}, bf16[256,2048]{1,0:T(8,128)(2,1)}, u32[]{:S(2)}, u32[]{:S(2)}) %collective-permute-start.19) | collective-permute-done | bytes 1048608 | tf_op jit(solution)/shard_map/ppermute | solution.py:161
  638.5 21.6 %collective-permute-done.23 = bf16[256,2048]{1,0:T(8,128)(2,1)S(1)} collective-permute-done((bf16[256,2048]{1,0:T(8,128)(2,1)S(1)}, bf16[256,2048]{1,0:T(8,128)(2,1)S(1)}, u32[]{:S(2)}, u32[]{:S(2)}) %collective-permute-start.23) | collective-permute-done | bytes 1048608 | tf_op jit(solution)/shard_map/ppermute | solution.py:161
  671.7 22.2 %collective-permute-done.26 = bf16[256,2048]{1,0:T(8,128)(2,1)S(1)} collective-permute-done((bf16[256,2048]{1,0:T(8,128)(2,1)S(1)}, bf16[256,2048]{1,0:T(8,128)(2,1)S(1)}, u32[]{:S(2)}, u32[]{:S(2)}) %collective-permute-start.26) | collective-permute-done | bytes 1048608 | tf_op jit(solution)/shard_map/ppermute | solution.py:161
  707.9 15.7 collective-permute-done.27
  762.5 22.7 %collective-permute-done.34 = bf16[256,2048]{1,0:T(8,128)(2,1)S(1)} collective-permute-done((bf16[256,2048]{1,0:T(8,128)(2,1)S(1)}, bf16[256,2048]{1,0:T(8,128)(2,1)S(1)}, u32[]{:S(2)}, u32[]{:S(2)}) %collective-permute-start.34) | collective-permute-done | bytes 1048608 | tf_op jit(solution)/shard_map/ppermute | solution.py:161
  791.1 21.4 %collective-permute-done.35 = bf16[256,2048]{1,0:T(8,128)(2,1)} collective-permute-done((bf16[256,2048]{1,0:T(8,128)(2,1)S(1)}, bf16[256,2048]{1,0:T(8,128)(2,1)}, u32[]{:S(2)}, u32[]{:S(2)}) %collective-permute-start.35) | collective-permute-done | bytes 1048608 | tf_op jit(solution)/shard_map/ppermute | solution.py:161
  850.7 8.9 collective-permute-done.36
  859.6 33.7 %collective-permute-done.39 = bf16[256,2048]{1,0:T(8,128)(2,1)} collective-permute-done((bf16[256,2048]{1,0:T(8,128)(2,1)}, bf16[256,2048]{1,0:T(8,128)(2,1)}, u32[]{:S(2)}, u32[]{:S(2)}) %collective-permute-start.39) | collective-permute-done | bytes 1048608 | tf_op jit(solution)/shard_map/ppermute | solution.py:161
  907.1 8.0 fusion.128
  973.7 45.1 %all-reduce.23.cloned.1.call-done = bf16[1024,1024]{1,0:T(8,128)(2,1)} async-done(((bf16[1024,1024]{1,0:T(8,128)(2,1)}), bf16[1024,1024]{1,0:T(8,128)(2,1)}) %all-reduce.23.cloned.1.call-update) | async-done | bytes 2097168 | tf_op jit(solution)/shard_map/psum | solution.py:397
  1031.6 9.7 fusion.176
  1075.0 8.6 convolution_convert_fusion
  1087.3 13.8 convert_bitcast_fusion
  1101.1 10.6 convert_bitcast_fusion.1
  1111.7 12.1 fusion.31
  1123.9 12.7 all-reduce.27.cloned.1.call-done
  1136.6 8.9 dynamic-slice_reduce_fusion
  1145.4 82.7 %reduce-scatter.5.cloned.1.call-done = bf16[256,2048]{1,0:T(8,128)(2,1)} async-done(((bf16[2048,2048]{1,0:T(8,128)(2,1)}), bf16[256,2048]{1,0:T(8,128)(2,1)}) %reduce-scatter.5.cloned.1.call-update) | async-done | bytes 1048592 | tf_op jit(solution)/shard_map/reduce_scatter | solution.py:434
  1228.2 130.5 %reduce-scatter.3.cloned.1.call-done = bf16[256,3072]{1,0:T(8,128)(2,1)} async-done(((bf16[2048,3072]{1,0:T(8,128)(2,1)}), bf16[256,3072]{1,0:T(8,128)(2,1)}) %reduce-scatter.3.cloned.1.call-update) | async-done | bytes 1572880 | tf_op jit(solution)/shard_map/reduce_scatter | solution.py:440
  1362.9 291.3 %all-reduce.29.cloned.1.call-done = (bf16[165440]{0:T(1024)(128)(2,1)}, bf16[256,3072]{1,0:T(8,128)(2,1)}, bf16[256,2048]{1,0:T(8,128)(2,1)}, bf16[1024,1,2048]{...) async-done(((bf16[165440]{0:T(1024)(128)(2,1)}, bf16[256,3072]{1,0:T(8,128)(2,1)}, bf16[256,2048]{1,0:T(8,128)(2,1)}, ...) | async-done | bytes 15535248 | tf_op jit(solution)/shard_map/psum | solution.py:436
  1670.1 9.1 maximum_convert_fusion
  1679.2 28.6 %copy.169 = f32[1024,2,2048]{2,1,0:T(2,128)} copy(f32[1024,2,2048]{2,0,1:T(8,128)} %maximum_convert_fusion) | data formatting | bytes 33554432
  (661 shorter events, 471.9 us)
Async XLA Ops:
  7.2 88.0 %all-reduce.25.cloned.1.call-start = ((), (), s32[]{:S(2)}) async-start(), calls=%async_computation.8 | async-start | bytes 5296128
  22.9 190.9 %all-gather.5.cloned.1.call-start = ((), (), s32[]{:S(2)}) async-start(), calls=%async_computation.2 | async-start | bytes 14155776 | tf_op jit(solution)/shard_map/all_gather | solution.py:236
  26.3 247.0 %all-gather.7.cloned.1.call-start = ((), (), s32[]{:S(2)}) async-start(), calls=%async_computation.3 | async-start | bytes 4718592 | tf_op jit(solution)/shard_map/all_gather | solution.py:286
  227.7 128.4 %all-gather.9.cloned.1.call-start = ((), (), s32[]{:S(2)}) async-start(), calls=%async_computation.4 | async-start | bytes 9437184 | tf_op jit(solution)/shard_map/all_gather | solution.py:237
  230.5 788.3 %all-reduce.23.cloned.1.call-start = ((), (), s32[]{:S(2)}) async-start(), calls=%async_computation.5 | async-start | bytes 4194304 | tf_op jit(solution)/shard_map/psum | solution.py:397
  365.9 24.7 %collective-permute-start.3 = (bf16[256,2048]{1,0:T(8,128)(2,1)}, bf16[256,2048]{1,0:T(8,128)(2,1)S(1)}, u32[]{:S(2)}, u32[]{:S(2)}) collective-permute-start(bf16[256,2048]{1,0:T(8,128)(2,1)} %get-tuple-element.183), channel_id=1, source_target_pairs={{0,2},{1,3},{2,4},{3,5},{4,6},{5,7},{8,10},{9,11},{10,12},{11,13},... | collective-permute-start | bytes 3145736 | tf_op jit(solution)/shard_map/ppermute | solution.py:161
  367.2 27.6 %collective-permute-start.2 = (bf16[256,2048]{1,0:T(8,128)(2,1)}, bf16[256,2048]{1,0:T(8,128)(2,1)}, u32[]{:S(2)}, u32[]{:S(2)}) collective-permute-start(bf16[256,2048]{1,0:T(8,128)(2,1)} %get-tuple-element.183), channel_id=1, source_target_pairs={{2,0},{3,1},{4,2},{5,3},{6,4},{7,5},{10,8},{11,9},{12,10},{13,11},... | collective-permute-start | bytes 3145736 | tf_op jit(solution)/shard_map/ppermute | solution.py:161
  397.8 24.6 %collective-permute-start.4 = (bf16[256,2048]{1,0:T(8,128)(2,1)}, bf16[256,2048]{1,0:T(8,128)(2,1)}, u32[]{:S(2)}, u32[]{:S(2)}) collective-permute-start(bf16[256,2048]{1,0:T(8,128)(2,1)} %get-tuple-element.181), channel_id=1, source_target_pairs={{0,1},{1,0},{2,3},{3,2},{4,5},{5,4},{6,7},{7,6},{8,9},{9,8},{10,11... | collective-permute-start | bytes 3145736 | tf_op jit(solution)/shard_map/ppermute | solution.py:150
  397.8 28.3 %collective-permute-start.8 = (bf16[256,2048]{1,0:T(8,128)(2,1)S(1)}, bf16[256,2048]{1,0:T(8,128)(2,1)}, u32[]{:S(2)}, u32[]{:S(2)}) collective-permute-start(bf16[256,2048]{1,0:T(8,128)(2,1)S(1)} %collective-permute-done.3), channel_id=1, source_target_pairs={{2,4},{3,5},{4,6},{5,7},{10,12},{11,13},{12,14},{13,15},{18,20},{1... | collective-permute-start | bytes 3145736 | tf_op jit(solution)/shard_map/ppermute | solution.py:161
  399.5 28.4 %collective-permute-start.6 = (bf16[256,2048]{1,0:T(8,128)(2,1)}, bf16[256,2048]{1,0:T(8,128)(2,1)}, u32[]{:S(2)}, u32[]{:S(2)}) collective-permute-start(bf16[256,2048]{1,0:T(8,128)(2,1)} %collective-permute-done.2), channel_id=1, source_target_pairs={{2,0},{3,1},{4,2},{5,3},{10,8},{11,9},{12,10},{13,11},{18,16},{19,... | collective-permute-start | bytes 3145736 | tf_op jit(solution)/shard_map/ppermute | solution.py:161
  431.1 27.7 %collective-permute-start.7 = (bf16[256,2048]{1,0:T(8,128)(2,1)}, bf16[256,2048]{1,0:T(8,128)(2,1)S(1)}, u32[]{:S(2)}, u32[]{:S(2)}) collective-permute-start(bf16[256,2048]{1,0:T(8,128)(2,1)} %collective-permute-done.6), channel_id=1, source_target_pairs={{2,0},{3,1},{10,8},{11,9},{18,16},{19,17},{26,24},{27,25}} | collective-permute-start | bytes 3145736 | tf_op jit(solution)/shard_map/ppermute | solution.py:161
  463.0 23.0 %collective-permute-start.5 = (bf16[256,2048]{1,0:T(8,128)(2,1)S(1)}, bf16[256,2048]{1,0:T(8,128)(2,1)S(1)}, u32[]{:S(2)}, u32[]{:S(2)}) collective-permute-start(bf16[256,2048]{1,0:T(8,128)(2,1)S(1)} %slice.404), channel_id=1, source_target_pairs={{0,1},{1,0},{2,3},{3,2},{4,5},{5,4},{6,7},{7,6},{8,9},{9,8},{10,11... | collective-permute-start | bytes 3145736 | tf_op jit(solution)/shard_map/ppermute | solution.py:150
  486.9 24.6 %collective-permute-start.14 = (bf16[256,2048]{1,0:T(8,128)(2,1)S(1)}, bf16[256,2048]{1,0:T(8,128)(2,1)S(1)}, u32[]{:S(2)}, u32[]{:S(2)}) collective-permute-start(bf16[256,2048]{1,0:T(8,128)(2,1)S(1)} %get-tuple-element.194), channel_id=1, source_target_pairs={{0,2},{1,3},{8,10},{9,11},{16,18},{17,19},{24,26},{25,27}} | collective-permute-start | bytes 3145736 | tf_op jit(solution)/shard_map/ppermute | solution.py:161
  512.0 26.7 %collective-permute-start.15 = (bf16[256,2048]{1,0:T(8,128)(2,1)S(1)}, bf16[256,2048]{1,0:T(8,128)(2,1)}, u32[]{:S(2)}, u32[]{:S(2)}) collective-permute-start(bf16[256,2048]{1,0:T(8,128)(2,1)S(1)} %add_convert_fusion.9), channel_id=1, source_target_pairs={{0,2},{1,3},{2,4},{3,5},{8,10},{9,11},{10,12},{11,13},{16,18},{17,... | collective-permute-start | bytes 3145736 | tf_op jit(solution)/shard_map/ppermute | solution.py:161
  547.2 16.1 collective-permute-start.18
  557.3 15.4 collective-permute-start.1
  557.3 28.4 %collective-permute-start.16 = (bf16[256,2048]{1,0:T(8,128)(2,1)}, bf16[256,2048]{1,0:T(8,128)(2,1)}, u32[]{:S(2)}, u32[]{:S(2)}) collective-permute-start(bf16[256,2048]{1,0:T(8,128)(2,1)} %get-tuple-element.192), channel_id=1, source_target_pairs={{0,2},{1,3},{2,4},{3,5},{4,6},{5,7},{8,10},{9,11},{10,12},{11,13},... | collective-permute-start | bytes 3145736 | tf_op jit(solution)/shard_map/ppermute | solution.py:161
  564.7 54.5 %collective-permute-start.19 = (bf16[256,2048]{1,0:T(8,128)(2,1)}, bf16[256,2048]{1,0:T(8,128)(2,1)}, u32[]{:S(2)}, u32[]{:S(2)}) collective-permute-start(bf16[256,2048]{1,0:T(8,128)(2,1)} %add_convert_fusion.6), channel_id=1, source_target_pairs={{2,0},{3,1},{4,2},{5,3},{6,4},{7,5},{10,8},{11,9},{12,10},{13,11},... | collective-permute-start | bytes 3145736 | tf_op jit(solution)/shard_map/ppermute | solution.py:161
  633.3 26.7 %collective-permute-start.23 = (bf16[256,2048]{1,0:T(8,128)(2,1)S(1)}, bf16[256,2048]{1,0:T(8,128)(2,1)S(1)}, u32[]{:S(2)}, u32[]{:S(2)}) collective-permute-start(bf16[256,2048]{1,0:T(8,128)(2,1)S(1)} %get-tuple-element.175), channel_id=1, source_target_pairs={{0,2},{1,3},{2,4},{3,5},{4,6},{5,7},{8,10},{9,11},{10,12},{11,13},... | collective-permute-start | bytes 3145736 | tf_op jit(solution)/shard_map/ppermute | solution.py:161
  637.0 27.2 %collective-permute-start.22 = (bf16[256,2048]{1,0:T(8,128)(2,1)S(1)}, bf16[256,2048]{1,0:T(8,128)(2,1)S(1)}, u32[]{:S(2)}, u32[]{:S(2)}) collective-permute-start(bf16[256,2048]{1,0:T(8,128)(2,1)S(1)} %get-tuple-element.175), channel_id=1, source_target_pairs={{2,0},{3,1},{4,2},{5,3},{6,4},{7,5},{10,8},{11,9},{12,10},{13,11},... | collective-permute-start | bytes 3145736 | tf_op jit(solution)/shard_map/ppermute | solution.py:161
  665.4 28.5 %collective-permute-start.26 = (bf16[256,2048]{1,0:T(8,128)(2,1)S(1)}, bf16[256,2048]{1,0:T(8,128)(2,1)S(1)}, u32[]{:S(2)}, u32[]{:S(2)}) collective-permute-start(bf16[256,2048]{1,0:T(8,128)(2,1)S(1)} %collective-permute-done.22), channel_id=1, source_target_pairs={{2,0},{3,1},{4,2},{5,3},{10,8},{11,9},{12,10},{13,11},{18,16},{19,... | collective-permute-start | bytes 3145736 | tf_op jit(solution)/shard_map/ppermute | solution.py:161
  696.3 27.3 %collective-permute-start.27 = (bf16[256,2048]{1,0:T(8,128)(2,1)S(1)}, bf16[256,2048]{1,0:T(8,128)(2,1)S(1)}, u32[]{:S(2)}, u32[]{:S(2)}) collective-permute-start(bf16[256,2048]{1,0:T(8,128)(2,1)S(1)} %collective-permute-done.26), channel_id=1, source_target_pairs={{2,0},{3,1},{10,8},{11,9},{18,16},{19,17},{26,24},{27,25}} | collective-permute-start | bytes 3145736 | tf_op jit(solution)/shard_map/ppermute | solution.py:161
  727.9 32.0 %collective-permute-start.25 = (bf16[256,2048]{1,0:T(8,128)(2,1)S(1)}, bf16[256,2048]{1,0:T(8,128)(2,1)S(1)}, u32[]{:S(2)}, u32[]{:S(2)}) collective-permute-start(bf16[256,2048]{1,0:T(8,128)(2,1)S(1)} %slice.400), channel_id=1, source_target_pairs={{0,1},{1,0},{2,3},{3,2},{4,5},{5,4},{6,7},{7,6},{8,9},{9,8},{10,11... | collective-permute-start | bytes 3145736 | tf_op jit(solution)/shard_map/ppermute | solution.py:150
  760.6 24.6 %collective-permute-start.34 = (bf16[256,2048]{1,0:T(8,128)(2,1)S(1)}, bf16[256,2048]{1,0:T(8,128)(2,1)S(1)}, u32[]{:S(2)}, u32[]{:S(2)}) collective-permute-start(bf16[256,2048]{1,0:T(8,128)(2,1)S(1)} %get-tuple-element.188), channel_id=1, source_target_pairs={{0,2},{1,3},{8,10},{9,11},{16,18},{17,19},{24,26},{25,27}} | collective-permute-start | bytes 3145736 | tf_op jit(solution)/shard_map/ppermute | solution.py:161
  785.7 26.8 %collective-permute-start.35 = (bf16[256,2048]{1,0:T(8,128)(2,1)S(1)}, bf16[256,2048]{1,0:T(8,128)(2,1)}, u32[]{:S(2)}, u32[]{:S(2)}) collective-permute-start(bf16[256,2048]{1,0:T(8,128)(2,1)S(1)} %add_convert_fusion.4), channel_id=1, source_target_pairs={{0,2},{1,3},{2,4},{3,5},{8,10},{9,11},{10,12},{11,13},{16,18},{17,... | collective-permute-start | bytes 3145736 | tf_op jit(solution)/shard_map/ppermute | solution.py:161
  831.2 19.6 %collective-permute-start.21 = (bf16[256,2048]{1,0:T(8,128)(2,1)}, bf16[256,2048]{1,0:T(8,128)(2,1)}, u32[]{:S(2)}, u32[]{:S(2)}) collective-permute-start(bf16[256,2048]{1,0:T(8,128)(2,1)} %slice.401), channel_id=1, source_target_pairs={{0,1},{1,0},{2,3},{3,2},{4,5},{5,4},{6,7},{7,6},{8,9},{9,8},{10,11... | collective-permute-start | bytes 3145736 | tf_op jit(solution)/shard_map/ppermute | solution.py:150
  831.2 28.4 %collective-permute-start.36 = (bf16[256,2048]{1,0:T(8,128)(2,1)}, bf16[256,2048]{1,0:T(8,128)(2,1)}, u32[]{:S(2)}, u32[]{:S(2)}) collective-permute-start(bf16[256,2048]{1,0:T(8,128)(2,1)} %get-tuple-element.186), channel_id=1, source_target_pairs={{0,2},{1,3},{2,4},{3,5},{4,6},{5,7},{8,10},{9,11},{10,12},{11,13},... | collective-permute-start | bytes 3145736 | tf_op jit(solution)/shard_map/ppermute | solution.py:161
  838.6 54.8 %collective-permute-start.39 = (bf16[256,2048]{1,0:T(8,128)(2,1)}, bf16[256,2048]{1,0:T(8,128)(2,1)}, u32[]{:S(2)}, u32[]{:S(2)}) collective-permute-start(bf16[256,2048]{1,0:T(8,128)(2,1)} %add_convert_fusion.1), channel_id=1, source_target_pairs={{2,0},{3,1},{4,2},{5,3},{6,4},{7,5},{10,8},{11,9},{12,10},{13,11},... | collective-permute-start | bytes 3145736 | tf_op jit(solution)/shard_map/ppermute | solution.py:161
  953.5 183.1 %all-reduce.27.cloned.1.call-start = ((), (), s32[]{:S(2)}) async-start(), calls=%async_computation.9 | async-start | bytes 5296128
  1067.4 160.8 %reduce-scatter.5.cloned.1.call-start = ((), (), s32[]{:S(2)}) async-start(), calls=%async_computation.7 | async-start | bytes 9437184 | tf_op jit(solution)/shard_map/reduce_scatter | solution.py:434
  1074.9 283.7 %reduce-scatter.3.cloned.1.call-start = ((), (), s32[]{:S(2)}) async-start(), calls=%async_computation.6 | async-start | bytes 14155776 | tf_op jit(solution)/shard_map/reduce_scatter | solution.py:440
  1083.5 570.7 %all-reduce.29.cloned.1.call-start = ((), (), s32[]{:S(2)}) async-start(), calls=%async_computation.10 | async-start | bytes 31072256 | tf_op jit(solution)/shard_map/psum | solution.py:436
  (178 other events, 3573.5 us)
Sparse Core Ops, SparseCore 0:
  23.0 72.1 all-reduce.24
  97.3 116.3 all-gather.4
  227.9 45.3 all-gather.6
  275.3 80.7 all-gather.8
  953.6 65.2 all-reduce.22
  1067.5 69.0 all-reduce.26
  1138.9 89.2 reduce-scatter.4
  1231.0 127.5 reduce-scatter.2
  1364.4 289.7 all-reduce.28

commit v2 on v0

v2 whole, which is shorter than its diff:
```python
import jax
import jax.numpy as jnp
from jax import lax
from jax.experimental import pallas as pl
from jax.experimental.pallas import tpu as pltpu
from jax.sharding import PartitionSpec as P

H = 8
KVH = 2
HD = 256
CONT_LEN = 256
PROMPT_DEVS = 4
CHUNKS = 1

EPSILON = 1e-06
THETA_BASE = 1000000.0
HALF_ROOT = 0.7071067811865476
NEG_FILL = -1e30
GELU_SCALE = 0.7978845608028654
GELU_CUBIC = 0.044715
BF = jnp.bfloat16
F32 = jnp.float32


def rms_norm(tensor):
    return tensor * lax.rsqrt(jnp.mean(tensor * tensor, axis=-1, keepdims=True) + EPSILON)


def dot(left_mat, right_mat):
    return jnp.dot(left_mat, right_mat, preferred_element_type=F32)


def outer_sum(left_mat, right_mat):
    return lax.dot_general(
        left_mat, right_mat, (((0,), (0,)), ((), ())), preferred_element_type=F32
    )


def back_dot(gradient, weight):
    return lax.dot_general(
        gradient, weight, (((1,), (1,)), ((), ())), preferred_element_type=F32
    )


def turn(tensor, cosine, sine, back=False):
    half = tensor.shape[-1] // 2
    first, second = tensor[:, :half], tensor[:, half:]
    if back:
        return jnp.concatenate(
            [first * cosine + second * sine, second * cosine - first * sine], axis=-1
        )
    return jnp.concatenate(
        [first * cosine - second * sine, second * cosine + first * sine], axis=-1
    )


def head_norm(tensor):
    inverse = lax.rsqrt(jnp.mean(tensor * tensor, axis=-1, keepdims=True) + EPSILON)
    return tensor * inverse, inverse


def head_norm_back(normed, inverse, gradient):
    return inverse * (gradient - normed * jnp.mean(gradient * normed, axis=-1, keepdims=True))


def head_shares(queries, keys, device):
    rows, key_count = queries.shape[0], keys.shape[0]
    prompt_len = key_count - rows
    scores = back_dot(queries, keys)
    local = lax.broadcasted_iota(jnp.int32, scores.shape, 0)
    index = lax.broadcasted_iota(jnp.int32, scores.shape, 1)
    own = index - prompt_len
    in_prompt = device < PROMPT_DEVS
    last_seen = jnp.where(in_prompt, device * rows, prompt_len) + local
    allowed = index <= last_seen
    if rows > CONT_LEN:
        piece = jnp.logical_or(own < 0, own // CONT_LEN == local // CONT_LEN)
        allowed = jnp.logical_and(allowed, piece)
    scores = jnp.where(allowed, scores, NEG_FILL)
    grown = jnp.exp(scores - jnp.max(scores, axis=-1, keepdims=True))
    return grown / jnp.sum(grown, axis=-1, keepdims=True)


def head_specs(rows, key_count):
    head = pl.BlockSpec((rows, HD), lambda h: (0, h))
    half = pl.BlockSpec((rows, HD // 2), lambda h: (0, 0))
    gain = pl.BlockSpec((2, HD), lambda h: (0, 0))
    keys = pl.BlockSpec((key_count, HD), lambda h: (0, h // (H // KVH)))
    values = pl.BlockSpec((key_count, HD), lambda h: (0, KVH + h // (H // KVH)))
    return head, half, gain, keys, values


def attend(projected, cosine, sine, gains, kv_seen, device):
    rows, key_count = projected.shape[0], kv_seen.shape[0]
    head, half, gain, keys, values = head_specs(rows, key_count)

    def kernel(at_ref, x_ref, c_ref, s_ref, g_ref, k_ref, v_ref, q_ref, o_ref):
        normed, _ = head_norm(x_ref[...])
        queries = turn(normed * g_ref[0:1, :], c_ref[...], s_ref[...]).astype(BF)
        q_ref[...] = queries
        shares = head_shares(queries, k_ref[...], at_ref[0])
        o_ref[...] = dot(shares.astype(BF), v_ref[...]).astype(BF)

    return pl.pallas_call(
        kernel,
        grid=(H,),
        in_specs=[pl.BlockSpec(memory_space=pltpu.SMEM), head, half, half, gain, keys, values],
        out_specs=[head, head],
        out_shape=[jax.ShapeDtypeStruct((rows, H * HD), BF)] * 2,
        cost_estimate=pl.CostEstimate(
            flops=4 * rows * H * HD * key_count,
            bytes_accessed=rows * H * HD * 8 + key_count * KVH * HD * 4,
            transcendentals=rows * H * key_count,
        ),
        name="attend",
    )(device.reshape(1), projected, cosine, sine, gains, kv_seen, kv_seen)


def attend_back(projected, queries, cosine, sine, gains, kv_seen, gradient, device):
    rows, key_count = projected.shape[0], kv_seen.shape[0]
    groups = H // KVH
    head, half, gain, keys, values = head_specs(rows, key_count)

    def kernel(
        at_ref, x_ref, q_ref, c_ref, s_ref, g_ref, k_ref, v_ref, do_ref,
        dx_ref, dk_ref, dv_ref, dg_ref,
    ):
        queries, grad = q_ref[...], do_ref[...]
        shares = head_shares(queries, k_ref[...], at_ref[0])
        grad_shares = back_dot(grad, v_ref[...])
        inner = jnp.sum(shares * grad_shares, axis=-1, keepdims=True)
        grad_scores = (shares * (grad_shares - inner)).astype(BF)
        key_grad = outer_sum(grad_scores, queries)
        value_grad = outer_sum(shares.astype(BF), grad)
        first = lax.rem(pl.program_id(0), groups) == 0

        @pl.when(first)
        def _():
            dk_ref[...] = key_grad
            dv_ref[...] = value_grad

        @pl.when(jnp.logical_not(first))
        def _():
            dk_ref[...] += key_grad
            dv_ref[...] += value_grad

        turned = turn(dot(grad_scores, k_ref[...]), c_ref[...], s_ref[...], back=True)
        normed, inverse = head_norm(x_ref[...])
        dg_ref[...] = jnp.sum(turned * normed, axis=0, keepdims=True)[None]
        dx_ref[...] = head_norm_back(normed, inverse, turned * g_ref[0:1, :]).astype(BF)

    shared = pl.BlockSpec((key_count, HD), lambda h: (0, h // groups))
    return pl.pallas_call(
        kernel,
        grid=(H,),
        in_specs=[
            pl.BlockSpec(memory_space=pltpu.SMEM), head, head, half, half, gain, keys, values, head,
        ],
        out_specs=[head, shared, shared, pl.BlockSpec((1, 1, HD), lambda h: (h, 0, 0))],
        out_shape=[
            jax.ShapeDtypeStruct((rows, H * HD), BF),
            jax.ShapeDtypeStruct((key_count, KVH * HD), F32),
            jax.ShapeDtypeStruct((key_count, KVH * HD), F32),
            jax.ShapeDtypeStruct((H, 1, HD), F32),
        ],
        cost_estimate=pl.CostEstimate(
            flops=10 * rows * H * HD * key_count,
            bytes_accessed=rows * H * HD * 10 + key_count * KVH * HD * 12,
            transcendentals=rows * H * key_count,
        ),
        name="attend_back",
    )(
        device.reshape(1), projected, queries, cosine, sine, gains, kv_seen, kv_seen, gradient,
    )


def kv_prep(projected, cosine, sine, gains):
    rows = projected.shape[0]

    def kernel(x_ref, c_ref, s_ref, g_ref, out_ref):
        for head in range(2 * KVH):
            columns = slice(head * HD, (head + 1) * HD)
            normed, _ = head_norm(x_ref[:, columns])
            if head < KVH:
                normed = turn(normed * g_ref[1:2, :], c_ref[...], s_ref[...])
            out_ref[:, columns] = normed.astype(BF)

    return pl.pallas_call(
        kernel,
        out_shape=jax.ShapeDtypeStruct((rows, 2 * KVH * HD), BF),
        name="kv_prep",
    )(projected, cosine, sine, gains)


def kv_prep_back(projected, gradient, cosine, sine, gains):
    rows = projected.shape[0]

    def kernel(x_ref, d_ref, c_ref, s_ref, g_ref, dx_ref, dg_ref):
        gain_grad = jnp.zeros((1, HD), F32)
        for head in range(2 * KVH):
            columns = slice(head * HD, (head + 1) * HD)
            normed, inverse = head_norm(x_ref[:, columns])
            grad = d_ref[:, columns]
            if head < KVH:
                grad = turn(grad, c_ref[...], s_ref[...], back=True)
                gain_grad = gain_grad + jnp.sum(grad * normed, axis=0, keepdims=True)
                grad = grad * g_ref[1:2, :]
            dx_ref[:, columns] = head_norm_back(normed, inverse, grad).astype(BF)
        dg_ref[...] = gain_grad

    return pl.pallas_call(
        kernel,
        out_shape=[
            jax.ShapeDtypeStruct((rows, 2 * KVH * HD), BF),
            jax.ShapeDtypeStruct((1, HD), F32),
        ],
        name="kv_prep_back",
    )(projected, gradient, cosine, sine, gains)


class Place:
    def __init__(self):
        self.count = lax.axis_size("fsdp")
        self.copies = lax.axis_size("rep")
        self.device = lax.axis_index("fsdp")
        self.copy = lax.axis_index("rep")
        self.chips = self.count // 2
        self.chip = self.device // 2
        self.core = self.device % 2
        self.at_end = jnp.logical_or(self.chip == 0, self.chip == self.chips - 1)
        self.four = self.chips == 4

    def core_swap(self, array):
        return lax.ppermute(array, "fsdp", [(i, i ^ 1) for i in range(self.count)])

    def copy_swap(self, array, mask):
        return lax.ppermute(array, "rep", [(i, i ^ mask) for i in range(self.copies)])

    def chip_send(self, array, moves):
        pairs = [(2 * a + core, 2 * b + core) for a, b in moves for core in range(2)]
        return lax.ppermute(array, "fsdp", pairs)

    def by_core(self, mine, other):
        first = self.core == 0
        return jnp.where(first, mine, other), jnp.where(first, other, mine)

    def owner(self, j):
        return self.chip ^ j

    def chip_swap(self, array, mask):
        return self.chip_send(array, [(i, i ^ mask) for i in range(self.chips)])

    def spread_near(self, array):
        if not self.four:
            return [self.chip_swap(array, mask) for mask in range(1, self.chips)]
        return [self.chip_swap(array, 1), self.chip_swap(array, 2)]

    def spread_far(self, array, near):
        if not self.four:
            return []
        ends = self.chip_send(near[1], [(1, 0), (2, 3)])
        return [jnp.where(self.at_end, ends, self.chip_send(array, [(1, 2), (2, 1)]))]

    def spread(self, array):
        near = self.spread_near(array)
        return [array] + near + self.spread_far(array, near)

    def collect_near(self, parts):
        if not self.four:
            return [
                self.chip_swap(parts[mask].astype(BF), mask) for mask in range(1, self.chips)
            ]
        last = parts[3].astype(BF)
        return [
            self.chip_send(last, [(0, 1), (3, 2)]),
            self.chip_swap(parts[1].astype(BF), 1),
            self.chip_send(last, [(1, 2), (2, 1)]),
        ]

    def collect_far(self, parts, near):
        if not self.four:
            return near
        return near[1:] + [self.chip_swap((parts[2] + near[0].astype(F32)).astype(BF), 2)]

    def collect_sum(self, own, arrived):
        total = own
        for array in arrived:
            total = total + array.astype(F32)
        return total

    def in_order(self, pieces):
        block = jnp.concatenate(pieces, axis=0)
        rows, columns = block.shape
        bit = 1
        while bit < self.copies:
            split = block.reshape(self.copies // (2 * bit), 2, rows // self.copies * bit, columns)
            flipped = jnp.concatenate([split[:, 1:], split[:, :1]], axis=1)
            block = jnp.where((self.copy // bit) % 2 == 1, flipped, split).reshape(rows, columns)
            bit *= 2
        return block

    def swap_copies(self, array):
        if self.copies != 4:
            return [array] + [self.copy_swap(array, mask) for mask in range(1, self.copies)]
        half = array.shape[0] // 2
        first, second = self.copy_swap(array, 1), self.copy_swap(array, 2)
        last = [self.copy_swap(second[:half], 1), self.copy_swap(first[half:], 2)]
        return [array, first, second, jnp.concatenate(last, axis=0)]

    def lay_out(self, shard, shard_other, lane, lane_other, copies):
        rows, columns = shard.shape
        share = rows // copies
        chips, count = self.chips, self.count
        where = jnp.stack(
            [self.chip, self.core, self.copy if copies > 1 else 0]
            + [self.owner(j) for j in range(1, chips)]
        ).astype(jnp.int32)

        def kernel(at_ref, shard_ref, other_ref, lane_ref, lane_other_ref, whole_ref):
            core = at_ref[1]
            for side, (own, far) in enumerate(
                ((shard_ref, lane_ref), (other_ref, lane_other_ref))
            ):
                on = core if side == 0 else 1 - core
                base = pl.multiple_of((2 * at_ref[0] + on) * rows, rows)
                whole_ref[pl.ds(base, rows), :] = own[...]
                for j in range(1, chips):
                    base = (2 * at_ref[2 + j] + on) * rows
                    for mask in range(copies):
                        spot = pl.multiple_of(
                            base + jnp.bitwise_xor(at_ref[2], mask) * share, share
                        )
                        start = (mask * (chips - 1) + j - 1) * share
                        whole_ref[pl.ds(spot, share), :] = far[start : start + share, :]

        return pl.pallas_call(
            kernel,
            out_shape=jax.ShapeDtypeStruct((count * rows, columns), shard.dtype),
            in_specs=[pl.BlockSpec(memory_space=pltpu.SMEM)]
            + [pl.BlockSpec(memory_space=pltpu.VMEM)] * 4,
            out_specs=pl.BlockSpec(memory_space=pltpu.VMEM),
            name="lay_out",
        )(where, shard, shard_other, lane, lane_other)

    def own_share(self, shard):
        share = shard.shape[0] // self.copies
        return lax.dynamic_slice_in_dim(shard, self.copy * share, share, 0)

    def along_chain(self, own):
        return jnp.concatenate(self.spread(own)[1:], axis=0)

    def across_copies(self, slots):
        return jnp.concatenate(self.swap_copies(slots), axis=0)

    def lanes(self, whole):
        rows = whole.shape[0] // self.count
        split = whole.reshape(self.chips, 2, rows, whole.shape[1])
        return [
            lax.dynamic_index_in_dim(split, core, 1, keepdims=False).reshape(-1, whole.shape[1])
            for core in (self.core, 1 - self.core)
        ]

    def lane_outer(self, left, right, core):
        rows = left.shape[1] // self.count
        height, width = right.shape

        def kernel(at_ref, left_ref, right_ref, out_ref):
            out_ref[...] = outer_sum(left_ref[...], right_ref[...]).astype(BF)

        return pl.pallas_call(
            kernel,
            grid_spec=pltpu.PrefetchScalarGridSpec(
                num_scalar_prefetch=1,
                grid=(self.chips,),
                in_specs=[
                    pl.BlockSpec((height, rows), lambda i, at: (0, 2 * i + at[0])),
                    pl.BlockSpec((height, width), lambda i, at: (0, 0)),
                ],
                out_specs=pl.BlockSpec((rows, width), lambda i, at: (i, 0)),
            ),
            out_shape=jax.ShapeDtypeStruct((self.chips * rows, width), BF),
            cost_estimate=pl.CostEstimate(
                flops=2 * height * self.chips * rows * width,
                bytes_accessed=2 * (height + self.chips * rows) * width,
                transcendentals=0,
            ),
            name="lane_outer",
        )(core.reshape(1), left, right)

    def lane_parts(self, mine, arrived):
        rows = arrived[0].shape[0] // self.chips

        def part(chip):
            sums = [
                lax.dynamic_slice_in_dim(own, chip * rows, rows, 0).astype(F32)
                + lax.dynamic_slice_in_dim(other, chip * rows, rows, 0).astype(F32)
                for own, other in zip(mine, arrived)
            ]
            return jnp.concatenate(sums, axis=-1)

        return [part(self.owner(j)) for j in range(self.chips)]

    def copies_sum(self, array):
        share = array.shape[0] // self.copies
        array = array.astype(BF)

        def take(mask):
            return lax.dynamic_slice_in_dim(array, (self.copy ^ mask) * share, share, 0)

        total = take(0).astype(F32)
        for mask in range(1, self.copies):
            total = total + self.copy_swap(take(mask), mask).astype(F32)
        return total.astype(BF)

    def copies_all(self, total):
        return self.in_order(
            [total] + [self.copy_swap(total, mask) for mask in range(1, self.copies)]
        )


def half_specs(units, width, tile):
    tiles = units // tile
    return [
        pl.BlockSpec((tile, width), lambda i: (jnp.minimum(i, tiles - 1), 0)),
        pl.BlockSpec((tile, width), lambda i: (jnp.maximum(i - tiles, 0), 0)),
    ]


def gelu_parts(value):
    inner = GELU_SCALE * (value + GELU_CUBIC * value * value * value)
    bent = jnp.tanh(inner)
    slope = GELU_SCALE * (1.0 + 3.0 * GELU_CUBIC * value * value)
    return 0.5 * value * (1.0 + bent), 0.5 * (1.0 + bent) + 0.5 * value * (1.0 - bent * bent) * slope


def stack_rows(refs):
    values = [ref[...] for ref in refs]
    return values[0] if len(values) == 1 else jnp.concatenate(values, axis=0)


def ffn_block(blocks, gates, ups, downs, sum_type):
    (piece, width), count = blocks[0].shape, len(blocks)
    rows = piece * count
    units = gates[0].shape[0]
    tile = min(units, 512)
    tiles = units // tile

    def kernel(*refs):
        x_refs, (g0, g1, u0, u1, d0, d1) = refs[:count], refs[count : count + 6]
        sum_refs = refs[count + 6 : 2 * count + 6]
        hid_ref, gate_ref, up_ref, total = refs[2 * count + 6 :]
        step = pl.program_id(0)

        def work(g_ref, u_ref, d_ref):
            x = stack_rows(x_refs)
            gate, up = back_dot(x, g_ref[...]), back_dot(x, u_ref[...])
            bent = jnp.tanh(GELU_SCALE * (gate + GELU_CUBIC * gate * gate * gate))
            hidden = (0.5 * gate * (1.0 + bent) * up).astype(BF)
            hid_ref[...] = hidden
            gate_ref[...] = gate.astype(BF)
            up_ref[...] = up.astype(BF)
            return dot(hidden, d_ref[...])

        @pl.when(step == 0)
        def _():
            total[...] = work(g0, u0, d0)

        @pl.when(jnp.logical_and(step > 0, step < tiles))
        def _():
            total[...] += work(g0, u0, d0)

        @pl.when(step >= tiles)
        def _():
            total[...] += work(g1, u1, d1)

        @pl.when(step == 2 * tiles - 1)
        def _():
            for i, sum_ref in enumerate(sum_refs):
                sum_ref[...] = total[i * piece : (i + 1) * piece, :].astype(sum_type)

    whole = pl.BlockSpec((piece, width), lambda i: (0, 0))
    part = pl.BlockSpec((rows, tile), lambda i: (0, i))
    *sums, hidden, gate, up = pl.pallas_call(
        kernel,
        grid=(2 * tiles,),
        in_specs=[whole] * count + half_specs(units, width, tile) * 3,
        out_specs=[whole] * count + [part] * 3,
        out_shape=[jax.ShapeDtypeStruct((piece, width), sum_type)] * count
        + [jax.ShapeDtypeStruct((rows, 2 * units), BF)] * 3,
        scratch_shapes=[pltpu.VMEM((rows, width), F32)],
        cost_estimate=pl.CostEstimate(
            flops=12 * rows * width * units,
            bytes_accessed=12 * units * width + 12 * rows * units + 6 * rows * width,
            transcendentals=2 * rows * units,
        ),
        name="ffn_block",
    )(*blocks, *gates, *ups, *downs)
    return sums, hidden, gate, up


def ffn_block_back(grads, gate, up, gates, ups, downs, sum_type):
    (piece, width), count = grads[0].shape, len(grads)
    rows = piece * count
    units = gates[0].shape[0]
    tile = min(units, 512)
    tiles = units // tile

    def kernel(*refs):
        x_refs, (gate_ref, up_ref) = refs[:count], refs[count : count + 2]
        g0, g1, u0, u1, d0, d1 = refs[count + 2 : count + 8]
        sum_refs = refs[count + 8 : 2 * count + 8]
        dg_ref, du_ref, total = refs[2 * count + 8 :]
        step = pl.program_id(0)

        def work(g_ref, u_ref, d_ref):
            value, slope = gelu_parts(gate_ref[...].astype(F32))
            hidden = back_dot(stack_rows(x_refs), d_ref[...])
            grad_gate = (hidden * up_ref[...].astype(F32) * slope).astype(BF)
            grad_up = (hidden * value).astype(BF)
            dg_ref[...] = grad_gate
            du_ref[...] = grad_up
            return dot(grad_gate, g_ref[...]) + dot(grad_up, u_ref[...])

        @pl.when(step == 0)
        def _():
            total[...] = work(g0, u0, d0)

        @pl.when(jnp.logical_and(step > 0, step < tiles))
        def _():
            total[...] += work(g0, u0, d0)

        @pl.when(step >= tiles)
        def _():
            total[...] += work(g1, u1, d1)

        @pl.when(step == 2 * tiles - 1)
        def _():
            for i, sum_ref in enumerate(sum_refs):
                sum_ref[...] = total[i * piece : (i + 1) * piece, :].astype(sum_type)

    whole = pl.BlockSpec((piece, width), lambda i: (0, 0))
    part = pl.BlockSpec((rows, tile), lambda i: (0, i))
    *sums, grad_gate, grad_up = pl.pallas_call(
        kernel,
        grid=(2 * tiles,),
        in_specs=[whole] * count + [part, part] + half_specs(units, width, tile) * 3,
        out_specs=[whole] * count + [part] * 2,
        out_shape=[jax.ShapeDtypeStruct((piece, width), sum_type)] * count
        + [jax.ShapeDtypeStruct((rows, 2 * units), BF)] * 2,
        scratch_shapes=[pltpu.VMEM((rows, width), F32)],
        cost_estimate=pl.CostEstimate(
            flops=12 * rows * width * units,
            bytes_accessed=12 * units * width + 16 * rows * units + 6 * rows * width,
            transcendentals=2 * rows * units,
        ),
        name="ffn_block_back",
    )(*grads, gate, up, *gates, *ups, *downs)
    return sums, grad_gate, grad_up


def outer_blocks(lefts, rights, start, columns, added=None, whole=None, place=0, places=1):
    width = rights[0].shape[1]
    tile = min(columns, 256)
    n_left, tiles = len(lefts), columns // tile
    n_both = n_left + len(rights)

    def kernel(*refs):
        out_ref = refs[-1]
        total = outer_sum(stack_rows(refs[:n_left]), stack_rows(refs[n_left:n_both]))
        if added is not None:
            total = total + refs[n_both][...].astype(F32)
        out_ref[...] = total.astype(BF)

    rows = sum(left.shape[0] for left in lefts)
    operands = [*lefts, *rights]
    specs = [pl.BlockSpec((left.shape[0], tile), lambda i: (0, i + start // tile)) for left in lefts]
    specs += [pl.BlockSpec(right.shape, lambda i: (0, 0)) for right in rights]
    if added is not None:
        operands.append(added)
        specs.append(pl.BlockSpec((tile, width), lambda i: (i, 0)))
    aliases = {}
    if whole is not None:
        aliases = {len(operands): 0}
        operands.append(whole)
        specs.append(pl.BlockSpec(memory_space=pl.ANY))
    return pl.pallas_call(
        kernel,
        grid=(tiles,),
        in_specs=specs,
        out_specs=pl.BlockSpec((tile, width), lambda i: (i + place * tiles, 0)),
        out_shape=jax.ShapeDtypeStruct((places * columns, width), BF),
        input_output_aliases=aliases,
        cost_estimate=pl.CostEstimate(
            flops=2 * rows * columns * width,
            bytes_accessed=2 * rows * (columns + width) + 4 * columns * width,
            transcendentals=0,
        ),
        name="outer_blocks",
    )(*operands)


def split_pair(pair):
    units, _, width = pair.shape
    rows = min(units, 128)

    def kernel(pair_ref, first_ref, second_ref):
        first_ref[...] = pair_ref[:, 0, :].astype(BF)
        second_ref[...] = pair_ref[:, 1, :].astype(BF)

    flat = pl.BlockSpec((rows, width), lambda i: (i, 0))
    return pl.pallas_call(
        kernel,
        grid=(units // rows,),
        in_specs=[pl.BlockSpec((rows, 2, width), lambda i: (i, 0, 0))],
        out_specs=[flat, flat],
        out_shape=[jax.ShapeDtypeStruct((units, width), BF)] * 2,
        cost_estimate=pl.CostEstimate(
            flops=0, bytes_accessed=units * width * 12, transcendentals=0
        ),
        name="split_pair",
    )(pair)


def join_pair(stacked, units):
    width = stacked.shape[1]
    rows = min(units, 128)
    tiles = units // rows

    def kernel(first_ref, second_ref, pair_ref):
        pair_ref[:, 0, :] = first_ref[...].astype(F32)
        pair_ref[:, 1, :] = second_ref[...].astype(F32)

    return pl.pallas_call(
        kernel,
        grid=(tiles,),
        in_specs=[
            pl.BlockSpec((rows, width), lambda i: (i + tiles, 0)),
            pl.BlockSpec((rows, width), lambda i: (i + 2 * tiles, 0)),
        ],
        out_specs=pl.BlockSpec((rows, 2, width), lambda i: (i, 0, 0)),
        out_shape=jax.ShapeDtypeStruct((units, 2, width), F32),
        cost_estimate=pl.CostEstimate(
            flops=0, bytes_accessed=units * width * 12, transcendentals=0
        ),
        name="join_pair",
    )(stacked, stacked)


def tie(*values):
    return lax.optimization_barrier(values)


def body(
    tokens,
    layer_input,
    cotangent,
    norm_gains,
    qk_gains,
    w_qkv,
    w_out,
    laurel_left,
    laurel_right,
    w_gate_up,
    w_down,
    pli_gate,
    pli_proj,
):
    at = Place()
    device = at.device
    rows_dev, width = tokens.shape
    shard = w_qkv.shape[0]
    prompt_len = PROMPT_DEVS * rows_dev
    q_cols = H * HD
    lr, pd = laurel_left.shape[1], pli_gate.shape[1]
    n_gain, n_qk = norm_gains.size, qk_gains.size

    def pack_gains(norm_part, qk_part):
        flat = jnp.concatenate([norm_part.reshape(-1), qk_part.reshape(-1)]).astype(BF)
        flat = jnp.pad(flat, (0, shard * 128 - flat.size))
        return flat.reshape(shard, 128)

    kv_pack = jnp.concatenate(
        [w_qkv[:, q_cols:].astype(BF), pack_gains(norm_gains, qk_gains)], axis=1
    )
    def gather_all(array):
        return lax.all_gather(at.own_share(array), ("fsdp", "rep"), axis=0, tiled=True)

    main_all = gather_all(
        jnp.concatenate(
            [
                w_qkv[:, :q_cols].astype(BF),
                w_out.astype(BF),
                laurel_left.astype(BF),
                laurel_right.astype(BF).reshape(shard, lr),
            ],
            axis=1,
        )
    )
    q_all = main_all[:, :q_cols]
    out_all = main_all[:, q_cols : q_cols + width]
    left_all = main_all[:, q_cols + width : q_cols + width + lr]
    right_all = main_all[:, q_cols + width + lr :].reshape(lr, width)
    pli_pack_all = gather_all(
        jnp.concatenate([pli_gate.astype(BF), pli_proj.astype(BF).reshape(shard, pd)], axis=1)
    )
    w_gate, w_up = split_pair(w_gate_up)
    w_down_bf = w_down.astype(BF)
    own_wide = (w_gate, w_up, w_down_bf)
    kv_twin = at.core_swap(kv_pack)
    kv_near = at.spread_near(kv_pack)
    kv_near, kv_twin, own_wide = tie(kv_near, kv_twin, own_wide)
    kv_far = at.spread_far(kv_pack, kv_near)
    their_wide = [at.core_swap(own) for own in own_wide]
    kv_lane = jnp.concatenate(kv_near + kv_far, axis=0)
    kv_all = at.lay_out(kv_pack, kv_twin, kv_lane, at.core_swap(kv_lane), 1)
    kv_weight = kv_all[:, : 2 * KVH * HD]
    gain_rows_all = kv_all[:, 2 * KVH * HD :].reshape(at.count, -1)[:, : n_gain + n_qk]
    gains = jnp.moveaxis(
        gain_rows_all[:, :n_gain].reshape(at.count, norm_gains.shape[0], -1), 0, 1
    ).reshape(norm_gains.shape[0], -1).astype(F32)
    qk_gain = jnp.moveaxis(
        gain_rows_all[:, n_gain:].reshape(at.count, qk_gains.shape[0], -1), 0, 1
    ).reshape(qk_gains.shape[0], -1).astype(F32)
    inputs = tokens.astype(F32)
    extra_input = layer_input.astype(F32)

    def input_norm(tensor, gain_rows):
        return rms_norm(tensor) * gain_rows[0]

    normed, input_pull = jax.vjp(input_norm, inputs, gains)
    normed_bf = normed.astype(BF)
    local_rows = jnp.arange(rows_dev, dtype=jnp.int32)
    places = jnp.where(
        device < PROMPT_DEVS, device * rows_dev + local_rows, prompt_len + local_rows % CONT_LEN
    )

    half = HD // 2
    frequency = THETA_BASE ** (-(jnp.arange(half, dtype=F32) * 2.0 / HD))
    angles = places.astype(F32)[:, None] * frequency
    cosine, sine = jnp.cos(angles), jnp.sin(angles)
    kv_proj = dot(normed_bf, kv_weight)
    kv_own = kv_prep(kv_proj, cosine, sine, qk_gain)

    prompt_chips = PROMPT_DEVS // 2
    if at.four:
        arrived = at.chip_send(kv_own, [(0, 2), (1, 3)])
        even = jnp.where(at.chip < prompt_chips, kv_own, arrived)
        odd = at.chip_swap(even, 1)
        kv_lane = [jnp.where(at.chip % 2 == i, even, odd) for i in range(2)]
    else:
        blocks = [kv_own] + [
            at.chip_send(kv_own, [(i, (i - j) % at.chips) for i in range(prompt_chips)])
            for j in range(1, at.chips)
        ]
        kv_lane = []
        for block in range(prompt_chips):
            seen = kv_own
            for j in range(1, at.chips):
                seen = jnp.where((at.chip + j) % at.chips == block, blocks[j], seen)
            kv_lane.append(seen)
    q_proj = dot(normed_bf, q_all)
    laurel_mid = dot(normed_bf, left_all).astype(BF)
    laurel_out = dot(laurel_mid, right_all)
    kv_lane, own_wide, their_wide, q_proj, laurel_out = tie(
        jnp.stack(kv_lane), own_wide, their_wide, q_proj, laurel_out
    )
    halves = list(zip(own_wide, their_wide))
    (gate_halves, up_halves, down_halves) = halves

    kv_other = at.core_swap(kv_lane)
    kv_pairs = [row for i in range(prompt_chips) for row in at.by_core(kv_lane[i], kv_other[i])]
    kv_seen = jnp.concatenate(kv_pairs + [kv_own], axis=0)
    queries_bf, attended_bf = attend(q_proj, cosine, sine, qk_gain, kv_seen, device)
    pgate_all = pli_pack_all[:, :pd]
    pproj_all = pli_pack_all[:, pd:].reshape(pd, width)
    attn_proj = dot(attended_bf, out_all)

    def middle(inputs, normed, attn_proj, laurel_out, gain_rows):
        first_sum = inputs + rms_norm(attn_proj) * gain_rows[1]
        laurel_sum = normed + rms_norm(laurel_out) * gain_rows[2]
        stream = (first_sum + laurel_sum) * HALF_ROOT
        return (stream, rms_norm(stream) * gain_rows[3])

    (stream, ffn_in), middle_pull = jax.vjp(middle, inputs, normed, attn_proj, laurel_out, gains)

    piece = rows_dev // CHUNKS
    units = w_down.shape[0]

    def staged(rows, work):
        near = at.spread_near(rows)
        first = work(0, [rows], F32)
        near, first = tie(near, first)
        far = at.spread_far(rows, near)
        pairs = [near[i : i + 2] for i in range(0, len(near), 2)]
        second = [work(j + 1, blocks, BF) for j, blocks in enumerate(pairs)]
        far, second = tie(far, second)
        parts = [part for sums, *_ in second for part in sums]
        back = [at.chip_swap(part, j + 1) for j, part in enumerate(parts)]
        done = [first, *second]
        last = None
        if far:
            third = work(len(done), far, BF)
            first_back, third = tie(back[0], third)
            back[0] = first_back
            done.append(third)
            last = third[0][0]
        return first[0][0], back, last, [kept for _, kept in done]

    def ffn_forward(rows):
        def work(j, blocks, sum_type):
            sums, *kept = ffn_block(blocks, gate_halves, up_halves, down_halves, sum_type)
            return sums, (blocks, *kept)

        own, back, last, kept = staged(rows, work)
        if last is not None:
            back = back + [at.chip_swap(last, at.chips - 1)]
        return at.collect_sum(own, back), kept

    def ffn_backward(rows, kept):
        def work(j, grads, sum_type):
            blocks, hidden, gate, up = kept[j]
            sums, grad_gate, grad_up = ffn_block_back(
                grads, gate, up, gate_halves, up_halves, down_halves, sum_type
            )
            return sums, (blocks, hidden, grads, grad_gate, grad_up)

        return staged(rows, work)

    def tail_norm(stream, ffn_out, gain_rows):
        return stream + rms_norm(ffn_out) * gain_rows[4]

    def pli_mix(pli_pre, extra_input):
        return jax.nn.gelu(pli_pre, approximate=True) * extra_input

    def final_norm(after_ffn, pli_out, gain_rows):
        return after_ffn + rms_norm(pli_out) * gain_rows[5]

    cuts = [slice(i * piece, (i + 1) * piece) for i in range(CHUNKS)]
    forwards = [ffn_forward(ffn_in[cut].astype(BF)) for cut in cuts]
    gain_total = 0.0
    results, extras, streams, ins, all_grads = [], [], [], [], []
    pli_rows = []
    for cut, (ffn_out, kept) in zip(cuts, forwards):
        after_ffn, tail_pull = jax.vjp(tail_norm, stream[cut], ffn_out, gains)
        after_bf = after_ffn.astype(BF)
        pli_mid, pli_pull = jax.vjp(pli_mix, dot(after_bf, pgate_all), extra_input[cut])
        pli_mid_bf = pli_mid.astype(BF)
        result, final_pull = jax.vjp(final_norm, after_ffn, dot(pli_mid_bf, pproj_all), gains)
        grad_after, grad_pli_out, gain_final = final_pull(cotangent[cut].astype(F32))
        grad_pli_out_bf = grad_pli_out.astype(BF)
        grad_pli_pre, grad_extra = pli_pull(back_dot(grad_pli_out_bf, pproj_all))
        grad_pli_pre_bf = grad_pli_pre.astype(BF)
        grad_after = grad_after + back_dot(grad_pli_pre_bf, pgate_all)
        grad_stream, grad_ffn_out, gain_tail = tail_pull(grad_after)
        own, back, last, grads = ffn_backward(grad_ffn_out.astype(BF), kept)
        gain_total = gain_total + gain_final + gain_tail
        results.append(result.astype(BF))
        extras.append(grad_extra)
        streams.append(grad_stream)
        ins.append((own, back, last))
        all_grads.append(grads)
        pli_rows.append((pli_mid_bf, grad_pli_out_bf, after_bf, grad_pli_pre_bf))

    kept = [[group[i] for grads in all_grads for group in grads] for i in range(5)]
    hiddens, gates, ups = kept[1], kept[3], kept[4]
    ins_blocks, outs_grad = [[block for blocks in kept[i] for block in blocks] for i in (0, 2)]
    pairs = [(hiddens, outs_grad), (gates, ins_blocks), (ups, ins_blocks)]
    theirs = [
        outer_blocks(lefts, rights, units, units) for lefts, rights in pairs
    ]
    mids, pli_outs, afters, pres = [jnp.concatenate(rows, axis=0) for rows in zip(*pli_rows)]
    grad_pproj = outer_sum(mids, pli_outs).astype(BF).reshape(-1, pd)
    grad_pgate = outer_sum(afters, pres).astype(BF)
    half_rows = piece // 2
    lasts = [last for _, _, last in ins if last is not None]
    upper = [at.chip_swap(last[:half_rows], at.chips - 1) for last in lasts]
    upper, theirs, grad_pproj, grad_pgate = tie(upper, theirs, grad_pproj, grad_pgate)
    under = [at.chip_swap(last[half_rows:], at.chips - 1) for last in lasts]
    wide_w = None
    for place, ((lefts, rights), their) in enumerate(zip(pairs, theirs)):
        wide_w = outer_blocks(
            lefts, rights, 0, units, at.core_swap(their), wide_w, place, 3
        )
    backs, under, wide_w = tie([back for _, back, _ in ins], under, wide_w)
    wide_part = lax.psum_scatter(wide_w, "rep", scatter_dimension=0, tiled=True)
    ends = [[jnp.concatenate(pair, axis=0)] for pair in zip(upper, under)] or [[]] * len(ins)
    ins = [
        at.collect_sum(own, back + end) for (own, _, _), back, end in zip(ins, backs, ends)
    ]

    grad_inputs, grad_normed, grad_attn_proj, grad_laurel_out, gain_middle = middle_pull(
        (jnp.concatenate(streams, axis=0), jnp.concatenate(ins, axis=0))
    )
    grad_attn_bf = grad_attn_proj.astype(BF)
    core, other_core = at.core, 1 - at.core
    out_leaving = at.core_swap(at.lane_outer(attended_bf, grad_attn_bf, other_core))
    out_mine = at.lane_outer(attended_bf, grad_attn_bf, core)
    grad_laurel_bf = grad_laurel_out.astype(BF)
    grad_right_w = outer_sum(laurel_mid, grad_laurel_bf).astype(BF).reshape(-1, lr)
    grad_mid_bf = back_dot(grad_laurel_bf, right_all).astype(BF)
    grad_left_w = outer_sum(normed_bf, grad_mid_bf).astype(BF)
    small_mine, small_leaving = at.lanes(
        jnp.concatenate([grad_left_w, grad_right_w, grad_pgate, grad_pproj], axis=1)
    )
    small_leaving = at.core_swap(small_leaving)
    out_leaving, small_leaving, out_mine, small_mine, grad_attn_bf = tie(
        out_leaving, small_leaving, out_mine, small_mine, grad_attn_bf
    )
    grad_attended = back_dot(grad_attn_bf, out_all).astype(BF)
    out_parts = at.lane_parts([out_mine, small_mine], [out_leaving, small_leaving])
    out_near = at.collect_near(out_parts)
    grad_q_bf, key_grad, value_grad, q_gain_rows = attend_back(
        q_proj, queries_bf, cosine, sine, qk_gain, kv_seen, grad_attended, device
    )
    out_near, grad_q_bf, key_grad, value_grad = tie(out_near, grad_q_bf, key_grad, value_grad)

    def kv_rows(first, core):
        begin = (2 * first + core) * rows_dev
        return jnp.concatenate(
            [
                lax.dynamic_slice_in_dim(grad, begin, rows_dev, 0).astype(BF)
                for grad in (key_grad, value_grad)
            ],
            axis=1,
        )

    kv_other = at.core_swap(
        jnp.stack([kv_rows(chip, other_core) for chip in range(prompt_chips)])
    )

    def kv_part(chip):
        index = jnp.clip(chip, 0, prompt_chips - 1)
        theirs = lax.dynamic_index_in_dim(kv_other, index, 0, keepdims=False)
        return kv_rows(index, core).astype(F32) + theirs.astype(F32)

    offsets = [0, 1] if at.four else range(at.chips)
    kv_parts = [
        kv_part((at.chip + j) % 2 if at.four else (at.chip + j) % at.chips) for j in offsets
    ]
    q_other_w = at.lane_outer(normed_bf, grad_q_bf, other_core)
    kv_parts, q_other_w, wide_part = tie(kv_parts, q_other_w, wide_part)
    wide_sum = lax.all_gather(wide_part, "rep", axis=0, tiled=True)
    if at.four:
        pair_sum = kv_parts[0] + at.chip_swap(kv_parts[1].astype(BF), 1).astype(F32)
        q_mine = at.lane_outer(normed_bf, grad_q_bf, core)
        pair_sum, q_mine = tie(pair_sum, q_mine)
        prompt_parts = [at.chip_send(pair_sum.astype(BF), [(2, 0), (3, 1)])]
    else:
        pair_sum = kv_parts[0]
        q_mine = at.lane_outer(normed_bf, grad_q_bf, core)
        prompt_parts = [
            at.chip_send(
                kv_parts[j].astype(BF), [((i - j) % at.chips, i) for i in range(prompt_chips)]
            )
            for j in range(1, at.chips)
        ]
    q_leaving = at.core_swap(q_other_w)
    grad_normed = grad_normed + back_dot(grad_mid_bf, left_all)
    grad_normed = grad_normed + back_dot(grad_q_bf, q_all)
    q_parts = at.lane_parts([q_mine], [q_leaving])
    prompt_parts, pair_sum, q_parts, grad_normed = tie(
        prompt_parts, pair_sum, q_parts, grad_normed
    )

    out_far = at.collect_far(out_parts, out_near)
    q_near = at.collect_near(q_parts)
    prompt_sum = pair_sum
    for sent in prompt_parts:
        prompt_sum = prompt_sum + sent.astype(F32)
    kv_sum = jnp.where(
        device < PROMPT_DEVS,
        prompt_sum,
        jnp.concatenate([key_grad[prompt_len:], value_grad[prompt_len:]], axis=1),
    )
    grad_kv_bf, k_gain_row = kv_prep_back(kv_proj, kv_sum, cosine, sine, qk_gain)
    kv_other_w = at.lane_outer(normed_bf, grad_kv_bf, other_core)
    kv_mine = at.lane_outer(normed_bf, grad_kv_bf, core)
    grad_normed = grad_normed + back_dot(grad_kv_bf, kv_weight)
    grad_first, gain_input = input_pull(grad_normed)
    grad_tokens = grad_inputs + grad_first
    gain_total = gain_total + gain_middle + gain_input
    qk_total = jnp.concatenate([jnp.sum(q_gain_rows, axis=0), k_gain_row], axis=0)

    def by_owner(array):
        return jnp.moveaxis(array.reshape(array.shape[0], at.count, -1), 1, 0).reshape(at.count, -1)

    gain_pack = jnp.concatenate([by_owner(gain_total), by_owner(qk_total)], axis=1).astype(BF)
    gain_pack = jnp.pad(gain_pack, ((0, 0), (0, shard * 128 - gain_pack.shape[1])))
    gain_mine, gain_leaving = at.lanes(gain_pack.reshape(-1, 128))
    out_far, q_near, kv_other_w, kv_mine, gain_mine, gain_leaving, grad_tokens = tie(
        out_far, q_near, kv_other_w, kv_mine, gain_mine, gain_leaving, grad_tokens
    )
    out_ready = at.collect_sum(out_parts[0], out_far).astype(BF)
    kv_leaving, gain_leaving, wide_sum, out_ready = tie(
        at.core_swap(kv_other_w), at.core_swap(gain_leaving), wide_sum, out_ready
    )
    q_far = at.collect_far(q_parts, q_near)
    kv_w_parts = at.lane_parts([kv_mine, gain_mine], [kv_leaving, gain_leaving])
    kv_near = at.collect_near(kv_w_parts)
    grad_gate_up, grad_down = join_pair(wide_sum, units), wide_sum[:units].astype(F32)
    q_far, kv_near, grad_gate_up, grad_down = tie(q_far, kv_near, grad_gate_up, grad_down)
    out_total = at.copies_sum(out_ready)
    kv_far = at.collect_far(kv_w_parts, kv_near)
    q_total = at.copies_sum(at.collect_sum(q_parts[0], q_far))
    kv_far, q_total, out_total = tie(kv_far, q_total, out_total)
    kv_total = at.copies_sum(at.collect_sum(kv_w_parts[0], kv_far))
    q_sum = at.copies_all(q_total)
    out_sum = at.copies_all(out_total)
    kv_total, q_sum, out_sum = tie(kv_total, q_sum, out_sum)
    kv_sum_w = at.copies_all(kv_total)
    gain_out = kv_sum_w[:, 2 * KVH * HD :].reshape(-1)
    return (
        jnp.concatenate(results, axis=0),
        grad_tokens,
        jnp.concatenate(extras, axis=0),
        gain_out[:n_gain].reshape(norm_gains.shape).astype(F32),
        gain_out[n_gain : n_gain + n_qk].reshape(qk_gains.shape).astype(F32),
        jnp.concatenate([q_sum, kv_sum_w[:, : 2 * KVH * HD]], axis=1).astype(F32),
        out_sum[:, :width].astype(F32),
        out_sum[:, width : width + lr].astype(F32),
        out_sum[:, width + lr : width + 2 * lr].reshape(laurel_right.shape).astype(F32),
        grad_gate_up,
        grad_down,
        out_sum[:, width + 2 * lr : width + 2 * lr + pd].astype(F32),
        out_sum[:, width + 2 * lr + pd :].reshape(pli_proj.shape).astype(F32),
    )


def solution(mesh):
    placed = (
        P(("rep", "fsdp"), None),
        P(("rep", "fsdp"), None),
        P(("rep", "fsdp"), None),
        P(None, "fsdp"),
        P(None, "fsdp"),
        P("fsdp", None),
        P("fsdp", None),
        P("fsdp", None),
        P("fsdp", None),
        P("fsdp", None, None),
        P("fsdp", None),
        P("fsdp", None),
        P("fsdp", None),
    )
    return jax.shard_map(
        body,
        mesh=mesh,
        in_specs=placed,
        out_specs=(
            P(("rep", "fsdp"), None),
            P(("rep", "fsdp"), None),
            P(("rep", "fsdp"), None),
            P(None, "fsdp"),
            P(None, "fsdp"),
            P("fsdp", None),
            P("fsdp", None),
            P("fsdp", None),
            P("fsdp", None),
            P("fsdp", None, None),
            P("fsdp", None),
            P("fsdp", None),
            P("fsdp", None),
        ),
        check_vma=False,
    )
```

time: 3130 us -> 1070 us (0.34)
  waiting for transfers between devices: 2630 us -> 412 us
  Pallas kernels: 0 us -> 275 us
  matrix products: 254 us -> 53 us
  starting transfers between devices: 0.87 us -> 141 us
  blocking collectives: 58 us -> 0 us
  local copies, waits for them, and re-layouts: 82.5 us -> 50.8 us
    reduce_scatter x9 -> x1, waiting for transfers between devices: 1270 us -> 8.54 us  [body(): wide_part = lax.psum_scatter(wide_w, 'rep', scatter_dimension=0, tiled=True)]
    all_gather x8 -> x3, waiting for transfers between devices: 970 us -> 0.04 us  [the longest x2 0.02 us: gather_all(): lax.all_gather(at.own_share(array), ('fsdp', 'rep'), axis=0, tiled=True)]
    ppermute x0 -> x68, waiting for transfers between devices: none -> 403 us  [the longest x35 354 us: chip_send(): return lax.ppermute(array, 'fsdp', pairs)]
    psum x3 -> x0, waiting for transfers between devices: 384 us -> none  [the longest x1 292 us: body(): lax.psum(grad_gate_up_w, 'rep').astype(jnp.float32)]
    pallas_call x0 -> x25, Pallas kernels: none -> 275 us  [the longest x3 59.3 us: ffn_block_back(): pl.pallas_call(kernel, grid=(2 * tiles,), in_specs=[whole] * count + [par...]
    dot_general x16 -> x7, matrix products: 166 us -> 21 us  [dot(): return jnp.dot(left_mat, right_mat, preferred_element_type=F32)]
    ppermute x0 -> x68, starting transfers between devices: none -> 140 us  [the longest x35 118 us: chip_send(): return lax.ppermute(array, 'fsdp', pairs)]
    all_gather x4 -> x0, blocking collectives: 58 us -> none  [the longest x1 15.3 us: body(): lax.all_gather(laurel_left.astype(jnp.bfloat16), 'fsdp', axis=0, tiled=True)]
  transfers between devices with their start and end apart: 21 -> 72, of which waited for: 16 -> 32; matrix products, arithmetic and copies ran while one was open for 8% -> 15% of each run, Pallas kernels for 0% -> 25%
where the time goes in v2:
time: 1070 us; the launch traced here: 1060 us
  waiting for transfers between devices  412 us (39%)
  Pallas kernels  275 us (26%)
  starting transfers between devices  141 us (13%)
  other arithmetic  114 us (11%)
  matrix products  53 us (5%)
  local copies, waits for them, and re-layouts  50.8 us (5%)
  between operations  15.7 us (1%)
    ppermute x35, waiting for transfers between devices, chip_send(): return lax.ppermute(array, 'fsdp', pairs)  354 us
    ppermute x35, starting transfers between devices, chip_send(): return lax.ppermute(array, 'fsdp', pairs)  118 us
    pallas_call x3, Pallas kernels, ffn_block_back(): pl.pallas_call(kernel, grid=(2 * tiles,), in_specs=[whole] * count + [par...  59.3 us
    pallas_call x6, Pallas kernels, outer_blocks(): pl.pallas_call(kernel, grid=(tiles,), in_specs=specs, out_specs=pl.BlockS...  55.2 us
    pallas_call x3, Pallas kernels, ffn_block(): pl.pallas_call(kernel, grid=(2 * tiles,), in_specs=[whole] * count + half...  53.3 us
    ppermute x18, waiting for transfers between devices, copy_swap(): lax.ppermute(array, 'rep', [(i, i ^ mask) for i in range(self.copies)])  40.6 us
    pallas_call x6, Pallas kernels, lane_outer(): pl.pallas_call(kernel, grid_spec=pltpu.PrefetchScalarGridSpec(num_scalar_...  29.4 us
    dot_general x7, matrix products, back_dot(): lax.dot_general(gradient, weight, (((1,), (1,)), ((), ())), preferred_ele...  26.7 us
  transfers between devices with their start and end apart: 72, of which 32 were waited for; matrix products, arithmetic and copies ran while one was open for 15% of the time, Pallas kernels for 25%

profile of v2, /device:TPU:0, one launch (start us, length us, event | category | flops | bytes accessed | tf_op | source)
XLA Modules:
  0.0 1060.6 jit_solution(7263680626490478243)
XLA Ops:
  25.1 19.0 %split_pair.1 = (bf16[1024,2048]{1,0:T(8,128)(2,1)}, bf16[1024,2048]{1,0:T(8,128)(2,1)}) custom-call(f32[1024,2,2048]{2,1,0:T(2,128)} %pair_ref.1), custom_call_target="tpu_custom_call" | custom-call | bytes 25165824 | tf_op jit(solution)/shard_map/split_pair/pallas_call | solution.py:611
  63.6 33.0 %collective-permute-done.3 = bf16[256,1152]{1,0:T(8,128)(2,1)} collective-permute-done((bf16[256,1152]{1,0:T(8,128)(2,1)S(1)}, bf16[256,1152]{1,0:T(8,128)(2,1)}, u32[]{:S(2)}, u32[]{:S(2)}) %collective-permute-start.3) | collective-permute-done | bytes 589856 | tf_op jit(solution)/shard_map/ppermute | solution.py:241
  120.5 23.4 %collective-permute-done.6 = bf16[256,1024]{1,0:T(8,128)(2,1)S(1)} collective-permute-done((bf16[256,1024]{1,0:T(8,128)(2,1)}, bf16[256,1024]{1,0:T(8,128)(2,1)S(1)}, u32[]{:S(2)}, u32[]{:S(2)}) %collective-permute-start.6) | collective-permute-done | bytes 524320 | tf_op jit(solution)/shard_map/ppermute | solution.py:241
  145.0 26.1 %collective-permute-start.7 = (bf16[256,1024]{1,0:T(8,128)(2,1)S(1)}, bf16[256,1024]{1,0:T(8,128)(2,1)S(1)}, u32[]{:S(2)}, u32[]{:S(2)}) collective-permute-start(bf16[256,1024]{1,0:T(8,128)(2,1)S(1)} %broadcast_select_fusion.6), channel_id=1, source_target_pairs={{0,2},{1,3},{2,0},{3,1},{4,6},{5,7},{6,4},{7,5},{8,10},{9,11},{10,... | collective-permute-start | bytes 1572872 | tf_op jit(solution)/shard_map/ppermute | solution.py:241
  171.0 11.4 %collective-permute-done.7 = bf16[256,1024]{1,0:T(8,128)(2,1)S(1)} collective-permute-done((bf16[256,1024]{1,0:T(8,128)(2,1)S(1)}, bf16[256,1024]{1,0:T(8,128)(2,1)S(1)}, u32[]{:S(2)}, u32[]{:S(2)}) %collective-permute-start.7) | collective-permute-done | bytes 524320 | tf_op jit(solution)/shard_map/ppermute | solution.py:241
  205.2 12.9 %attend.1 = (bf16[256,2048]{1,0:T(8,128)(2,1)}, bf16[256,2048]{1,0:T(8,128)(2,1)}) custom-call(s32[1]{0:T(128)} %bitcast.at_ref, f32[256,2048]{1,0:T(8,128)} %fusion.6.x_ref, f32[256,128]{1,0:T(8,128)} %get-tuple-element.477.c_ref, f32[256,128]{1,0:T(8,128)} %get-tuple-element.476.s_ref, f32[2,256]{1,0:T(2,128)} %reshape.446.g_ref, ...), custom_call_target="tpu_custom_call" | custom-call | flops 2684354560 | bytes 6815744 | tf_op jit(solution)/shard_map/attend/pallas_call | solution.py:104
  241.1 16.0 %ffn_block.3 = (f32[256,2048]{1,0:T(8,128)}, bf16[256,2048]{1,0:T(8,128)(2,1)}, bf16[256,2048]{1,0:T(8,128)(2,1)}, bf16[256,2048]{1,0:T(8,128)(2,1)}) custom-call(bf16[256,2048]{1,0:T(8,128)(2,1)} %multiply_convert_fusion.refs_0_.refs_3_, bf16[1024,2048]{1,0:T(8,128)(2,1)} %get-tuple-element.184.refs_1_.refs_2_.refs_3_.refs_4_, ...), custom_call_target="tpu_custom_call" | custom-call | flops 6442450944 | bytes 31457280 | tf_op jit(solution)/shard_map/ffn_block/pallas_call | solution.py:483
  257.1 19.9 %collective-permute-done.12.refs_0_.refs_4_ = bf16[256,2048]{1,0:T(8,128)(2,1)} collective-permute-done((bf16[256,2048]{1,0:T(8,128)(2,1)}, bf16[256,2048]{1,0:T(8,128)(2,1)}, u32[]{:S(2)}, u32[]{:S(2)}) %collective-permute-start.12) | collective-permute-done | bytes 1048608 | tf_op jit(solution)/shard_map/ppermute | solution.py:241
  285.2 21.5 %ffn_block.4 = (bf16[256,2048]{1,0:T(8,128)(2,1)}, bf16[256,2048]{1,0:T(8,128)(2,1)}, bf16[512,2048]{1,0:T(8,128)(2,1)}, bf16[512,2048]{1,0:T(8,128)(2,1)}, bf16[512,2048]{1,0:T(8,128)(2,1)}) custom-call(bf16[256,2048]{1,0:T(8,128)(2,1)} %collective-permute-done.12.refs_0_.refs_4_, bf16[256,2048]{1,0:T(8,128)(2,1)} %collective-permute-done.13.refs_1_.refs_5_, ...), custom_call_target="tpu_custom_call" | custom-call | flops 12884901888 | bytes 37748736 | tf_op jit(solution)/shard_map/ffn_block/pallas_call | solution.py:483
  306.7 11.1 %collective-permute-done.14 = bf16[256,2048]{1,0:T(8,128)(2,1)} collective-permute-done((bf16[256,2048]{1,0:T(8,128)(2,1)}, bf16[256,2048]{1,0:T(8,128)(2,1)}, u32[]{:S(2)}, u32[]{:S(2)}) %collective-permute-start.14) | collective-permute-done | bytes 1048608 | tf_op jit(solution)/shard_map/ppermute | solution.py:241
  323.5 15.8 %ffn_block.5 = (bf16[256,2048]{1,0:T(8,128)(2,1)}, bf16[256,2048]{1,0:T(8,128)(2,1)}, bf16[256,2048]{1,0:T(8,128)(2,1)}, bf16[256,2048]{1,0:T(8,128)(2,1)}) custom-call(bf16[256,2048]{1,0:T(8,128)(2,1)} %broadcast_select_fusion.3.refs_0_.refs_6_, bf16[1024,2048]{1,0:T(8,128)(2,1)} %get-tuple-element.184.refs_1_.refs_2_.refs_3_.refs_4_, ...), custom_call_target="tpu_custom_call" | custom-call | flops 6442450944 | bytes 31457280 | tf_op jit(solution)/shard_map/ffn_block/pallas_call | solution.py:483
  339.2 21.9 %collective-permute-done.16 = bf16[256,2048]{1,0:T(8,128)(2,1)} collective-permute-done((bf16[256,2048]{1,0:T(8,128)(2,1)}, bf16[256,2048]{1,0:T(8,128)(2,1)}, u32[]{:S(2)}, u32[]{:S(2)}) %collective-permute-start.16) | collective-permute-done | bytes 1048608 | tf_op jit(solution)/shard_map/ppermute | solution.py:241
  366.4 22.3 %collective-permute-done.17 = bf16[256,2048]{1,0:T(8,128)(2,1)} collective-permute-done((bf16[256,2048]{1,0:T(8,128)(2,1)}, bf16[256,2048]{1,0:T(8,128)(2,1)}, u32[]{:S(2)}, u32[]{:S(2)}) %collective-permute-start.17) | collective-permute-done | bytes 1048608 | tf_op jit(solution)/shard_map/ppermute | solution.py:241
  404.6 22.9 %collective-permute-start.19 = (bf16[256,2048]{1,0:T(8,128)(2,1)}, bf16[256,2048]{1,0:T(8,128)(2,1)}, u32[]{:S(2)}, u32[]{:S(2)}) collective-permute-start(bf16[256,2048]{1,0:T(8,128)(2,1)} %fusion.33.refs_0_.refs_3_), channel_id=1, source_target_pairs={{0,2},{1,3},{2,0},{3,1},{4,6},{5,7},{6,4},{7,5},{8,10},{9,11},{10,... | collective-permute-start | bytes 3145736 | tf_op jit(solution)/shard_map/ppermute | solution.py:241
  430.1 17.0 %ffn_block_back.3 = (f32[256,2048]{1,0:T(8,128)}, bf16[256,2048]{1,0:T(8,128)(2,1)}, bf16[256,2048]{1,0:T(8,128)(2,1)}) custom-call(bf16[256,2048]{1,0:T(8,128)(2,1)} %fusion.33.refs_0_.refs_3_, bf16[256,2048]{1,0:T(8,128)(2,1)} %get-tuple-element.211.refs_1_, bf16[256,2048]{1,0:T(8,128)(2,1)} %get-tuple-element.212.refs_2_, ...), custom_call_target="tpu_custom_call" | custom-call | flops 6442450944 | bytes 32505856 | tf_op jit(solution)/shard_map/ffn_block_back/pallas_call | solution.py:543
  447.1 24.3 %collective-permute-done.19.refs_0_.refs_4_ = bf16[256,2048]{1,0:T(8,128)(2,1)} collective-permute-done((bf16[256,2048]{1,0:T(8,128)(2,1)}, bf16[256,2048]{1,0:T(8,128)(2,1)}, u32[]{:S(2)}, u32[]{:S(2)}) %collective-permute-start.19) | collective-permute-done | bytes 1048608 | tf_op jit(solution)/shard_map/ppermute | solution.py:241
  478.5 25.6 %ffn_block_back.4 = (bf16[256,2048]{1,0:T(8,128)(2,1)}, bf16[256,2048]{1,0:T(8,128)(2,1)}, bf16[512,2048]{1,0:T(8,128)(2,1)}, bf16[512,2048]{1,0:T(8,128)(2,1)}) custom-call(bf16[256,2048]{1,0:T(8,128)(2,1)} %collective-permute-done.19.refs_0_.refs_4_, bf16[256,2048]{1,0:T(8,128)(2,1)} %collective-permute-done.20.refs_1_.refs_5_, ...), custom_call_target="tpu_custom_call" | custom-call | flops 12884901888 | bytes 39845888 | tf_op jit(solution)/shard_map/ffn_block_back/pallas_call | solution.py:543
  517.2 16.7 %ffn_block_back.5 = (bf16[256,2048]{1,0:T(8,128)(2,1)}, bf16[256,2048]{1,0:T(8,128)(2,1)}, bf16[256,2048]{1,0:T(8,128)(2,1)}) custom-call(bf16[256,2048]{1,0:T(8,128)(2,1)} %broadcast_select_fusion.2.refs_0_.refs_6_, bf16[256,2048]{1,0:T(8,128)(2,1)} %get-tuple-element.232.refs_1_, bf16[256,2048]{1,0:T(8,128)(2,1)} %get-tuple-element.233.refs_2_, ...), custom_call_target="tpu_custom_call" | custom-call | flops 6442450944 | bytes 32505856 | tf_op jit(solution)/shard_map/ffn_block_back/pallas_call | solution.py:543
  572.7 9.6 outer_blocks.9.refs_8_
  582.2 9.6 outer_blocks.10.refs_8_
  591.8 9.6 outer_blocks.11
  601.5 23.5 %collective-permute-done.24 = bf16[256,2048]{1,0:T(8,128)(2,1)} collective-permute-done((bf16[256,2048]{1,0:T(8,128)(2,1)}, bf16[256,2048]{1,0:T(8,128)(2,1)}, u32[]{:S(2)}, u32[]{:S(2)}) %collective-permute-start.24) | collective-permute-done | bytes 1048608 | tf_op jit(solution)/shard_map/ppermute | solution.py:241
  663.0 14.3 %collective-permute-start.32 = (bf16[256,2688]{1,0:T(8,128)(2,1)}, bf16[256,2688]{1,0:T(8,128)(2,1)S(1)}, u32[]{:S(2)}, u32[]{:S(2)}) collective-permute-start(bf16[256,2688]{1,0:T(8,128)(2,1)} %pad_maximum_fusion.2), channel_id=1, source_target_pairs={{0,2},{1,3},{6,4},{7,5},{8,10},{9,11},{14,12},{15,13},{16,18},{17,... | collective-permute-start | bytes 4128776 | tf_op jit(solution)/shard_map/ppermute | solution.py:241
  688.4 23.2 %attend_back.1 = (bf16[256,2048]{1,0:T(8,128)(2,1)}, f32[1280,512]{1,0:T(8,128)}, f32[1280,512]{1,0:T(8,128)}, f32[8,1,256]{2,1,0:T(1,128)}) custom-call(s32[1]{0:T(128)} %bitcast.at_ref, f32[256,2048]{1,0:T(8,128)} %fusion.6.x_ref, bf16[256,2048]{1,0:T(8,128)(2,1)} %get-tuple-element.272.q_ref, f32[256,128]{1,0:T(8,128)} %get-tuple-element.477.c_ref, ...), custom_call_target="tpu_custom_call" | custom-call | flops 6710886400 | bytes 13107200 | tf_op jit(solution)/shard_map/attend_back/pallas_call | solution.py:153
  711.6 24.9 %collective-permute-done.33 = bf16[256,2688]{1,0:T(8,128)(2,1)} collective-permute-done((bf16[256,2688]{1,0:T(8,128)(2,1)}, bf16[256,2688]{1,0:T(8,128)(2,1)}, u32[]{:S(2)}, u32[]{:S(2)}) %collective-permute-start.33) | collective-permute-done | bytes 1376288 | tf_op jit(solution)/shard_map/ppermute | solution.py:241
  784.2 27.1 %collective-permute-done.37 = bf16[256,1024]{1,0:T(8,128)(2,1)S(1)} collective-permute-done((bf16[256,1024]{1,0:T(8,128)(2,1)}, bf16[256,1024]{1,0:T(8,128)(2,1)S(1)}, u32[]{:S(2)}, u32[]{:S(2)}) %collective-permute-start.37) | collective-permute-done | bytes 524320 | tf_op jit(solution)/shard_map/ppermute | solution.py:241
  821.6 31.4 %collective-permute-done.38 = bf16[256,1024]{1,0:T(8,128)(2,1)S(1)} collective-permute-done((bf16[256,1024]{1,0:T(8,128)(2,1)S(1)}, bf16[256,1024]{1,0:T(8,128)(2,1)S(1)}, u32[]{:S(2)}, u32[]{:S(2)}) %collective-permute-start.38) | collective-permute-done | bytes 524320 | tf_op jit(solution)/shard_map/ppermute | solution.py:241
  883.0 16.7 %collective-permute-done.41 = bf16[256,2048]{1,0:T(8,128)(2,1)} collective-permute-done((bf16[256,2048]{1,0:T(8,128)(2,1)}, bf16[256,2048]{1,0:T(8,128)(2,1)}, u32[]{:S(2)}, u32[]{:S(2)}) %collective-permute-start.41) | collective-permute-done | bytes 1048608 | tf_op jit(solution)/shard_map/ppermute | solution.py:241
  920.2 11.3 %join_pair.1 = f32[1024,2,2048]{2,1,0:T(2,128)} custom-call(bf16[3072,2048]{1,0:T(8,128)(2,1)} %all-gather.8.cloned.1.call-done.first_ref.second_ref, bf16[3072,2048]{1,0:T(8,128)(2,1)} %all-gather.8.cloned.1.call-done.first_ref.second_ref), custom_call_target="tpu_custom_call" | custom-call | bytes 25165824 | tf_op jit(solution)/shard_map/join_pair/pallas_call | solution.py:633
  939.1 14.2 %collective-permute-done.45 = bf16[256,2048]{1,0:T(8,128)(2,1)} collective-permute-done((bf16[256,2048]{1,0:T(8,128)(2,1)}, bf16[256,2048]{1,0:T(8,128)(2,1)}, u32[]{:S(2)}, u32[]{:S(2)}) %collective-permute-start.45) | collective-permute-done | bytes 1048608 | tf_op jit(solution)/shard_map/ppermute | solution.py:241
  954.4 10.4 collective-permute-done.47
  987.2 13.6 %collective-permute-done.49 = bf16[256,1152]{1,0:T(8,128)(2,1)S(1)} collective-permute-done((bf16[256,1152]{1,0:T(8,128)(2,1)S(1)}, bf16[256,1152]{1,0:T(8,128)(2,1)S(1)}, u32[]{:S(2)}, u32[]{:S(2)}) %collective-permute-start.49) | collective-permute-done | bytes 589856 | tf_op jit(solution)/shard_map/ppermute | solution.py:241
  (521 shorter events, 444.9 us)
Async XLA Ops:
  7.2 176.4 %all-gather.4.cloned.1.call-start = ((), (), s32[]{:S(2)}) async-start(), calls=%async_computation.1 | async-start | bytes 17842176 | tf_op jit(solution)/shard_map/all_gather | solution.py:686
  18.4 343.3 %all-gather.6.cloned.1.call-start = ((), (), s32[]{:S(2)}) async-start(), calls=%async_computation.2 | async-start | bytes 2162688 | tf_op jit(solution)/shard_map/all_gather | solution.py:686
  18.7 39.1 %collective-permute-start = (bf16[256,1152]{1,0:T(8,128)(2,1)S(1)}, bf16[256,1152]{1,0:T(8,128)(2,1)S(1)}, u32[]{:S(2)}, u32[]{:S(2)}) collective-permute-start(bf16[256,1152]{1,0:T(8,128)(2,1)S(1)} %pad_maximum_fusion.10.shard_ref), channel_id=1, source_target_pairs={{0,2},{1,3},{2,0},{3,1},{4,6},{5,7},{6,4},{7,5},{8,10},{9,11},{10,... | collective-permute-start | bytes 1769480 | tf_op jit(solution)/shard_map/ppermute | solution.py:241
  21.8 40.4 %collective-permute-start.1 = (bf16[256,1152]{1,0:T(8,128)(2,1)S(1)}, bf16[256,1152]{1,0:T(8,128)(2,1)S(1)}, u32[]{:S(2)}, u32[]{:S(2)}) collective-permute-start(bf16[256,1152]{1,0:T(8,128)(2,1)S(1)} %pad_maximum_fusion.10.shard_ref), channel_id=1, source_target_pairs={{0,4},{1,5},{2,6},{3,7},{4,0},{5,1},{6,2},{7,3},{8,12},{9,13},{10,... | collective-permute-start | bytes 1769480 | tf_op jit(solution)/shard_map/ppermute | solution.py:241
  24.4 39.2 %collective-permute-start.4 = (bf16[256,1152]{1,0:T(8,128)(2,1)S(1)}, bf16[256,1152]{1,0:T(8,128)(2,1)S(1)}, u32[]{:S(2)}, u32[]{:S(2)}) collective-permute-start(bf16[256,1152]{1,0:T(8,128)(2,1)S(1)} %pad_maximum_fusion.10.shard_ref), channel_id=1, source_target_pairs={{2,4},{3,5},{4,2},{5,3},{10,12},{11,13},{12,10},{13,11},{18,20},{1... | collective-permute-start | bytes 1769480 | tf_op jit(solution)/shard_map/ppermute | solution.py:241
  101.7 93.2 %collective-permute-start.10 = (bf16[1024,2048]{1,0:T(8,128)(2,1)}, bf16[1024,2048]{1,0:T(8,128)(2,1)}, u32[]{:S(2)}, u32[]{:S(2)}) collective-permute-start(bf16[1024,2048]{1,0:T(8,128)(2,1)} %convert_element_type.450.refs_5_.refs_6_.refs_7_.refs_8_), channel_id=1, source_target_pairs={{0,1},{1,0},{2,3},{3,2},{4,5},{5,4},{6,7},{7,6},{8,9},{9,8},{10,11... | collective-permute-start | bytes 12582920 | tf_op jit(solution)/shard_map/ppermute | solution.py:234
  102.1 92.9 %collective-permute-start.8 = (bf16[1024,2048]{1,0:T(8,128)(2,1)}, bf16[1024,2048]{1,0:T(8,128)(2,1)}, u32[]{:S(2)}, u32[]{:S(2)}) collective-permute-start(bf16[1024,2048]{1,0:T(8,128)(2,1)} %get-tuple-element.184.refs_1_.refs_2_.refs_3_.refs_4_), channel_id=1, source_target_pairs={{0,1},{1,0},{2,3},{3,2},{4,5},{5,4},{6,7},{7,6},{8,9},{9,8},{10,11... | collective-permute-start | bytes 12582920 | tf_op jit(solution)/shard_map/ppermute | solution.py:234
  102.3 92.7 %collective-permute-start.9 = (bf16[1024,2048]{1,0:T(8,128)(2,1)}, bf16[1024,2048]{1,0:T(8,128)(2,1)}, u32[]{:S(2)}, u32[]{:S(2)}) collective-permute-start(bf16[1024,2048]{1,0:T(8,128)(2,1)} %get-tuple-element.186.refs_3_.refs_4_.refs_5_.refs_6_), channel_id=1, source_target_pairs={{0,1},{1,0},{2,3},{3,2},{4,5},{5,4},{6,7},{7,6},{8,9},{9,8},{10,11... | collective-permute-start | bytes 12582920 | tf_op jit(solution)/shard_map/ppermute | solution.py:234
  228.3 48.7 %collective-permute-start.12 = (bf16[256,2048]{1,0:T(8,128)(2,1)}, bf16[256,2048]{1,0:T(8,128)(2,1)}, u32[]{:S(2)}, u32[]{:S(2)}) collective-permute-start(bf16[256,2048]{1,0:T(8,128)(2,1)} %multiply_convert_fusion.refs_0_.refs_3_), channel_id=1, source_target_pairs={{0,2},{1,3},{2,0},{3,1},{4,6},{5,7},{6,4},{7,5},{8,10},{9,11},{10,... | collective-permute-start | bytes 3145736 | tf_op jit(solution)/shard_map/ppermute | solution.py:241
  230.1 53.9 %collective-permute-start.13 = (bf16[256,2048]{1,0:T(8,128)(2,1)}, bf16[256,2048]{1,0:T(8,128)(2,1)}, u32[]{:S(2)}, u32[]{:S(2)}) collective-permute-start(bf16[256,2048]{1,0:T(8,128)(2,1)} %multiply_convert_fusion.refs_0_.refs_3_), channel_id=1, source_target_pairs={{0,4},{1,5},{2,6},{3,7},{4,0},{5,1},{6,2},{7,3},{8,12},{9,13},{10,... | collective-permute-start | bytes 3145736 | tf_op jit(solution)/shard_map/ppermute | solution.py:241
  239.0 518.3 %reduce-scatter.2.cloned.1.call-start = ((), (), s32[]{:S(2)}) async-start(), calls=%async_computation.3 | async-start | bytes 15728640 | tf_op jit(solution)/shard_map/reduce_scatter | solution.py:885
  239.0 67.7 %collective-permute-start.15 = (bf16[256,2048]{1,0:T(8,128)(2,1)}, bf16[256,2048]{1,0:T(8,128)(2,1)}, u32[]{:S(2)}, u32[]{:S(2)}) collective-permute-start(bf16[256,2048]{1,0:T(8,128)(2,1)} %multiply_convert_fusion.refs_0_.refs_3_), channel_id=1, source_target_pairs={{2,4},{3,5},{4,2},{5,3},{10,12},{11,13},{12,10},{13,11},{18,20},{1... | collective-permute-start | bytes 3145736 | tf_op jit(solution)/shard_map/ppermute | solution.py:241
  320.2 40.9 %collective-permute-start.16 = (bf16[256,2048]{1,0:T(8,128)(2,1)}, bf16[256,2048]{1,0:T(8,128)(2,1)}, u32[]{:S(2)}, u32[]{:S(2)}) collective-permute-start(bf16[256,2048]{1,0:T(8,128)(2,1)} %get-tuple-element.202), channel_id=1, source_target_pairs={{0,2},{1,3},{2,0},{3,1},{4,6},{5,7},{6,4},{7,5},{8,10},{9,11},{10,... | collective-permute-start | bytes 3145736 | tf_op jit(solution)/shard_map/ppermute | solution.py:241
  320.2 68.5 %collective-permute-start.17 = (bf16[256,2048]{1,0:T(8,128)(2,1)}, bf16[256,2048]{1,0:T(8,128)(2,1)}, u32[]{:S(2)}, u32[]{:S(2)}) collective-permute-start(bf16[256,2048]{1,0:T(8,128)(2,1)} %get-tuple-element.209), channel_id=1, source_target_pairs={{0,4},{1,5},{2,6},{3,7},{4,0},{5,1},{6,2},{7,3},{8,12},{9,13},{10,... | collective-permute-start | bytes 3145736 | tf_op jit(solution)/shard_map/ppermute | solution.py:241
  404.6 66.8 %collective-permute-start.19 = (bf16[256,2048]{1,0:T(8,128)(2,1)}, bf16[256,2048]{1,0:T(8,128)(2,1)}, u32[]{:S(2)}, u32[]{:S(2)}) collective-permute-start(bf16[256,2048]{1,0:T(8,128)(2,1)} %fusion.33.refs_0_.refs_3_), channel_id=1, source_target_pairs={{0,2},{1,3},{2,0},{3,1},{4,6},{5,7},{6,4},{7,5},{8,10},{9,11},{10,... | collective-permute-start | bytes 3145736 | tf_op jit(solution)/shard_map/ppermute | solution.py:241
  427.5 49.8 %collective-permute-start.20 = (bf16[256,2048]{1,0:T(8,128)(2,1)}, bf16[256,2048]{1,0:T(8,128)(2,1)}, u32[]{:S(2)}, u32[]{:S(2)}) collective-permute-start(bf16[256,2048]{1,0:T(8,128)(2,1)} %fusion.33.refs_0_.refs_3_), channel_id=1, source_target_pairs={{0,4},{1,5},{2,6},{3,7},{4,0},{5,1},{6,2},{7,3},{8,12},{9,13},{10,... | collective-permute-start | bytes 3145736 | tf_op jit(solution)/shard_map/ppermute | solution.py:241
  428.4 75.7 %collective-permute-start.22 = (bf16[256,2048]{1,0:T(8,128)(2,1)}, bf16[256,2048]{1,0:T(8,128)(2,1)}, u32[]{:S(2)}, u32[]{:S(2)}) collective-permute-start(bf16[256,2048]{1,0:T(8,128)(2,1)} %fusion.33.refs_0_.refs_3_), channel_id=1, source_target_pairs={{2,4},{3,5},{4,2},{5,3},{10,12},{11,13},{12,10},{13,11},{18,20},{1... | collective-permute-start | bytes 3145736 | tf_op jit(solution)/shard_map/ppermute | solution.py:241
  565.8 59.2 %collective-permute-start.24 = (bf16[256,2048]{1,0:T(8,128)(2,1)}, bf16[256,2048]{1,0:T(8,128)(2,1)}, u32[]{:S(2)}, u32[]{:S(2)}) collective-permute-start(bf16[256,2048]{1,0:T(8,128)(2,1)} %get-tuple-element.240), channel_id=1, source_target_pairs={{0,4},{1,5},{2,6},{3,7},{4,0},{5,1},{6,2},{7,3},{8,12},{9,13},{10,... | collective-permute-start | bytes 3145736 | tf_op jit(solution)/shard_map/ppermute | solution.py:241
  565.8 59.2 %collective-permute-start.25 = (bf16[128,2048]{1,0:T(8,128)(2,1)}, bf16[128,2048]{1,0:T(8,128)(2,1)}, u32[]{:S(2)}, u32[]{:S(2)}) collective-permute-start(bf16[128,2048]{1,0:T(8,128)(2,1)} %get-tuple-element.452), channel_id=1, source_target_pairs={{0,6},{1,7},{2,4},{3,5},{4,2},{5,3},{6,0},{7,1},{8,14},{9,15},{10,... | collective-permute-start | bytes 1572872 | tf_op jit(solution)/shard_map/ppermute | solution.py:241
  625.0 284.0 %all-gather.8.cloned.1.call-start = ((), (), s32[]{:S(2)}) async-start(), calls=%async_computation.4 | async-start | bytes 15728640 | tf_op jit(solution)/shard_map/all_gather | solution.py:942
  663.0 73.5 %collective-permute-start.32 = (bf16[256,2688]{1,0:T(8,128)(2,1)}, bf16[256,2688]{1,0:T(8,128)(2,1)S(1)}, u32[]{:S(2)}, u32[]{:S(2)}) collective-permute-start(bf16[256,2688]{1,0:T(8,128)(2,1)} %pad_maximum_fusion.2), channel_id=1, source_target_pairs={{0,2},{1,3},{6,4},{7,5},{8,10},{9,11},{14,12},{15,13},{16,18},{17,... | collective-permute-start | bytes 4128776 | tf_op jit(solution)/shard_map/ppermute | solution.py:241
  677.3 59.2 %collective-permute-start.34 = (bf16[256,2688]{1,0:T(8,128)(2,1)}, bf16[256,2688]{1,0:T(8,128)(2,1)}, u32[]{:S(2)}, u32[]{:S(2)}) collective-permute-start(bf16[256,2688]{1,0:T(8,128)(2,1)} %pad_maximum_fusion.2), channel_id=1, source_target_pairs={{2,4},{3,5},{4,2},{5,3},{10,12},{11,13},{12,10},{13,11},{18,20},{1... | collective-permute-start | bytes 4128776 | tf_op jit(solution)/shard_map/ppermute | solution.py:241
  680.6 55.9 %collective-permute-start.33 = (bf16[256,2688]{1,0:T(8,128)(2,1)}, bf16[256,2688]{1,0:T(8,128)(2,1)}, u32[]{:S(2)}, u32[]{:S(2)}) collective-permute-start(bf16[256,2688]{1,0:T(8,128)(2,1)} %pad_maximum_fusion.3), channel_id=1, source_target_pairs={{0,2},{1,3},{2,0},{3,1},{4,6},{5,7},{6,4},{7,5},{8,10},{9,11},{10,... | collective-permute-start | bytes 4128776 | tf_op jit(solution)/shard_map/ppermute | solution.py:241
  757.3 55.5 %collective-permute-start.39 = (bf16[1024,2048]{1,0:T(8,128)(2,1)}, bf16[1024,2048]{1,0:T(8,128)(2,1)}, u32[]{:S(2)}, u32[]{:S(2)}) collective-permute-start(bf16[1024,2048]{1,0:T(8,128)(2,1)} %lane_outer.8), channel_id=1, source_target_pairs={{0,1},{1,0},{2,3},{3,2},{4,5},{5,4},{6,7},{7,6},{8,9},{9,8},{10,11... | collective-permute-start | bytes 12582920 | tf_op jit(solution)/shard_map/ppermute | solution.py:234
  767.2 115.8 %collective-permute-start.35 = (bf16[256,2688]{1,0:T(8,128)(2,1)}, bf16[256,2688]{1,0:T(8,128)(2,1)}, u32[]{:S(2)}, u32[]{:S(2)}) collective-permute-start(bf16[256,2688]{1,0:T(8,128)(2,1)} %fusion.12), channel_id=1, source_target_pairs={{0,4},{1,5},{2,6},{3,7},{4,0},{5,1},{6,2},{7,3},{8,12},{9,13},{10,... | collective-permute-start | bytes 4128776 | tf_op jit(solution)/shard_map/ppermute | solution.py:241
  811.5 41.4 %collective-permute-start.38 = (bf16[256,1024]{1,0:T(8,128)(2,1)S(1)}, bf16[256,1024]{1,0:T(8,128)(2,1)S(1)}, u32[]{:S(2)}, u32[]{:S(2)}) collective-permute-start(bf16[256,1024]{1,0:T(8,128)(2,1)S(1)} %convert_element_type.519), channel_id=1, source_target_pairs={{4,0},{5,1},{6,2},{7,3},{12,8},{13,9},{14,10},{15,11},{20,16},{21,... | collective-permute-start | bytes 1572872 | tf_op jit(solution)/shard_map/ppermute | solution.py:241
  855.2 44.5 %collective-permute-start.42 = (bf16[256,2048]{1,0:T(8,128)(2,1)}, bf16[256,2048]{1,0:T(8,128)(2,1)}, u32[]{:S(2)}, u32[]{:S(2)}) collective-permute-start(bf16[256,2048]{1,0:T(8,128)(2,1)} %get-tuple-element.289), channel_id=1, source_target_pairs={{2,4},{3,5},{4,2},{5,3},{10,12},{11,13},{12,10},{13,11},{18,20},{1... | collective-permute-start | bytes 3145736 | tf_op jit(solution)/shard_map/ppermute | solution.py:241
  903.6 49.8 %collective-permute-start.45 = (bf16[256,2048]{1,0:T(8,128)(2,1)}, bf16[256,2048]{1,0:T(8,128)(2,1)}, u32[]{:S(2)}, u32[]{:S(2)}) collective-permute-start(bf16[256,2048]{1,0:T(8,128)(2,1)} %add_convert_fusion.1), channel_id=1, source_target_pairs={{0,4},{1,5},{2,6},{3,7},{4,0},{5,1},{6,2},{7,3},{8,12},{9,13},{10,... | collective-permute-start | bytes 3145736 | tf_op jit(solution)/shard_map/ppermute | solution.py:241
  914.4 51.5 %collective-permute-start.46 = (bf16[256,1152]{1,0:T(8,128)(2,1)S(1)}, bf16[256,1152]{1,0:T(8,128)(2,1)}, u32[]{:S(2)}, u32[]{:S(2)}) collective-permute-start(bf16[256,1152]{1,0:T(8,128)(2,1)S(1)} %pad_maximum_fusion.11), channel_id=1, source_target_pairs={{0,2},{1,3},{6,4},{7,5},{8,10},{9,11},{14,12},{15,13},{16,18},{17,... | collective-permute-start | bytes 1769480 | tf_op jit(solution)/shard_map/ppermute | solution.py:241
  917.3 48.6 %collective-permute-start.48 = (bf16[256,1152]{1,0:T(8,128)(2,1)S(1)}, bf16[256,1152]{1,0:T(8,128)(2,1)S(1)}, u32[]{:S(2)}, u32[]{:S(2)}) collective-permute-start(bf16[256,1152]{1,0:T(8,128)(2,1)S(1)} %pad_maximum_fusion.11), channel_id=1, source_target_pairs={{2,4},{3,5},{4,2},{5,3},{10,12},{11,13},{12,10},{13,11},{18,20},{1... | collective-permute-start | bytes 1769480 | tf_op jit(solution)/shard_map/ppermute | solution.py:241
  919.2 53.1 %collective-permute-start.53 = (bf16[64,2688]{1,0:T(8,128)(2,1)}, bf16[64,2688]{1,0:T(8,128)(2,1)}, u32[]{:S(2)}, u32[]{:S(2)}) collective-permute-start(bf16[64,2688]{1,0:T(8,128)(2,1)} %get-tuple-element.441), channel_id=1, source_target_pairs={{0,8},{8,0},{16,24},{24,16},{1,9},{9,1},{17,25},{25,17},{2,10},{10... | collective-permute-start | bytes 1032200 | tf_op jit(solution)/shard_map/ppermute | solution.py:237
  1000.7 39.5 %collective-permute-start.62 = (bf16[64,2688]{1,0:T(8,128)(2,1)S(1)}, bf16[64,2688]{1,0:T(8,128)(2,1)S(1)}, u32[]{:S(2)}, u32[]{:S(2)}) collective-permute-start(bf16[64,2688]{1,0:T(8,128)(2,1)S(1)} %add_convert_fusion.7), channel_id=1, source_target_pairs={{0,8},{8,0},{16,24},{24,16},{1,9},{9,1},{17,25},{25,17},{2,10},{10... | collective-permute-start | bytes 1032200 | tf_op jit(solution)/shard_map/ppermute | solution.py:237
  (132 other events, 2524.0 us)
Sparse Core Ops, SparseCore 0:
  18.6 144.2 all-gather.3
  239.1 80.3 all-gather.5
  625.1 132.1 reduce-scatter.1
  759.0 122.4 all-gather.7

commit v3 on v2

--- a/solution.py
+++ b/solution.py
@@ -116,16 +116,18 @@
     )(device.reshape(1), projected, cosine, sine, gains, kv_seen, kv_seen)
 
 
-def attend_back(projected, queries, cosine, sine, gains, kv_seen, gradient, device):
+def attend_back(projected, queries, cosine, sine, gains, kv_seen, gradient, weights, device):
     rows, key_count = projected.shape[0], kv_seen.shape[0]
     groups = H // KVH
+    width = gradient.shape[1]
     head, half, gain, keys, values = head_specs(rows, key_count)
 
     def kernel(
-        at_ref, x_ref, q_ref, c_ref, s_ref, g_ref, k_ref, v_ref, do_ref,
+        at_ref, x_ref, q_ref, c_ref, s_ref, g_ref, k_ref, v_ref, do_ref, w_ref,
         dx_ref, dk_ref, dv_ref, dg_ref,
     ):
-        queries, grad = q_ref[...], do_ref[...]
+        queries = q_ref[...]
+        grad = back_dot(do_ref[...], w_ref[...]).astype(BF)
         shares = head_shares(queries, k_ref[...], at_ref[0])
         grad_shares = back_dot(grad, v_ref[...])
         inner = jnp.sum(shares * grad_shares, axis=-1, keepdims=True)
@@ -154,7 +156,9 @@
         kernel,
         grid=(H,),
         in_specs=[
-            pl.BlockSpec(memory_space=pltpu.SMEM), head, head, half, half, gain, keys, values, head,
+            pl.BlockSpec(memory_space=pltpu.SMEM), head, head, half, half, gain, keys, values,
+            pl.BlockSpec((rows, width), lambda h: (0, 0)),
+            pl.BlockSpec((HD, width), lambda h: (h, H * HD // width)),
         ],
         out_specs=[head, shared, shared, pl.BlockSpec((1, 1, HD), lambda h: (h, 0, 0))],
         out_shape=[
@@ -170,7 +174,7 @@
         ),
         name="attend_back",
     )(
-        device.reshape(1), projected, queries, cosine, sine, gains, kv_seen, kv_seen, gradient,
+        device.reshape(1), projected, queries, cosine, sine, gains, kv_seen, kv_seen, gradient, weights,
     )
 
 
@@ -270,20 +274,27 @@
             return [
                 self.chip_swap(parts[mask].astype(BF), mask) for mask in range(1, self.chips)
             ]
-        last = parts[3].astype(BF)
+        return self.collect_ends(parts) + self.collect_beside(parts)
+
+    def collect_ends(self, parts):
+        return [self.chip_send(parts[3].astype(BF), [(0, 1), (3, 2)])] if self.four else []
+
+    def collect_beside(self, parts):
+        if not self.four:
+            return self.collect_near(parts)
         return [
-            self.chip_send(last, [(0, 1), (3, 2)]),
             self.chip_swap(parts[1].astype(BF), 1),
-            self.chip_send(last, [(1, 2), (2, 1)]),
+            self.chip_send(parts[3].astype(BF), [(1, 2), (2, 1)]),
         ]
 
     def collect_far(self, parts, near):
         if not self.four:
             return near
-        return near[1:] + [self.chip_swap((parts[2] + near[0].astype(F32)).astype(BF), 2)]
+        passed = parts[2].astype(F32) + near[0].astype(F32)
+        return near[1:] + [self.chip_swap(passed.astype(BF), 2)]
 
     def collect_sum(self, own, arrived):
-        total = own
+        total = own.astype(F32)
         for array in arrived:
             total = total + array.astype(F32)
         return total
@@ -360,32 +371,15 @@
             for core in (self.core, 1 - self.core)
         ]
 
-    def lane_outer(self, left, right, core):
-        rows = left.shape[1] // self.count
-        height, width = right.shape
-
-        def kernel(at_ref, left_ref, right_ref, out_ref):
-            out_ref[...] = outer_sum(left_ref[...], right_ref[...]).astype(BF)
-
-        return pl.pallas_call(
-            kernel,
-            grid_spec=pltpu.PrefetchScalarGridSpec(
-                num_scalar_prefetch=1,
-                grid=(self.chips,),
-                in_specs=[
-                    pl.BlockSpec((height, rows), lambda i, at: (0, 2 * i + at[0])),
-                    pl.BlockSpec((height, width), lambda i, at: (0, 0)),
-                ],
-                out_specs=pl.BlockSpec((rows, width), lambda i, at: (i, 0)),
-            ),
-            out_shape=jax.ShapeDtypeStruct((self.chips * rows, width), BF),
-            cost_estimate=pl.CostEstimate(
-                flops=2 * height * self.chips * rows * width,
-                bytes_accessed=2 * (height + self.chips * rows) * width,
-                transcendentals=0,
-            ),
-            name="lane_outer",
-        )(core.reshape(1), left, right)
+    def lane_columns(self, whole, core):
+        columns = whole.shape[1] // self.count
+        return jnp.concatenate(
+            [
+                lax.dynamic_slice_in_dim(whole, (2 * chip + core) * columns, columns, 1)
+                for chip in range(self.chips)
+            ],
+            axis=1,
+        )
 
     def lane_parts(self, mine, arrived):
         rows = arrived[0].shape[0] // self.chips
@@ -396,7 +390,7 @@
                 + lax.dynamic_slice_in_dim(other, chip * rows, rows, 0).astype(F32)
                 for own, other in zip(mine, arrived)
             ]
-            return jnp.concatenate(sums, axis=-1)
+            return jnp.concatenate(sums, axis=-1).astype(BF)
 
         return [part(self.owner(j)) for j in range(self.chips)]
 
@@ -634,8 +628,8 @@
         kernel,
         grid=(tiles,),
         in_specs=[
+            pl.BlockSpec((rows, width), lambda i: (i, 0)),
             pl.BlockSpec((rows, width), lambda i: (i + tiles, 0)),
-            pl.BlockSpec((rows, width), lambda i: (i + 2 * tiles, 0)),
         ],
         out_specs=pl.BlockSpec((rows, 2, width), lambda i: (i, 0, 0)),
         out_shape=jax.ShapeDtypeStruct((units, 2, width), F32),
@@ -786,10 +780,10 @@
     piece = rows_dev // CHUNKS
     units = w_down.shape[0]
 
-    def staged(rows, work):
+    def staged(rows, work, extra=()):
         near = at.spread_near(rows)
         first = work(0, [rows], F32)
-        near, first = tie(near, first)
+        near, first, extra = tie(near, first, extra)
         far = at.spread_far(rows, near)
         pairs = [near[i : i + 2] for i in range(0, len(near), 2)]
         second = [work(j + 1, blocks, BF) for j, blocks in enumerate(pairs)]
@@ -804,17 +798,17 @@
             back[0] = first_back
             done.append(third)
             last = third[0][0]
-        return first[0][0], back, last, [kept for _, kept in done]
-
-    def ffn_forward(rows):
+        return first[0][0], back, last, [kept for _, kept in done], extra
+
+    def ffn_forward(rows, extra):
         def work(j, blocks, sum_type):
             sums, *kept = ffn_block(blocks, gate_halves, up_halves, down_halves, sum_type)
             return sums, (blocks, *kept)
 
-        own, back, last, kept = staged(rows, work)
+        own, back, last, kept, extra = staged(rows, work, extra)
         if last is not None:
             back = back + [at.chip_swap(last, at.chips - 1)]
-        return at.collect_sum(own, back), kept
+        return at.collect_sum(own, back), kept, extra
 
     def ffn_backward(rows, kept):
         def work(j, grads, sum_type):
@@ -836,7 +830,15 @@
         return after_ffn + rms_norm(pli_out) * gain_rows[5]
 
     cuts = [slice(i * piece, (i + 1) * piece) for i in range(CHUNKS)]
-    forwards = [ffn_forward(ffn_in[cut].astype(BF)) for cut in cuts]
+    core, other_core = at.core, 1 - at.core
+    lanes = [
+        at.lane_columns(rows, side) for rows in (attended_bf, normed_bf) for side in (core, other_core)
+    ]
+    forwards = []
+    for cut in cuts:
+        ffn_out, kept, lanes = ffn_forward(ffn_in[cut].astype(BF), lanes)
+        forwards.append((ffn_out, kept))
+    attended_mine, attended_other, normed_mine, normed_other = lanes
     gain_total = 0.0
     results, extras, streams, ins, all_grads = [], [], [], [], []
     pli_rows = []
@@ -852,7 +854,7 @@
         grad_pli_pre_bf = grad_pli_pre.astype(BF)
         grad_after = grad_after + back_dot(grad_pli_pre_bf, pgate_all)
         grad_stream, grad_ffn_out, gain_tail = tail_pull(grad_after)
-        own, back, last, grads = ffn_backward(grad_ffn_out.astype(BF), kept)
+        own, back, last, grads, _ = ffn_backward(grad_ffn_out.astype(BF), kept)
         gain_total = gain_total + gain_final + gain_tail
         results.append(result.astype(BF))
         extras.append(grad_extra)
@@ -864,37 +866,30 @@
     kept = [[group[i] for grads in all_grads for group in grads] for i in range(5)]
     hiddens, gates, ups = kept[1], kept[3], kept[4]
     ins_blocks, outs_grad = [[block for blocks in kept[i] for block in blocks] for i in (0, 2)]
+    lasts = [last for _, _, last in ins if last is not None]
+    lasts, pli_rows, hiddens, gates, ups = tie(lasts, pli_rows, hiddens, gates, ups)
     pairs = [(hiddens, outs_grad), (gates, ins_blocks), (ups, ins_blocks)]
     theirs = [
         outer_blocks(lefts, rights, units, units) for lefts, rights in pairs
     ]
     mids, pli_outs, afters, pres = [jnp.concatenate(rows, axis=0) for rows in zip(*pli_rows)]
-    grad_pproj = outer_sum(mids, pli_outs).astype(BF).reshape(-1, pd)
-    grad_pgate = outer_sum(afters, pres).astype(BF)
-    half_rows = piece // 2
-    lasts = [last for _, _, last in ins if last is not None]
-    upper = [at.chip_swap(last[:half_rows], at.chips - 1) for last in lasts]
-    upper, theirs, grad_pproj, grad_pgate = tie(upper, theirs, grad_pproj, grad_pgate)
-    under = [at.chip_swap(last[half_rows:], at.chips - 1) for last in lasts]
-    wide_w = None
-    for place, ((lefts, rights), their) in enumerate(zip(pairs, theirs)):
-        wide_w = outer_blocks(
-            lefts, rights, 0, units, at.core_swap(their), wide_w, place, 3
-        )
-    backs, under, wide_w = tie([back for _, back, _ in ins], under, wide_w)
-    wide_part = lax.psum_scatter(wide_w, "rep", scatter_dimension=0, tiled=True)
-    ends = [[jnp.concatenate(pair, axis=0)] for pair in zip(upper, under)] or [[]] * len(ins)
-    ins = [
-        at.collect_sum(own, back + end) for (own, _, _), back, end in zip(ins, backs, ends)
-    ]
+    grad_pproj = outer_blocks([mids], [pli_outs], 0, pd)
+    grad_pgate = outer_blocks([afters], [pres], 0, width)
+    lasts = [at.chip_swap(last, at.chips - 1) for last in lasts]
+    backs = [back for _, back, _ in ins]
+    backs, lasts, theirs, grad_pproj, grad_pgate = tie(
+        backs, lasts, theirs, grad_pproj, grad_pgate
+    )
+    grad_pproj = grad_pproj.reshape(-1, pd)
+    ends = [[last] for last in lasts] or [[]] * len(ins)
+    ins = [at.collect_sum(own, back + end) for (own, _, _), back, end in zip(ins, backs, ends)]
 
     grad_inputs, grad_normed, grad_attn_proj, grad_laurel_out, gain_middle = middle_pull(
         (jnp.concatenate(streams, axis=0), jnp.concatenate(ins, axis=0))
     )
     grad_attn_bf = grad_attn_proj.astype(BF)
-    core, other_core = at.core, 1 - at.core
-    out_leaving = at.core_swap(at.lane_outer(attended_bf, grad_attn_bf, other_core))
-    out_mine = at.lane_outer(attended_bf, grad_attn_bf, core)
+    out_leaving = at.core_swap(outer_sum(attended_other, grad_attn_bf).astype(BF))
+    out_mine = outer_sum(attended_mine, grad_attn_bf).astype(BF)
     grad_laurel_bf = grad_laurel_out.astype(BF)
     grad_right_w = outer_sum(laurel_mid, grad_laurel_bf).astype(BF).reshape(-1, lr)
     grad_mid_bf = back_dot(grad_laurel_bf, right_all).astype(BF)
@@ -903,16 +898,26 @@
         jnp.concatenate([grad_left_w, grad_right_w, grad_pgate, grad_pproj], axis=1)
     )
     small_leaving = at.core_swap(small_leaving)
-    out_leaving, small_leaving, out_mine, small_mine, grad_attn_bf = tie(
-        out_leaving, small_leaving, out_mine, small_mine, grad_attn_bf
-    )
-    grad_attended = back_dot(grad_attn_bf, out_all).astype(BF)
+    their_down = at.core_swap(theirs[0])
+    out_leaving, small_leaving, out_mine, small_mine, theirs, their_down, grad_attn_bf = tie(
+        out_leaving, small_leaving, out_mine, small_mine, theirs, their_down, grad_attn_bf
+    )
     out_parts = at.lane_parts([out_mine, small_mine], [out_leaving, small_leaving])
-    out_near = at.collect_near(out_parts)
+    out_ends = at.collect_ends(out_parts)
+    theirs = [at.core_swap(their) for their in theirs[1:]]
     grad_q_bf, key_grad, value_grad, q_gain_rows = attend_back(
-        q_proj, queries_bf, cosine, sine, qk_gain, kv_seen, grad_attended, device
-    )
-    out_near, grad_q_bf, key_grad, value_grad = tie(out_near, grad_q_bf, key_grad, value_grad)
+        q_proj, queries_bf, cosine, sine, qk_gain, kv_seen, grad_attn_bf, main_all, device
+    )
+    down_w = outer_blocks(*pairs[0], 0, units, their_down)
+    out_ends, theirs, out_parts, grad_q_bf, key_grad, value_grad, down_w = tie(
+        out_ends, theirs, out_parts, grad_q_bf, key_grad, value_grad, down_w
+    )
+    down_part = lax.psum_scatter(down_w, "rep", scatter_dimension=0, tiled=True)
+    out_beside = at.collect_beside(out_parts)
+    out_near = out_ends + out_beside
+    wide_w = None
+    for place, ((lefts, rights), their) in enumerate(zip(pairs[1:], theirs)):
+        wide_w = outer_blocks(lefts, rights, 0, units, their, wide_w, place, 2)
 
     def kv_rows(first, core):
         begin = (2 * first + core) * rows_dev
@@ -937,17 +942,18 @@
     kv_parts = [
         kv_part((at.chip + j) % 2 if at.four else (at.chip + j) % at.chips) for j in offsets
     ]
-    q_other_w = at.lane_outer(normed_bf, grad_q_bf, other_core)
-    kv_parts, q_other_w, wide_part = tie(kv_parts, q_other_w, wide_part)
-    wide_sum = lax.all_gather(wide_part, "rep", axis=0, tiled=True)
+    q_other_w = outer_blocks([normed_other], [grad_q_bf], 0, width // 2)
+    q_mine = outer_blocks([normed_mine], [grad_q_bf], 0, width // 2)
+    kv_parts, out_near, wide_w, q_other_w, q_mine = tie(
+        kv_parts, out_near, wide_w, q_other_w, q_mine
+    )
+    wide_part = lax.psum_scatter(wide_w, "rep", scatter_dimension=0, tiled=True)
     if at.four:
         pair_sum = kv_parts[0] + at.chip_swap(kv_parts[1].astype(BF), 1).astype(F32)
-        q_mine = at.lane_outer(normed_bf, grad_q_bf, core)
-        pair_sum, q_mine = tie(pair_sum, q_mine)
+        pair_sum, out_near, down_part = tie(pair_sum, out_near, down_part)
         prompt_parts = [at.chip_send(pair_sum.astype(BF), [(2, 0), (3, 1)])]
     else:
         pair_sum = kv_parts[0]
-        q_mine = at.lane_outer(normed_bf, grad_q_bf, core)
         prompt_parts = [
             at.chip_send(
                 kv_parts[j].astype(BF), [((i - j) % at.chips, i) for i in range(prompt_chips)]
@@ -955,14 +961,10 @@
             for j in range(1, at.chips)
         ]
     q_leaving = at.core_swap(q_other_w)
-    grad_normed = grad_normed + back_dot(grad_mid_bf, left_all)
-    grad_normed = grad_normed + back_dot(grad_q_bf, q_all)
+    out_far = at.collect_far(out_parts, out_near)
+    down_sum = lax.all_gather(down_part, "rep", axis=0, tiled=True)
+    prompt_parts, pair_sum, q_leaving = tie(prompt_parts, pair_sum, q_leaving)
     q_parts = at.lane_parts([q_mine], [q_leaving])
-    prompt_parts, pair_sum, q_parts, grad_normed = tie(
-        prompt_parts, pair_sum, q_parts, grad_normed
-    )
-
-    out_far = at.collect_far(out_parts, out_near)
     q_near = at.collect_near(q_parts)
     prompt_sum = pair_sum
     for sent in prompt_parts:
@@ -973,9 +975,10 @@
         jnp.concatenate([key_grad[prompt_len:], value_grad[prompt_len:]], axis=1),
     )
     grad_kv_bf, k_gain_row = kv_prep_back(kv_proj, kv_sum, cosine, sine, qk_gain)
-    kv_other_w = at.lane_outer(normed_bf, grad_kv_bf, other_core)
-    kv_mine = at.lane_outer(normed_bf, grad_kv_bf, core)
-    grad_normed = grad_normed + back_dot(grad_kv_bf, kv_weight)
+    kv_other_w = outer_sum(normed_other, grad_kv_bf).astype(BF)
+    kv_mine = outer_sum(normed_mine, grad_kv_bf).astype(BF)
+    grad_normed = grad_normed + back_dot(grad_mid_bf, left_all)
+    grad_normed = grad_normed + back_dot(grad_q_bf, q_all) + back_dot(grad_kv_bf, kv_weight)
     grad_first, gain_input = input_pull(grad_normed)
     grad_tokens = grad_inputs + grad_first
     gain_total = gain_total + gain_middle + gain_input
@@ -987,26 +990,28 @@
     gain_pack = jnp.concatenate([by_owner(gain_total), by_owner(qk_total)], axis=1).astype(BF)
     gain_pack = jnp.pad(gain_pack, ((0, 0), (0, shard * 128 - gain_pack.shape[1])))
     gain_mine, gain_leaving = at.lanes(gain_pack.reshape(-1, 128))
-    out_far, q_near, kv_other_w, kv_mine, gain_mine, gain_leaving, grad_tokens = tie(
-        out_far, q_near, kv_other_w, kv_mine, gain_mine, gain_leaving, grad_tokens
-    )
+    out_far, q_near, kv_other_w, kv_mine, gain_mine, gain_leaving, grad_tokens, wide_part = tie(
+        out_far, q_near, kv_other_w, kv_mine, gain_mine, gain_leaving, grad_tokens, wide_part
+    )
+    wide_sum = lax.all_gather(wide_part, "rep", axis=0, tiled=True)
     out_ready = at.collect_sum(out_parts[0], out_far).astype(BF)
-    kv_leaving, gain_leaving, wide_sum, out_ready = tie(
-        at.core_swap(kv_other_w), at.core_swap(gain_leaving), wide_sum, out_ready
-    )
     q_far = at.collect_far(q_parts, q_near)
+    kv_leaving, gain_leaving, out_ready = tie(
+        at.core_swap(kv_other_w), at.core_swap(gain_leaving), out_ready
+    )
     kv_w_parts = at.lane_parts([kv_mine, gain_mine], [kv_leaving, gain_leaving])
     kv_near = at.collect_near(kv_w_parts)
-    grad_gate_up, grad_down = join_pair(wide_sum, units), wide_sum[:units].astype(F32)
-    q_far, kv_near, grad_gate_up, grad_down = tie(q_far, kv_near, grad_gate_up, grad_down)
     out_total = at.copies_sum(out_ready)
+    q_far, kv_near, out_total, down_sum = tie(q_far, kv_near, out_total, down_sum)
     kv_far = at.collect_far(kv_w_parts, kv_near)
     q_total = at.copies_sum(at.collect_sum(q_parts[0], q_far))
-    kv_far, q_total, out_total = tie(kv_far, q_total, out_total)
+    out_sum = at.copies_all(out_total)
+    grad_down = down_sum.astype(F32)
+    kv_far, q_total, out_sum, grad_down = tie(kv_far, q_total, out_sum, grad_down)
     kv_total = at.copies_sum(at.collect_sum(kv_w_parts[0], kv_far))
     q_sum = at.copies_all(q_total)
-    out_sum = at.copies_all(out_total)
-    kv_total, q_sum, out_sum = tie(kv_total, q_sum, out_sum)
+    kv_total, q_sum = tie(kv_total, q_sum)
+    grad_gate_up = join_pair(wide_sum, units)
     kv_sum_w = at.copies_all(kv_total)
     gain_out = kv_sum_w[:, 2 * KVH * HD :].reshape(-1)
     return (

time: 1070 us -> 1060 us (level)
    ppermute x18, waiting for transfers between devices: 40.6 us -> 78.2 us  [copy_swap(): lax.ppermute(array, 'rep', [(i, i ^ mask) for i in range(self.copies)])]
    ppermute x35 -> x34, waiting for transfers between devices: 354 us -> 322 us  [chip_send(): return lax.ppermute(array, 'fsdp', pairs)]
    pallas_call x6 -> x0, Pallas kernels: 29.4 us -> none  [lane_outer(): pl.pallas_call(kernel, grid_spec=pltpu.PrefetchScalarGridSpec(num_scalar_...]
    add x7 -> x0, other arithmetic: 23.4 us -> none  [the longest x6 23 us: part(): lax.dynamic_slice_in_dim(own, chip * rows, rows, 0).astype(F32)]
    pallas_call x6 -> x10, Pallas kernels: 55.2 us -> 74.9 us  [outer_blocks(): pl.pallas_call(kernel, grid=(tiles,), in_specs=specs, out_specs=pl.BlockS...]
    dot_general x7 -> x6, matrix products: 26.7 us -> 17.7 us  [back_dot(): lax.dot_general(gradient, weight, (((1,), (1,)), ((), ())), preferred_ele...]
    ppermute x35 -> x34, starting transfers between devices: 118 us -> 123 us  [chip_send(): return lax.ppermute(array, 'fsdp', pairs)]
  transfers between devices with their start and end apart: 72 -> 73, of which waited for: 32 -> 33; matrix products, arithmetic and copies ran while one was open for 15% -> 16% of each run, Pallas kernels for 25% -> 25%
where the time goes in v3:
time: 1060 us; the launch traced here: 1040 us
  waiting for transfers between devices  404 us (38%)
  Pallas kernels  268 us (25%)
  starting transfers between devices  146 us (14%)
  other arithmetic  107 us (10%)
  matrix products  52.4 us (5%)
  local copies, waits for them, and re-layouts  50.4 us (5%)
  between operations  16.2 us (2%)
    ppermute x34, waiting for transfers between devices, chip_send(): return lax.ppermute(array, 'fsdp', pairs)  322 us
    ppermute x34, starting transfers between devices, chip_send(): return lax.ppermute(array, 'fsdp', pairs)  123 us
    ppermute x18, waiting for transfers between devices, copy_swap(): lax.ppermute(array, 'rep', [(i, i ^ mask) for i in range(self.copies)])  78.2 us
    pallas_call x10, Pallas kernels, outer_blocks(): pl.pallas_call(kernel, grid=(tiles,), in_specs=specs, out_specs=pl.BlockS...  74.9 us
    pallas_call x3, Pallas kernels, ffn_block_back(): pl.pallas_call(kernel, grid=(2 * tiles,), in_specs=[whole] * count + [par...  58.7 us
    pallas_call x3, Pallas kernels, ffn_block(): pl.pallas_call(kernel, grid=(2 * tiles,), in_specs=[whole] * count + half...  53.3 us
    pallas_call x1, Pallas kernels, attend_back(): pl.pallas_call(kernel, grid=(H,), in_specs=[pl.BlockSpec(memory_space=plt...  26.4 us
    dot_general x7, matrix products, dot(): return jnp.dot(left_mat, right_mat, preferred_element_type=F32)  21.9 us
  transfers between devices with their start and end apart: 73, of which 33 were waited for; matrix products, arithmetic and copies ran while one was open for 16% of the time, Pallas kernels for 25%

profile of v3, /device:TPU:0, one launch (start us, length us, event | category | flops | bytes accessed | tf_op | source)
XLA Modules:
  0.0 1044.6 jit_solution(746586662152775873)
XLA Ops:
  25.1 19.0 %split_pair.1 = (bf16[1024,2048]{1,0:T(8,128)(2,1)}, bf16[1024,2048]{1,0:T(8,128)(2,1)}) custom-call(f32[1024,2,2048]{2,1,0:T(2,128)} %pair_ref.1), custom_call_target="tpu_custom_call" | custom-call | bytes 25165824 | tf_op jit(solution)/shard_map/split_pair/pallas_call | solution.py:605
  63.6 32.9 %collective-permute-done.3 = bf16[256,1152]{1,0:T(8,128)(2,1)S(1)} collective-permute-done((bf16[256,1152]{1,0:T(8,128)(2,1)S(1)}, bf16[256,1152]{1,0:T(8,128)(2,1)S(1)}, u32[]{:S(2)}, u32[]{:S(2)}) %collective-permute-start.3) | collective-permute-done | bytes 589856 | tf_op jit(solution)/shard_map/ppermute | solution.py:245
  119.6 23.7 %collective-permute-done.6 = bf16[256,1024]{1,0:T(8,128)(2,1)S(1)} collective-permute-done((bf16[256,1024]{1,0:T(8,128)(2,1)}, bf16[256,1024]{1,0:T(8,128)(2,1)S(1)}, u32[]{:S(2)}, u32[]{:S(2)}) %collective-permute-start.6) | collective-permute-done | bytes 524320 | tf_op jit(solution)/shard_map/ppermute | solution.py:245
  144.4 26.7 %collective-permute-start.7 = (bf16[256,1024]{1,0:T(8,128)(2,1)S(1)}, bf16[256,1024]{1,0:T(8,128)(2,1)}, u32[]{:S(2)}, u32[]{:S(2)}) collective-permute-start(bf16[256,1024]{1,0:T(8,128)(2,1)S(1)} %broadcast_select_fusion.6), channel_id=1, source_target_pairs={{0,2},{1,3},{2,0},{3,1},{4,6},{5,7},{6,4},{7,5},{8,10},{9,11},{10,... | collective-permute-start | bytes 1572872 | tf_op jit(solution)/shard_map/ppermute | solution.py:245
  171.1 11.5 %collective-permute-done.7 = bf16[256,1024]{1,0:T(8,128)(2,1)} collective-permute-done((bf16[256,1024]{1,0:T(8,128)(2,1)S(1)}, bf16[256,1024]{1,0:T(8,128)(2,1)}, u32[]{:S(2)}, u32[]{:S(2)}) %collective-permute-start.7) | collective-permute-done | bytes 524320 | tf_op jit(solution)/shard_map/ppermute | solution.py:245
  213.3 12.9 %attend.1 = (bf16[256,2048]{1,0:T(8,128)(2,1)}, bf16[256,2048]{1,0:T(8,128)(2,1)}) custom-call(s32[1]{0:T(128)} %bitcast.at_ref, f32[256,2048]{1,0:T(8,128)} %fusion.4.x_ref, f32[256,128]{1,0:T(8,128)} %get-tuple-element.543.c_ref, f32[256,128]{1,0:T(8,128)} %get-tuple-element.542.s_ref, f32[2,256]{1,0:T(2,128)} %reshape.435.g_ref, ...), custom_call_target="tpu_custom_call" | custom-call | flops 2684354560 | bytes 6815744 | tf_op jit(solution)/shard_map/attend/pallas_call | solution.py:104
  245.2 16.2 %ffn_block.3 = (f32[256,2048]{1,0:T(8,128)}, bf16[256,2048]{1,0:T(8,128)(2,1)}, bf16[256,2048]{1,0:T(8,128)(2,1)}, bf16[256,2048]{1,0:T(8,128)(2,1)}) custom-call(bf16[256,2048]{1,0:T(8,128)(2,1)} %copy-done.9, bf16[1024,2048]{1,0:T(8,128)(2,1)} %get-tuple-element.211.refs_1_.refs_2_.refs_3_.refs_4_, ...), custom_call_target="tpu_custom_call" | custom-call | flops 6442450944 | bytes 31457280 | tf_op jit(solution)/shard_map/ffn_block/pallas_call | solution.py:477
  263.9 25.5 %collective-permute-done.12.refs_0_.refs_4_ = bf16[256,2048]{1,0:T(8,128)(2,1)} collective-permute-done((bf16[256,2048]{1,0:T(8,128)(2,1)S(1)}, bf16[256,2048]{1,0:T(8,128)(2,1)}, u32[]{:S(2)}, u32[]{:S(2)}) %collective-permute-start.12) | collective-permute-done | bytes 1048608 | tf_op jit(solution)/shard_map/ppermute | solution.py:245
  296.0 21.4 %ffn_block.4 = (bf16[256,2048]{1,0:T(8,128)(2,1)}, bf16[256,2048]{1,0:T(8,128)(2,1)}, bf16[512,2048]{1,0:T(8,128)(2,1)}, bf16[512,2048]{1,0:T(8,128)(2,1)}, bf16[512,2048]{1,0:T(8,128)(2,1)}) custom-call(bf16[256,2048]{1,0:T(8,128)(2,1)} %collective-permute-done.12.refs_0_.refs_4_, bf16[256,2048]{1,0:T(8,128)(2,1)} %collective-permute-done.13.refs_1_.refs_5_, ...), custom_call_target="tpu_custom_call" | custom-call | flops 12884901888 | bytes 37748736 | tf_op jit(solution)/shard_map/ffn_block/pallas_call | solution.py:477
  326.5 15.7 %ffn_block.5 = (bf16[256,2048]{1,0:T(8,128)(2,1)}, bf16[256,2048]{1,0:T(8,128)(2,1)}, bf16[256,2048]{1,0:T(8,128)(2,1)}, bf16[256,2048]{1,0:T(8,128)(2,1)}) custom-call(bf16[256,2048]{1,0:T(8,128)(2,1)} %broadcast_select_fusion.3.refs_0_.refs_6_, bf16[1024,2048]{1,0:T(8,128)(2,1)} %get-tuple-element.211.refs_1_.refs_2_.refs_3_.refs_4_, ...), custom_call_target="tpu_custom_call" | custom-call | flops 6442450944 | bytes 31457280 | tf_op jit(solution)/shard_map/ffn_block/pallas_call | solution.py:477
  342.2 24.6 %collective-permute-done.16 = bf16[256,2048]{1,0:T(8,128)(2,1)S(1)} collective-permute-done((bf16[256,2048]{1,0:T(8,128)(2,1)}, bf16[256,2048]{1,0:T(8,128)(2,1)S(1)}, u32[]{:S(2)}, u32[]{:S(2)}) %collective-permute-start.16) | collective-permute-done | bytes 1048608 | tf_op jit(solution)/shard_map/ppermute | solution.py:245
  372.8 20.7 %collective-permute-done.18 = bf16[256,2048]{1,0:T(8,128)(2,1)} collective-permute-done((bf16[256,2048]{1,0:T(8,128)(2,1)}, bf16[256,2048]{1,0:T(8,128)(2,1)}, u32[]{:S(2)}, u32[]{:S(2)}) %collective-permute-start.18) | collective-permute-done | bytes 1048608 | tf_op jit(solution)/shard_map/ppermute | solution.py:245
  406.9 22.9 %collective-permute-start.19 = (bf16[256,2048]{1,0:T(8,128)(2,1)S(1)}, bf16[256,2048]{1,0:T(8,128)(2,1)}, u32[]{:S(2)}, u32[]{:S(2)}) collective-permute-start(bf16[256,2048]{1,0:T(8,128)(2,1)S(1)} %get-tuple-element.283.refs_0_.refs_3_), channel_id=1, source_target_pairs={{0,2},{1,3},{2,0},{3,1},{4,6},{5,7},{6,4},{7,5},{8,10},{9,11},{10,... | collective-permute-start | bytes 3145736 | tf_op jit(solution)/shard_map/ppermute | solution.py:245
  432.8 17.2 %ffn_block_back.3 = (f32[256,2048]{1,0:T(8,128)}, bf16[256,2048]{1,0:T(8,128)(2,1)}, bf16[256,2048]{1,0:T(8,128)(2,1)}) custom-call(bf16[256,2048]{1,0:T(8,128)(2,1)} %copy-done.18, bf16[256,2048]{1,0:T(8,128)(2,1)} %get-tuple-element.239.refs_1_, bf16[256,2048]{1,0:T(8,128)(2,1)} %get-tuple-element.240.refs_2_, ...), custom_call_target="tpu_custom_call" | custom-call | flops 6442450944 | bytes 32505856 | tf_op jit(solution)/shard_map/ffn_block_back/pallas_call | solution.py:537
  450.0 23.7 %collective-permute-done.19.refs_0_.refs_4_ = bf16[256,2048]{1,0:T(8,128)(2,1)} collective-permute-done((bf16[256,2048]{1,0:T(8,128)(2,1)S(1)}, bf16[256,2048]{1,0:T(8,128)(2,1)}, u32[]{:S(2)}, u32[]{:S(2)}) %collective-permute-start.19) | collective-permute-done | bytes 1048608 | tf_op jit(solution)/shard_map/ppermute | solution.py:245
  480.6 24.8 %ffn_block_back.4 = (bf16[256,2048]{1,0:T(8,128)(2,1)}, bf16[256,2048]{1,0:T(8,128)(2,1)}, bf16[512,2048]{1,0:T(8,128)(2,1)}, bf16[512,2048]{1,0:T(8,128)(2,1)}) custom-call(bf16[256,2048]{1,0:T(8,128)(2,1)} %collective-permute-done.19.refs_0_.refs_4_, bf16[256,2048]{1,0:T(8,128)(2,1)} %collective-permute-done.20.refs_1_.refs_5_, ...), custom_call_target="tpu_custom_call" | custom-call | flops 12884901888 | bytes 39845888 | tf_op jit(solution)/shard_map/ffn_block_back/pallas_call | solution.py:537
  512.8 16.7 %ffn_block_back.5 = (bf16[256,2048]{1,0:T(8,128)(2,1)}, bf16[256,2048]{1,0:T(8,128)(2,1)}, bf16[256,2048]{1,0:T(8,128)(2,1)}) custom-call(bf16[256,2048]{1,0:T(8,128)(2,1)} %broadcast_select_fusion.2.refs_0_.refs_6_, bf16[256,2048]{1,0:T(8,128)(2,1)} %get-tuple-element.260.refs_1_, bf16[256,2048]{1,0:T(8,128)(2,1)} %get-tuple-element.261.refs_2_, ...), custom_call_target="tpu_custom_call" | custom-call | flops 6442450944 | bytes 32505856 | tf_op jit(solution)/shard_map/ffn_block_back/pallas_call | solution.py:537
  529.5 22.4 %collective-permute-done.23 = bf16[256,2048]{1,0:T(8,128)(2,1)S(1)} collective-permute-done((bf16[256,2048]{1,0:T(8,128)(2,1)}, bf16[256,2048]{1,0:T(8,128)(2,1)S(1)}, u32[]{:S(2)}, u32[]{:S(2)}) %collective-permute-start.23) | collective-permute-done | bytes 1048608 | tf_op jit(solution)/shard_map/ppermute | solution.py:245
  624.7 14.4 %collective-permute-start.29 = (bf16[256,2688]{1,0:T(8,128)(2,1)S(1)}, bf16[256,2688]{1,0:T(8,128)(2,1)S(1)}, u32[]{:S(2)}, u32[]{:S(2)}) collective-permute-start(bf16[256,2688]{1,0:T(8,128)(2,1)S(1)} %pad_maximum_fusion.2), channel_id=1, source_target_pairs={{0,2},{1,3},{6,4},{7,5},{8,10},{9,11},{14,12},{15,13},{16,18},{17,... | collective-permute-start | bytes 4128776 | tf_op jit(solution)/shard_map/ppermute | solution.py:245
  642.8 10.0 outer_blocks.15
  652.8 26.4 %attend_back.1 = (bf16[256,2048]{1,0:T(8,128)(2,1)}, f32[1280,512]{1,0:T(8,128)}, f32[1280,512]{1,0:T(8,128)}, f32[8,1,256]{2,1,0:T(1,128)}) custom-call(s32[1]{0:T(128)} %bitcast.at_ref, f32[256,2048]{1,0:T(8,128)} %fusion.4.x_ref, bf16[256,2048]{1,0:T(8,128)(2,1)} %get-tuple-element.316.q_ref, f32[256,128]{1,0:T(8,128)} %get-tuple-element.543.c_ref, ...), custom_call_target="tpu_custom_call" | custom-call | flops 6710886400 | bytes 13107200 | tf_op jit(solution)/shard_map/attend_back/pallas_call | solution.py:155
  696.4 9.7 outer_blocks.16.refs_8_
  706.2 9.7 outer_blocks.17
  726.0 12.5 %collective-permute-done.35 = bf16[256,1024]{1,0:T(8,128)(2,1)S(1)} collective-permute-done((bf16[256,1024]{1,0:T(8,128)(2,1)S(1)}, bf16[256,1024]{1,0:T(8,128)(2,1)S(1)}, u32[]{:S(2)}, u32[]{:S(2)}) %collective-permute-start.35) | collective-permute-done | bytes 524320 | tf_op jit(solution)/shard_map/ppermute | solution.py:245
  751.9 52.0 %collective-permute-done.37 = bf16[256,1024]{1,0:T(8,128)(2,1)S(1)} collective-permute-done((bf16[256,1024]{1,0:T(8,128)(2,1)S(1)}, bf16[256,1024]{1,0:T(8,128)(2,1)S(1)}, u32[]{:S(2)}, u32[]{:S(2)}) %collective-permute-start.37) | collective-permute-done | bytes 524320 | tf_op jit(solution)/shard_map/ppermute | solution.py:245
  836.6 18.2 %collective-permute-done.40 = bf16[256,2048]{1,0:T(8,128)(2,1)} collective-permute-done((bf16[256,2048]{1,0:T(8,128)(2,1)}, bf16[256,2048]{1,0:T(8,128)(2,1)}, u32[]{:S(2)}, u32[]{:S(2)}) %collective-permute-start.40) | collective-permute-done | bytes 1048608 | tf_op jit(solution)/shard_map/ppermute | solution.py:245
  891.1 16.6 %collective-permute-done.44 = bf16[256,2048]{1,0:T(8,128)(2,1)} collective-permute-done((bf16[256,2048]{1,0:T(8,128)(2,1)}, bf16[256,2048]{1,0:T(8,128)(2,1)}, u32[]{:S(2)}, u32[]{:S(2)}) %collective-permute-start.44) | collective-permute-done | bytes 1048608 | tf_op jit(solution)/shard_map/ppermute | solution.py:245
  907.7 12.1 %collective-permute-done.46 = bf16[256,1152]{1,0:T(8,128)(2,1)} collective-permute-done((bf16[256,1152]{1,0:T(8,128)(2,1)S(1)}, bf16[256,1152]{1,0:T(8,128)(2,1)}, u32[]{:S(2)}, u32[]{:S(2)}) %collective-permute-start.46) | collective-permute-done | bytes 589856 | tf_op jit(solution)/shard_map/ppermute | solution.py:245
  936.4 10.6 %collective-permute-done.52 = bf16[64,2048]{1,0:T(8,128)(2,1)S(1)} collective-permute-done((bf16[64,2048]{1,0:T(8,128)(2,1)S(1)}, bf16[64,2048]{1,0:T(8,128)(2,1)S(1)}, u32[]{:S(2)}, u32[]{:S(2)}) %collective-permute-start.52) | collective-permute-done | bytes 262176 | tf_op jit(solution)/shard_map/ppermute | solution.py:241
  959.0 12.7 %collective-permute-done.57 = bf16[64,2688]{1,0:T(8,128)(2,1)S(1)} collective-permute-done((bf16[64,2688]{1,0:T(8,128)(2,1)S(1)}, bf16[64,2688]{1,0:T(8,128)(2,1)S(1)}, u32[]{:S(2)}, u32[]{:S(2)}) %collective-permute-start.57) | collective-permute-done | bytes 344096 | tf_op jit(solution)/shard_map/ppermute | solution.py:241
  985.5 10.0 collective-permute-done.58
  1026.3 11.3 %join_pair.1 = f32[1024,2,2048]{2,1,0:T(2,128)} custom-call(bf16[2048,2048]{1,0:T(8,128)(2,1)} %all-gather.11.cloned.1.call-done.first_ref.second_ref, bf16[2048,2048]{1,0:T(8,128)(2,1)} %all-gather.11.cloned.1.call-done.first_ref.second_ref), custom_call_target="tpu_custom_call" | custom-call | bytes 25165824 | tf_op jit(solution)/shard_map/join_pair/pallas_call | solution.py:627
  (534 shorter events, 423.6 us)
Async XLA Ops:
  7.2 177.6 %all-gather.5.cloned.1.call-start = ((), (), s32[]{:S(2)}) async-start(), calls=%async_computation.2 | async-start | bytes 17842176 | tf_op jit(solution)/shard_map/all_gather | solution.py:680
  18.4 350.6 %all-gather.7.cloned.1.call-start = ((), (), s32[]{:S(2)}) async-start(), calls=%async_computation.3 | async-start | bytes 2162688 | tf_op jit(solution)/shard_map/all_gather | solution.py:680
  21.8 40.4 %collective-permute-start.1 = (bf16[256,1152]{1,0:T(8,128)(2,1)S(1)}, bf16[256,1152]{1,0:T(8,128)(2,1)S(1)}, u32[]{:S(2)}, u32[]{:S(2)}) collective-permute-start(bf16[256,1152]{1,0:T(8,128)(2,1)S(1)} %pad_maximum_fusion.12.shard_ref), channel_id=1, source_target_pairs={{0,4},{1,5},{2,6},{3,7},{4,0},{5,1},{6,2},{7,3},{8,12},{9,13},{10,... | collective-permute-start | bytes 1769480 | tf_op jit(solution)/shard_map/ppermute | solution.py:245
  24.4 39.2 %collective-permute-start.4 = (bf16[256,1152]{1,0:T(8,128)(2,1)S(1)}, bf16[256,1152]{1,0:T(8,128)(2,1)S(1)}, u32[]{:S(2)}, u32[]{:S(2)}) collective-permute-start(bf16[256,1152]{1,0:T(8,128)(2,1)S(1)} %pad_maximum_fusion.12.shard_ref), channel_id=1, source_target_pairs={{2,4},{3,5},{4,2},{5,3},{10,12},{11,13},{12,10},{13,11},{18,20},{1... | collective-permute-start | bytes 1769480 | tf_op jit(solution)/shard_map/ppermute | solution.py:245
  100.6 97.1 %collective-permute-start.10 = (bf16[1024,2048]{1,0:T(8,128)(2,1)}, bf16[1024,2048]{1,0:T(8,128)(2,1)}, u32[]{:S(2)}, u32[]{:S(2)}) collective-permute-start(bf16[1024,2048]{1,0:T(8,128)(2,1)} %convert_element_type.481.refs_5_.refs_6_.refs_7_.refs_8_), channel_id=1, source_target_pairs={{0,1},{1,0},{2,3},{3,2},{4,5},{5,4},{6,7},{7,6},{8,9},{9,8},{10,11... | collective-permute-start | bytes 12582920 | tf_op jit(solution)/shard_map/ppermute | solution.py:238
  100.9 96.8 %collective-permute-start.8 = (bf16[1024,2048]{1,0:T(8,128)(2,1)}, bf16[1024,2048]{1,0:T(8,128)(2,1)}, u32[]{:S(2)}, u32[]{:S(2)}) collective-permute-start(bf16[1024,2048]{1,0:T(8,128)(2,1)} %get-tuple-element.211.refs_1_.refs_2_.refs_3_.refs_4_), channel_id=1, source_target_pairs={{0,1},{1,0},{2,3},{3,2},{4,5},{5,4},{6,7},{7,6},{8,9},{9,8},{10,11... | collective-permute-start | bytes 12582920 | tf_op jit(solution)/shard_map/ppermute | solution.py:238
  101.1 96.6 %collective-permute-start.9 = (bf16[1024,2048]{1,0:T(8,128)(2,1)}, bf16[1024,2048]{1,0:T(8,128)(2,1)}, u32[]{:S(2)}, u32[]{:S(2)}) collective-permute-start(bf16[1024,2048]{1,0:T(8,128)(2,1)} %get-tuple-element.213.refs_3_.refs_4_.refs_5_.refs_6_), channel_id=1, source_target_pairs={{0,1},{1,0},{2,3},{3,2},{4,5},{5,4},{6,7},{7,6},{8,9},{9,8},{10,11... | collective-permute-start | bytes 12582920 | tf_op jit(solution)/shard_map/ppermute | solution.py:238
  201.0 538.8 %reduce-scatter.3.cloned.1.call-start = ((), (), s32[]{:S(2)}) async-start(), calls=%async_computation.4 | async-start | bytes 5242880 | tf_op jit(solution)/shard_map/reduce_scatter | solution.py:915
  234.8 54.6 %collective-permute-start.12 = (bf16[256,2048]{1,0:T(8,128)(2,1)S(1)}, bf16[256,2048]{1,0:T(8,128)(2,1)}, u32[]{:S(2)}, u32[]{:S(2)}) collective-permute-start(bf16[256,2048]{1,0:T(8,128)(2,1)S(1)} %multiply_convert_fusion.refs_0_.refs_3_), channel_id=1, source_target_pairs={{0,2},{1,3},{2,0},{3,1},{4,6},{5,7},{6,4},{7,5},{8,10},{9,11},{10,... | collective-permute-start | bytes 3145736 | tf_op jit(solution)/shard_map/ppermute | solution.py:245
  236.6 57.7 %collective-permute-start.13 = (bf16[256,2048]{1,0:T(8,128)(2,1)S(1)}, bf16[256,2048]{1,0:T(8,128)(2,1)}, u32[]{:S(2)}, u32[]{:S(2)}) collective-permute-start(bf16[256,2048]{1,0:T(8,128)(2,1)S(1)} %multiply_convert_fusion.refs_0_.refs_3_), channel_id=1, source_target_pairs={{0,4},{1,5},{2,6},{3,7},{4,0},{5,1},{6,2},{7,3},{8,12},{9,13},{10,... | collective-permute-start | bytes 3145736 | tf_op jit(solution)/shard_map/ppermute | solution.py:245
  243.5 73.9 %collective-permute-start.15 = (bf16[256,2048]{1,0:T(8,128)(2,1)S(1)}, bf16[256,2048]{1,0:T(8,128)(2,1)}, u32[]{:S(2)}, u32[]{:S(2)}) collective-permute-start(bf16[256,2048]{1,0:T(8,128)(2,1)S(1)} %multiply_convert_fusion.refs_0_.refs_3_), channel_id=1, source_target_pairs={{2,4},{3,5},{4,2},{5,3},{10,12},{11,13},{12,10},{13,11},{18,20},{1... | collective-permute-start | bytes 3145736 | tf_op jit(solution)/shard_map/ppermute | solution.py:245
  321.5 45.2 %collective-permute-start.16 = (bf16[256,2048]{1,0:T(8,128)(2,1)}, bf16[256,2048]{1,0:T(8,128)(2,1)S(1)}, u32[]{:S(2)}, u32[]{:S(2)}) collective-permute-start(bf16[256,2048]{1,0:T(8,128)(2,1)} %get-tuple-element.229), channel_id=1, source_target_pairs={{0,2},{1,3},{2,0},{3,1},{4,6},{5,7},{6,4},{7,5},{8,10},{9,11},{10,... | collective-permute-start | bytes 3145736 | tf_op jit(solution)/shard_map/ppermute | solution.py:245
  323.4 49.4 %collective-permute-start.17 = (bf16[256,2048]{1,0:T(8,128)(2,1)}, bf16[256,2048]{1,0:T(8,128)(2,1)}, u32[]{:S(2)}, u32[]{:S(2)}) collective-permute-start(bf16[256,2048]{1,0:T(8,128)(2,1)} %get-tuple-element.236), channel_id=1, source_target_pairs={{0,4},{1,5},{2,6},{3,7},{4,0},{5,1},{6,2},{7,3},{8,12},{9,13},{10,... | collective-permute-start | bytes 3145736 | tf_op jit(solution)/shard_map/ppermute | solution.py:245
  406.9 66.8 %collective-permute-start.19 = (bf16[256,2048]{1,0:T(8,128)(2,1)S(1)}, bf16[256,2048]{1,0:T(8,128)(2,1)}, u32[]{:S(2)}, u32[]{:S(2)}) collective-permute-start(bf16[256,2048]{1,0:T(8,128)(2,1)S(1)} %get-tuple-element.283.refs_0_.refs_3_), channel_id=1, source_target_pairs={{0,2},{1,3},{2,0},{3,1},{4,6},{5,7},{6,4},{7,5},{8,10},{9,11},{10,... | collective-permute-start | bytes 3145736 | tf_op jit(solution)/shard_map/ppermute | solution.py:245
  429.8 49.5 %collective-permute-start.20 = (bf16[256,2048]{1,0:T(8,128)(2,1)S(1)}, bf16[256,2048]{1,0:T(8,128)(2,1)}, u32[]{:S(2)}, u32[]{:S(2)}) collective-permute-start(bf16[256,2048]{1,0:T(8,128)(2,1)S(1)} %get-tuple-element.283.refs_0_.refs_3_), channel_id=1, source_target_pairs={{0,4},{1,5},{2,6},{3,7},{4,0},{5,1},{6,2},{7,3},{8,12},{9,13},{10,... | collective-permute-start | bytes 3145736 | tf_op jit(solution)/shard_map/ppermute | solution.py:245
  431.1 74.3 %collective-permute-start.22 = (bf16[256,2048]{1,0:T(8,128)(2,1)S(1)}, bf16[256,2048]{1,0:T(8,128)(2,1)}, u32[]{:S(2)}, u32[]{:S(2)}) collective-permute-start(bf16[256,2048]{1,0:T(8,128)(2,1)S(1)} %get-tuple-element.283.refs_0_.refs_3_), channel_id=1, source_target_pairs={{2,4},{3,5},{4,2},{5,3},{10,12},{11,13},{12,10},{13,11},{18,20},{1... | collective-permute-start | bytes 3145736 | tf_op jit(solution)/shard_map/ppermute | solution.py:245
  507.8 44.0 %collective-permute-start.23 = (bf16[256,2048]{1,0:T(8,128)(2,1)}, bf16[256,2048]{1,0:T(8,128)(2,1)S(1)}, u32[]{:S(2)}, u32[]{:S(2)}) collective-permute-start(bf16[256,2048]{1,0:T(8,128)(2,1)} %get-tuple-element.258), channel_id=1, source_target_pairs={{0,2},{1,3},{2,0},{3,1},{4,6},{5,7},{6,4},{7,5},{8,10},{9,11},{10,... | collective-permute-start | bytes 3145736 | tf_op jit(solution)/shard_map/ppermute | solution.py:245
  511.5 78.5 %collective-permute-start.24 = (bf16[256,2048]{1,0:T(8,128)(2,1)}, bf16[256,2048]{1,0:T(8,128)(2,1)}, u32[]{:S(2)}, u32[]{:S(2)}) collective-permute-start(bf16[256,2048]{1,0:T(8,128)(2,1)} %get-tuple-element.268), channel_id=1, source_target_pairs={{0,4},{1,5},{2,6},{3,7},{4,0},{5,1},{6,2},{7,3},{8,12},{9,13},{10,... | collective-permute-start | bytes 3145736 | tf_op jit(solution)/shard_map/ppermute | solution.py:245
  617.2 62.0 %collective-permute-start.30 = (bf16[1024,2048]{1,0:T(8,128)(2,1)}, bf16[1024,2048]{1,0:T(8,128)(2,1)}, u32[]{:S(2)}, u32[]{:S(2)}) collective-permute-start(bf16[1024,2048]{1,0:T(8,128)(2,1)} %outer_blocks.11), channel_id=1, source_target_pairs={{0,1},{1,0},{2,3},{3,2},{4,5},{5,4},{6,7},{7,6},{8,9},{9,8},{10,11... | collective-permute-start | bytes 12582920 | tf_op jit(solution)/shard_map/ppermute | solution.py:238
  617.3 61.9 %collective-permute-start.31 = (bf16[1024,2048]{1,0:T(8,128)(2,1)}, bf16[1024,2048]{1,0:T(8,128)(2,1)}, u32[]{:S(2)}, u32[]{:S(2)}) collective-permute-start(bf16[1024,2048]{1,0:T(8,128)(2,1)} %outer_blocks.12), channel_id=1, source_target_pairs={{0,1},{1,0},{2,3},{3,2},{4,5},{5,4},{6,7},{7,6},{8,9},{9,8},{10,11... | collective-permute-start | bytes 12582920 | tf_op jit(solution)/shard_map/ppermute | solution.py:238
  624.7 54.4 %collective-permute-start.29 = (bf16[256,2688]{1,0:T(8,128)(2,1)S(1)}, bf16[256,2688]{1,0:T(8,128)(2,1)S(1)}, u32[]{:S(2)}, u32[]{:S(2)}) collective-permute-start(bf16[256,2688]{1,0:T(8,128)(2,1)S(1)} %pad_maximum_fusion.2), channel_id=1, source_target_pairs={{0,2},{1,3},{6,4},{7,5},{8,10},{9,11},{14,12},{15,13},{16,18},{17,... | collective-permute-start | bytes 4128776 | tf_op jit(solution)/shard_map/ppermute | solution.py:245
  680.2 174.6 %reduce-scatter.5.cloned.1.call-start = ((), (), s32[]{:S(2)}) async-start(), calls=%async_computation.5 | async-start | bytes 10485760 | tf_op jit(solution)/shard_map/reduce_scatter | solution.py:950
  680.2 40.0 %collective-permute-start.33 = (bf16[256,2688]{1,0:T(8,128)(2,1)}, bf16[256,2688]{1,0:T(8,128)(2,1)S(1)}, u32[]{:S(2)}, u32[]{:S(2)}) collective-permute-start(bf16[256,2688]{1,0:T(8,128)(2,1)} %pad_maximum_fusion.4), channel_id=1, source_target_pairs={{0,2},{1,3},{2,0},{3,1},{4,6},{5,7},{6,4},{7,5},{8,10},{9,11},{10,... | collective-permute-start | bytes 4128776 | tf_op jit(solution)/shard_map/ppermute | solution.py:245
  680.2 40.0 %collective-permute-start.34 = (bf16[256,2688]{1,0:T(8,128)(2,1)}, bf16[256,2688]{1,0:T(8,128)(2,1)S(1)}, u32[]{:S(2)}, u32[]{:S(2)}) collective-permute-start(bf16[256,2688]{1,0:T(8,128)(2,1)} %copy-done.44), channel_id=1, source_target_pairs={{2,4},{3,5},{4,2},{5,3},{10,12},{11,13},{12,10},{13,11},{18,20},{1... | collective-permute-start | bytes 4128776 | tf_op jit(solution)/shard_map/ppermute | solution.py:245
  721.8 169.2 %all-gather.9.cloned.1.call-start = ((), (), s32[]{:S(2)}) async-start(), calls=%async_computation.6 | async-start | bytes 5242880 | tf_op jit(solution)/shard_map/all_gather | solution.py:965
  739.9 286.4 %all-gather.11.cloned.1.call-start = ((), (), s32[]{:S(2)}) async-start(), calls=%async_computation.7 | async-start | bytes 10485760 | tf_op jit(solution)/shard_map/all_gather | solution.py:996
  745.3 58.6 %collective-permute-start.37 = (bf16[256,1024]{1,0:T(8,128)(2,1)S(1)}, bf16[256,1024]{1,0:T(8,128)(2,1)S(1)}, u32[]{:S(2)}, u32[]{:S(2)}) collective-permute-start(bf16[256,1024]{1,0:T(8,128)(2,1)S(1)} %convert_element_type.555), channel_id=1, source_target_pairs={{4,0},{5,1},{6,2},{7,3},{12,8},{13,9},{14,10},{15,11},{20,16},{21,... | collective-permute-start | bytes 1572872 | tf_op jit(solution)/shard_map/ppermute | solution.py:245
  748.3 88.3 %collective-permute-start.36 = (bf16[256,2688]{1,0:T(8,128)(2,1)}, bf16[256,2688]{1,0:T(8,128)(2,1)}, u32[]{:S(2)}, u32[]{:S(2)}) collective-permute-start(bf16[256,2688]{1,0:T(8,128)(2,1)} %add_convert_fusion.1), channel_id=1, source_target_pairs={{0,4},{1,5},{2,6},{3,7},{4,0},{5,1},{6,2},{7,3},{8,12},{9,13},{10,... | collective-permute-start | bytes 4128776 | tf_op jit(solution)/shard_map/ppermute | solution.py:245
  810.0 44.9 %collective-permute-start.41 = (bf16[256,2048]{1,0:T(8,128)(2,1)}, bf16[256,2048]{1,0:T(8,128)(2,1)}, u32[]{:S(2)}, u32[]{:S(2)}) collective-permute-start(bf16[256,2048]{1,0:T(8,128)(2,1)} %get-tuple-element.458), channel_id=1, source_target_pairs={{2,4},{3,5},{4,2},{5,3},{10,12},{11,13},{12,10},{13,11},{18,20},{1... | collective-permute-start | bytes 3145736 | tf_op jit(solution)/shard_map/ppermute | solution.py:245
  858.8 48.9 %collective-permute-start.44 = (bf16[256,2048]{1,0:T(8,128)(2,1)}, bf16[256,2048]{1,0:T(8,128)(2,1)}, u32[]{:S(2)}, u32[]{:S(2)}) collective-permute-start(bf16[256,2048]{1,0:T(8,128)(2,1)} %add_convert_fusion.4), channel_id=1, source_target_pairs={{0,4},{1,5},{2,6},{3,7},{4,0},{5,1},{6,2},{7,3},{8,12},{9,13},{10,... | collective-permute-start | bytes 3145736 | tf_op jit(solution)/shard_map/ppermute | solution.py:245
  869.6 50.3 %collective-permute-start.45 = (bf16[256,1152]{1,0:T(8,128)(2,1)S(1)}, bf16[256,1152]{1,0:T(8,128)(2,1)S(1)}, u32[]{:S(2)}, u32[]{:S(2)}) collective-permute-start(bf16[256,1152]{1,0:T(8,128)(2,1)S(1)} %pad_maximum_fusion.13), channel_id=1, source_target_pairs={{0,2},{1,3},{6,4},{7,5},{8,10},{9,11},{14,12},{15,13},{16,18},{17,... | collective-permute-start | bytes 1769480 | tf_op jit(solution)/shard_map/ppermute | solution.py:245
  919.8 39.1 %collective-permute-start.55 = (bf16[64,2688]{1,0:T(8,128)(2,1)S(1)}, bf16[64,2688]{1,0:T(8,128)(2,1)S(1)}, u32[]{:S(2)}, u32[]{:S(2)}) collective-permute-start(bf16[64,2688]{1,0:T(8,128)(2,1)S(1)} %add_convert_fusion.19), channel_id=1, source_target_pairs={{0,8},{8,0},{16,24},{24,16},{1,9},{9,1},{17,25},{25,17},{2,10},{10... | collective-permute-start | bytes 1032200 | tf_op jit(solution)/shard_map/ppermute | solution.py:241
  (136 other events, 1880.8 us)
Sparse Core Ops, SparseCore 0:
  18.5 144.2 all-gather.4
  201.2 95.2 all-gather.6
  679.3 51.5 reduce-scatter.2
  734.7 86.3 reduce-scatter.4
  822.8 61.8 all-gather.8
  886.4 130.2 all-gather.10

commit v4 on v3

--- a/solution.py
+++ b/solution.py
@@ -1006,12 +1006,11 @@
     kv_far = at.collect_far(kv_w_parts, kv_near)
     q_total = at.copies_sum(at.collect_sum(q_parts[0], q_far))
     out_sum = at.copies_all(out_total)
-    grad_down = down_sum.astype(F32)
-    kv_far, q_total, out_sum, grad_down = tie(kv_far, q_total, out_sum, grad_down)
+    kv_far, q_total, out_sum, down_sum = tie(kv_far, q_total, out_sum, down_sum)
     kv_total = at.copies_sum(at.collect_sum(kv_w_parts[0], kv_far))
     q_sum = at.copies_all(q_total)
-    kv_total, q_sum = tie(kv_total, q_sum)
-    grad_gate_up = join_pair(wide_sum, units)
+    kv_total, q_sum, down_sum = tie(kv_total, q_sum, down_sum)
+    grad_gate_up, grad_down = join_pair(wide_sum, units), down_sum.astype(F32)
     kv_sum_w = at.copies_all(kv_total)
     gain_out = kv_sum_w[:, 2 * KVH * HD :].reshape(-1)
     return (

time: 1060 us -> 1050 us (level)
  transfers between devices with their start and end apart: 73 -> 73, of which waited for: 33 -> 35; matrix products, arithmetic and copies ran while one was open for 16% -> 16% of each run, Pallas kernels for 25% -> 25%
where the time goes in v4:
time: 1050 us; the launch traced here: 1040 us
  waiting for transfers between devices  400 us (38%)
  Pallas kernels  268 us (26%)
  starting transfers between devices  150 us (14%)
  other arithmetic  105 us (10%)
  matrix products  52.3 us (5%)
  local copies, waits for them, and re-layouts  50.5 us (5%)
  between operations  16.2 us (2%)
    ppermute x34, waiting for transfers between devices, chip_send(): return lax.ppermute(array, 'fsdp', pairs)  321 us
    ppermute x34, starting transfers between devices, chip_send(): return lax.ppermute(array, 'fsdp', pairs)  124 us
    pallas_call x10, Pallas kernels, outer_blocks(): pl.pallas_call(kernel, grid=(tiles,), in_specs=specs, out_specs=pl.BlockS...  74.9 us
    ppermute x18, waiting for transfers between devices, copy_swap(): lax.ppermute(array, 'rep', [(i, i ^ mask) for i in range(self.copies)])  74.7 us
    pallas_call x3, Pallas kernels, ffn_block_back(): pl.pallas_call(kernel, grid=(2 * tiles,), in_specs=[whole] * count + [par...  58.7 us
    pallas_call x3, Pallas kernels, ffn_block(): pl.pallas_call(kernel, grid=(2 * tiles,), in_specs=[whole] * count + half...  53.3 us
    pallas_call x1, Pallas kernels, attend_back(): pl.pallas_call(kernel, grid=(H,), in_specs=[pl.BlockSpec(memory_space=plt...  26.4 us
    ppermute x18, starting transfers between devices, copy_swap(): lax.ppermute(array, 'rep', [(i, i ^ mask) for i in range(self.copies)])  21.9 us
  transfers between devices with their start and end apart: 73, of which 35 were waited for; matrix products, arithmetic and copies ran while one was open for 16% of the time, Pallas kernels for 25%

profile of v4, /device:TPU:0, one launch (start us, length us, event | category | flops | bytes accessed | tf_op | source)
XLA Modules:
  0.0 1041.4 jit_solution(4303255875962751948)
XLA Ops:
  25.1 19.0 %split_pair.1 = (bf16[1024,2048]{1,0:T(8,128)(2,1)}, bf16[1024,2048]{1,0:T(8,128)(2,1)}) custom-call(f32[1024,2,2048]{2,1,0:T(2,128)} %pair_ref.1), custom_call_target="tpu_custom_call" | custom-call | bytes 25165824 | tf_op jit(solution)/shard_map/split_pair/pallas_call | solution.py:605
  63.6 32.9 %collective-permute-done.3 = bf16[256,1152]{1,0:T(8,128)(2,1)S(1)} collective-permute-done((bf16[256,1152]{1,0:T(8,128)(2,1)S(1)}, bf16[256,1152]{1,0:T(8,128)(2,1)S(1)}, u32[]{:S(2)}, u32[]{:S(2)}) %collective-permute-start.3) | collective-permute-done | bytes 589856 | tf_op jit(solution)/shard_map/ppermute | solution.py:245
  119.6 23.7 %collective-permute-done.6 = bf16[256,1024]{1,0:T(8,128)(2,1)S(1)} collective-permute-done((bf16[256,1024]{1,0:T(8,128)(2,1)}, bf16[256,1024]{1,0:T(8,128)(2,1)S(1)}, u32[]{:S(2)}, u32[]{:S(2)}) %collective-permute-start.6) | collective-permute-done | bytes 524320 | tf_op jit(solution)/shard_map/ppermute | solution.py:245
  144.4 26.7 %collective-permute-start.7 = (bf16[256,1024]{1,0:T(8,128)(2,1)S(1)}, bf16[256,1024]{1,0:T(8,128)(2,1)}, u32[]{:S(2)}, u32[]{:S(2)}) collective-permute-start(bf16[256,1024]{1,0:T(8,128)(2,1)S(1)} %broadcast_select_fusion.6), channel_id=1, source_target_pairs={{0,2},{1,3},{2,0},{3,1},{4,6},{5,7},{6,4},{7,5},{8,10},{9,11},{10,... | collective-permute-start | bytes 1572872 | tf_op jit(solution)/shard_map/ppermute | solution.py:245
  171.1 11.5 %collective-permute-done.7 = bf16[256,1024]{1,0:T(8,128)(2,1)} collective-permute-done((bf16[256,1024]{1,0:T(8,128)(2,1)S(1)}, bf16[256,1024]{1,0:T(8,128)(2,1)}, u32[]{:S(2)}, u32[]{:S(2)}) %collective-permute-start.7) | collective-permute-done | bytes 524320 | tf_op jit(solution)/shard_map/ppermute | solution.py:245
  213.3 12.9 %attend.1 = (bf16[256,2048]{1,0:T(8,128)(2,1)}, bf16[256,2048]{1,0:T(8,128)(2,1)}) custom-call(s32[1]{0:T(128)} %bitcast.at_ref, f32[256,2048]{1,0:T(8,128)} %fusion.4.x_ref, f32[256,128]{1,0:T(8,128)} %get-tuple-element.545.c_ref, f32[256,128]{1,0:T(8,128)} %get-tuple-element.544.s_ref, f32[2,256]{1,0:T(2,128)} %reshape.435.g_ref, ...), custom_call_target="tpu_custom_call" | custom-call | flops 2684354560 | bytes 6815744 | tf_op jit(solution)/shard_map/attend/pallas_call | solution.py:104
  245.1 16.2 %ffn_block.3 = (f32[256,2048]{1,0:T(8,128)}, bf16[256,2048]{1,0:T(8,128)(2,1)}, bf16[256,2048]{1,0:T(8,128)(2,1)}, bf16[256,2048]{1,0:T(8,128)(2,1)}) custom-call(bf16[256,2048]{1,0:T(8,128)(2,1)} %copy-done.9, bf16[1024,2048]{1,0:T(8,128)(2,1)} %get-tuple-element.212.refs_1_.refs_2_.refs_3_.refs_4_, ...), custom_call_target="tpu_custom_call" | custom-call | flops 6442450944 | bytes 31457280 | tf_op jit(solution)/shard_map/ffn_block/pallas_call | solution.py:477
  263.9 25.5 %collective-permute-done.12.refs_0_.refs_4_ = bf16[256,2048]{1,0:T(8,128)(2,1)} collective-permute-done((bf16[256,2048]{1,0:T(8,128)(2,1)S(1)}, bf16[256,2048]{1,0:T(8,128)(2,1)}, u32[]{:S(2)}, u32[]{:S(2)}) %collective-permute-start.12) | collective-permute-done | bytes 1048608 | tf_op jit(solution)/shard_map/ppermute | solution.py:245
  296.0 21.4 %ffn_block.4 = (bf16[256,2048]{1,0:T(8,128)(2,1)}, bf16[256,2048]{1,0:T(8,128)(2,1)}, bf16[512,2048]{1,0:T(8,128)(2,1)}, bf16[512,2048]{1,0:T(8,128)(2,1)}, bf16[512,2048]{1,0:T(8,128)(2,1)}) custom-call(bf16[256,2048]{1,0:T(8,128)(2,1)} %collective-permute-done.12.refs_0_.refs_4_, bf16[256,2048]{1,0:T(8,128)(2,1)} %collective-permute-done.13.refs_1_.refs_5_, ...), custom_call_target="tpu_custom_call" | custom-call | flops 12884901888 | bytes 37748736 | tf_op jit(solution)/shard_map/ffn_block/pallas_call | solution.py:477
  326.5 15.7 %ffn_block.5 = (bf16[256,2048]{1,0:T(8,128)(2,1)}, bf16[256,2048]{1,0:T(8,128)(2,1)}, bf16[256,2048]{1,0:T(8,128)(2,1)}, bf16[256,2048]{1,0:T(8,128)(2,1)}) custom-call(bf16[256,2048]{1,0:T(8,128)(2,1)} %broadcast_select_fusion.3.refs_0_.refs_6_, bf16[1024,2048]{1,0:T(8,128)(2,1)} %get-tuple-element.212.refs_1_.refs_2_.refs_3_.refs_4_, ...), custom_call_target="tpu_custom_call" | custom-call | flops 6442450944 | bytes 31457280 | tf_op jit(solution)/shard_map/ffn_block/pallas_call | solution.py:477
  342.2 24.5 %collective-permute-done.16 = bf16[256,2048]{1,0:T(8,128)(2,1)S(1)} collective-permute-done((bf16[256,2048]{1,0:T(8,128)(2,1)}, bf16[256,2048]{1,0:T(8,128)(2,1)S(1)}, u32[]{:S(2)}, u32[]{:S(2)}) %collective-permute-start.16) | collective-permute-done | bytes 1048608 | tf_op jit(solution)/shard_map/ppermute | solution.py:245
  372.8 20.6 %collective-permute-done.18 = bf16[256,2048]{1,0:T(8,128)(2,1)} collective-permute-done((bf16[256,2048]{1,0:T(8,128)(2,1)}, bf16[256,2048]{1,0:T(8,128)(2,1)}, u32[]{:S(2)}, u32[]{:S(2)}) %collective-permute-start.18) | collective-permute-done | bytes 1048608 | tf_op jit(solution)/shard_map/ppermute | solution.py:245
  406.8 22.9 %collective-permute-start.19 = (bf16[256,2048]{1,0:T(8,128)(2,1)S(1)}, bf16[256,2048]{1,0:T(8,128)(2,1)}, u32[]{:S(2)}, u32[]{:S(2)}) collective-permute-start(bf16[256,2048]{1,0:T(8,128)(2,1)S(1)} %get-tuple-element.284.refs_0_.refs_3_), channel_id=1, source_target_pairs={{0,2},{1,3},{2,0},{3,1},{4,6},{5,7},{6,4},{7,5},{8,10},{9,11},{10,... | collective-permute-start | bytes 3145736 | tf_op jit(solution)/shard_map/ppermute | solution.py:245
  432.7 17.3 %ffn_block_back.3 = (f32[256,2048]{1,0:T(8,128)}, bf16[256,2048]{1,0:T(8,128)(2,1)}, bf16[256,2048]{1,0:T(8,128)(2,1)}) custom-call(bf16[256,2048]{1,0:T(8,128)(2,1)} %copy-done.18, bf16[256,2048]{1,0:T(8,128)(2,1)} %get-tuple-element.240.refs_1_, bf16[256,2048]{1,0:T(8,128)(2,1)} %get-tuple-element.241.refs_2_, ...), custom_call_target="tpu_custom_call" | custom-call | flops 6442450944 | bytes 32505856 | tf_op jit(solution)/shard_map/ffn_block_back/pallas_call | solution.py:537
  450.0 23.6 %collective-permute-done.19.refs_0_.refs_4_ = bf16[256,2048]{1,0:T(8,128)(2,1)} collective-permute-done((bf16[256,2048]{1,0:T(8,128)(2,1)S(1)}, bf16[256,2048]{1,0:T(8,128)(2,1)}, u32[]{:S(2)}, u32[]{:S(2)}) %collective-permute-start.19) | collective-permute-done | bytes 1048608 | tf_op jit(solution)/shard_map/ppermute | solution.py:245
  480.6 24.8 %ffn_block_back.4 = (bf16[256,2048]{1,0:T(8,128)(2,1)}, bf16[256,2048]{1,0:T(8,128)(2,1)}, bf16[512,2048]{1,0:T(8,128)(2,1)}, bf16[512,2048]{1,0:T(8,128)(2,1)}) custom-call(bf16[256,2048]{1,0:T(8,128)(2,1)} %collective-permute-done.19.refs_0_.refs_4_, bf16[256,2048]{1,0:T(8,128)(2,1)} %collective-permute-done.20.refs_1_.refs_5_, ...), custom_call_target="tpu_custom_call" | custom-call | flops 12884901888 | bytes 39845888 | tf_op jit(solution)/shard_map/ffn_block_back/pallas_call | solution.py:537
  512.8 16.7 %ffn_block_back.5 = (bf16[256,2048]{1,0:T(8,128)(2,1)}, bf16[256,2048]{1,0:T(8,128)(2,1)}, bf16[256,2048]{1,0:T(8,128)(2,1)}) custom-call(bf16[256,2048]{1,0:T(8,128)(2,1)} %broadcast_select_fusion.2.refs_0_.refs_6_, bf16[256,2048]{1,0:T(8,128)(2,1)} %get-tuple-element.261.refs_1_, bf16[256,2048]{1,0:T(8,128)(2,1)} %get-tuple-element.262.refs_2_, ...), custom_call_target="tpu_custom_call" | custom-call | flops 6442450944 | bytes 32505856 | tf_op jit(solution)/shard_map/ffn_block_back/pallas_call | solution.py:537
  529.4 22.4 %collective-permute-done.23 = bf16[256,2048]{1,0:T(8,128)(2,1)S(1)} collective-permute-done((bf16[256,2048]{1,0:T(8,128)(2,1)}, bf16[256,2048]{1,0:T(8,128)(2,1)S(1)}, u32[]{:S(2)}, u32[]{:S(2)}) %collective-permute-start.23) | collective-permute-done | bytes 1048608 | tf_op jit(solution)/shard_map/ppermute | solution.py:245
  624.7 14.4 %collective-permute-start.29 = (bf16[256,2688]{1,0:T(8,128)(2,1)S(1)}, bf16[256,2688]{1,0:T(8,128)(2,1)S(1)}, u32[]{:S(2)}, u32[]{:S(2)}) collective-permute-start(bf16[256,2688]{1,0:T(8,128)(2,1)S(1)} %pad_maximum_fusion.2), channel_id=1, source_target_pairs={{0,2},{1,3},{6,4},{7,5},{8,10},{9,11},{14,12},{15,13},{16,18},{17,... | collective-permute-start | bytes 4128776 | tf_op jit(solution)/shard_map/ppermute | solution.py:245
  642.7 10.0 outer_blocks.15
  652.7 26.4 %attend_back.1 = (bf16[256,2048]{1,0:T(8,128)(2,1)}, f32[1280,512]{1,0:T(8,128)}, f32[1280,512]{1,0:T(8,128)}, f32[8,1,256]{2,1,0:T(1,128)}) custom-call(s32[1]{0:T(128)} %bitcast.at_ref, f32[256,2048]{1,0:T(8,128)} %fusion.4.x_ref, bf16[256,2048]{1,0:T(8,128)(2,1)} %get-tuple-element.317.q_ref, f32[256,128]{1,0:T(8,128)} %get-tuple-element.545.c_ref, ...), custom_call_target="tpu_custom_call" | custom-call | flops 6710886400 | bytes 13107200 | tf_op jit(solution)/shard_map/attend_back/pallas_call | solution.py:155
  696.3 9.7 outer_blocks.16.refs_8_
  706.1 9.7 outer_blocks.17
  725.9 12.5 %collective-permute-done.35 = bf16[256,1024]{1,0:T(8,128)(2,1)S(1)} collective-permute-done((bf16[256,1024]{1,0:T(8,128)(2,1)S(1)}, bf16[256,1024]{1,0:T(8,128)(2,1)S(1)}, u32[]{:S(2)}, u32[]{:S(2)}) %collective-permute-start.35) | collective-permute-done | bytes 524320 | tf_op jit(solution)/shard_map/ppermute | solution.py:245
  751.8 52.0 %collective-permute-done.37 = bf16[256,1024]{1,0:T(8,128)(2,1)S(1)} collective-permute-done((bf16[256,1024]{1,0:T(8,128)(2,1)S(1)}, bf16[256,1024]{1,0:T(8,128)(2,1)S(1)}, u32[]{:S(2)}, u32[]{:S(2)}) %collective-permute-start.37) | collective-permute-done | bytes 524320 | tf_op jit(solution)/shard_map/ppermute | solution.py:245
  836.6 18.2 %collective-permute-done.40 = bf16[256,2048]{1,0:T(8,128)(2,1)} collective-permute-done((bf16[256,2048]{1,0:T(8,128)(2,1)}, bf16[256,2048]{1,0:T(8,128)(2,1)}, u32[]{:S(2)}, u32[]{:S(2)}) %collective-permute-start.40) | collective-permute-done | bytes 1048608 | tf_op jit(solution)/shard_map/ppermute | solution.py:245
  872.1 9.4 collective-permute-done.48
  891.0 16.6 %collective-permute-done.44 = bf16[256,2048]{1,0:T(8,128)(2,1)} collective-permute-done((bf16[256,2048]{1,0:T(8,128)(2,1)}, bf16[256,2048]{1,0:T(8,128)(2,1)}, u32[]{:S(2)}, u32[]{:S(2)}) %collective-permute-start.44) | collective-permute-done | bytes 1048608 | tf_op jit(solution)/shard_map/ppermute | solution.py:245
  907.6 12.1 %collective-permute-done.46 = bf16[256,1152]{1,0:T(8,128)(2,1)} collective-permute-done((bf16[256,1152]{1,0:T(8,128)(2,1)S(1)}, bf16[256,1152]{1,0:T(8,128)(2,1)}, u32[]{:S(2)}, u32[]{:S(2)}) %collective-permute-start.46) | collective-permute-done | bytes 589856 | tf_op jit(solution)/shard_map/ppermute | solution.py:245
  950.6 14.0 %collective-permute-done.57 = bf16[64,2688]{1,0:T(8,128)(2,1)S(1)} collective-permute-done((bf16[64,2688]{1,0:T(8,128)(2,1)S(1)}, bf16[64,2688]{1,0:T(8,128)(2,1)S(1)}, u32[]{:S(2)}, u32[]{:S(2)}) %collective-permute-start.57) | collective-permute-done | bytes 344096 | tf_op jit(solution)/shard_map/ppermute | solution.py:241
  978.2 9.4 collective-permute-done.58
  1023.0 11.3 %join_pair.1 = f32[1024,2,2048]{2,1,0:T(2,128)} custom-call(bf16[2048,2048]{1,0:T(8,128)(2,1)} %all-gather.11.cloned.1.call-done.first_ref.second_ref, bf16[2048,2048]{1,0:T(8,128)(2,1)} %all-gather.11.cloned.1.call-done.first_ref.second_ref), custom_call_target="tpu_custom_call" | custom-call | bytes 25165824 | tf_op jit(solution)/shard_map/join_pair/pallas_call | solution.py:627
  (536 shorter events, 421.1 us)
Async XLA Ops:
  7.2 177.6 %all-gather.5.cloned.1.call-start = ((), (), s32[]{:S(2)}) async-start(), calls=%async_computation.2 | async-start | bytes 17842176 | tf_op jit(solution)/shard_map/all_gather | solution.py:680
  18.4 350.5 %all-gather.7.cloned.1.call-start = ((), (), s32[]{:S(2)}) async-start(), calls=%async_computation.3 | async-start | bytes 2162688 | tf_op jit(solution)/shard_map/all_gather | solution.py:680
  18.7 39.1 %collective-permute-start = (bf16[256,1152]{1,0:T(8,128)(2,1)S(1)}, bf16[256,1152]{1,0:T(8,128)(2,1)S(1)}, u32[]{:S(2)}, u32[]{:S(2)}) collective-permute-start(bf16[256,1152]{1,0:T(8,128)(2,1)S(1)} %pad_maximum_fusion.12.shard_ref), channel_id=1, source_target_pairs={{0,2},{1,3},{2,0},{3,1},{4,6},{5,7},{6,4},{7,5},{8,10},{9,11},{10,... | collective-permute-start | bytes 1769480 | tf_op jit(solution)/shard_map/ppermute | solution.py:245
  21.8 40.4 %collective-permute-start.1 = (bf16[256,1152]{1,0:T(8,128)(2,1)S(1)}, bf16[256,1152]{1,0:T(8,128)(2,1)S(1)}, u32[]{:S(2)}, u32[]{:S(2)}) collective-permute-start(bf16[256,1152]{1,0:T(8,128)(2,1)S(1)} %pad_maximum_fusion.12.shard_ref), channel_id=1, source_target_pairs={{0,4},{1,5},{2,6},{3,7},{4,0},{5,1},{6,2},{7,3},{8,12},{9,13},{10,... | collective-permute-start | bytes 1769480 | tf_op jit(solution)/shard_map/ppermute | solution.py:245
  24.4 39.2 %collective-permute-start.4 = (bf16[256,1152]{1,0:T(8,128)(2,1)S(1)}, bf16[256,1152]{1,0:T(8,128)(2,1)S(1)}, u32[]{:S(2)}, u32[]{:S(2)}) collective-permute-start(bf16[256,1152]{1,0:T(8,128)(2,1)S(1)} %pad_maximum_fusion.12.shard_ref), channel_id=1, source_target_pairs={{2,4},{3,5},{4,2},{5,3},{10,12},{11,13},{12,10},{13,11},{18,20},{1... | collective-permute-start | bytes 1769480 | tf_op jit(solution)/shard_map/ppermute | solution.py:245
  100.6 97.1 %collective-permute-start.10 = (bf16[1024,2048]{1,0:T(8,128)(2,1)}, bf16[1024,2048]{1,0:T(8,128)(2,1)}, u32[]{:S(2)}, u32[]{:S(2)}) collective-permute-start(bf16[1024,2048]{1,0:T(8,128)(2,1)} %convert_element_type.481.refs_5_.refs_6_.refs_7_.refs_8_), channel_id=1, source_target_pairs={{0,1},{1,0},{2,3},{3,2},{4,5},{5,4},{6,7},{7,6},{8,9},{9,8},{10,11... | collective-permute-start | bytes 12582920 | tf_op jit(solution)/shard_map/ppermute | solution.py:238
  100.9 96.8 %collective-permute-start.8 = (bf16[1024,2048]{1,0:T(8,128)(2,1)}, bf16[1024,2048]{1,0:T(8,128)(2,1)}, u32[]{:S(2)}, u32[]{:S(2)}) collective-permute-start(bf16[1024,2048]{1,0:T(8,128)(2,1)} %get-tuple-element.212.refs_1_.refs_2_.refs_3_.refs_4_), channel_id=1, source_target_pairs={{0,1},{1,0},{2,3},{3,2},{4,5},{5,4},{6,7},{7,6},{8,9},{9,8},{10,11... | collective-permute-start | bytes 12582920 | tf_op jit(solution)/shard_map/ppermute | solution.py:238
  101.1 96.6 %collective-permute-start.9 = (bf16[1024,2048]{1,0:T(8,128)(2,1)}, bf16[1024,2048]{1,0:T(8,128)(2,1)}, u32[]{:S(2)}, u32[]{:S(2)}) collective-permute-start(bf16[1024,2048]{1,0:T(8,128)(2,1)} %get-tuple-element.214.refs_3_.refs_4_.refs_5_.refs_6_), channel_id=1, source_target_pairs={{0,1},{1,0},{2,3},{3,2},{4,5},{5,4},{6,7},{7,6},{8,9},{9,8},{10,11... | collective-permute-start | bytes 12582920 | tf_op jit(solution)/shard_map/ppermute | solution.py:238
  201.0 538.7 %reduce-scatter.3.cloned.1.call-start = ((), (), s32[]{:S(2)}) async-start(), calls=%async_computation.4 | async-start | bytes 5242880 | tf_op jit(solution)/shard_map/reduce_scatter | solution.py:915
  234.7 54.7 %collective-permute-start.12 = (bf16[256,2048]{1,0:T(8,128)(2,1)S(1)}, bf16[256,2048]{1,0:T(8,128)(2,1)}, u32[]{:S(2)}, u32[]{:S(2)}) collective-permute-start(bf16[256,2048]{1,0:T(8,128)(2,1)S(1)} %multiply_convert_fusion.refs_0_.refs_3_), channel_id=1, source_target_pairs={{0,2},{1,3},{2,0},{3,1},{4,6},{5,7},{6,4},{7,5},{8,10},{9,11},{10,... | collective-permute-start | bytes 3145736 | tf_op jit(solution)/shard_map/ppermute | solution.py:245
  236.5 57.8 %collective-permute-start.13 = (bf16[256,2048]{1,0:T(8,128)(2,1)S(1)}, bf16[256,2048]{1,0:T(8,128)(2,1)}, u32[]{:S(2)}, u32[]{:S(2)}) collective-permute-start(bf16[256,2048]{1,0:T(8,128)(2,1)S(1)} %multiply_convert_fusion.refs_0_.refs_3_), channel_id=1, source_target_pairs={{0,4},{1,5},{2,6},{3,7},{4,0},{5,1},{6,2},{7,3},{8,12},{9,13},{10,... | collective-permute-start | bytes 3145736 | tf_op jit(solution)/shard_map/ppermute | solution.py:245
  243.5 73.9 %collective-permute-start.15 = (bf16[256,2048]{1,0:T(8,128)(2,1)S(1)}, bf16[256,2048]{1,0:T(8,128)(2,1)}, u32[]{:S(2)}, u32[]{:S(2)}) collective-permute-start(bf16[256,2048]{1,0:T(8,128)(2,1)S(1)} %multiply_convert_fusion.refs_0_.refs_3_), channel_id=1, source_target_pairs={{2,4},{3,5},{4,2},{5,3},{10,12},{11,13},{12,10},{13,11},{18,20},{1... | collective-permute-start | bytes 3145736 | tf_op jit(solution)/shard_map/ppermute | solution.py:245
  321.5 45.2 %collective-permute-start.16 = (bf16[256,2048]{1,0:T(8,128)(2,1)}, bf16[256,2048]{1,0:T(8,128)(2,1)S(1)}, u32[]{:S(2)}, u32[]{:S(2)}) collective-permute-start(bf16[256,2048]{1,0:T(8,128)(2,1)} %get-tuple-element.230), channel_id=1, source_target_pairs={{0,2},{1,3},{2,0},{3,1},{4,6},{5,7},{6,4},{7,5},{8,10},{9,11},{10,... | collective-permute-start | bytes 3145736 | tf_op jit(solution)/shard_map/ppermute | solution.py:245
  323.3 49.5 %collective-permute-start.17 = (bf16[256,2048]{1,0:T(8,128)(2,1)}, bf16[256,2048]{1,0:T(8,128)(2,1)}, u32[]{:S(2)}, u32[]{:S(2)}) collective-permute-start(bf16[256,2048]{1,0:T(8,128)(2,1)} %get-tuple-element.237), channel_id=1, source_target_pairs={{0,4},{1,5},{2,6},{3,7},{4,0},{5,1},{6,2},{7,3},{8,12},{9,13},{10,... | collective-permute-start | bytes 3145736 | tf_op jit(solution)/shard_map/ppermute | solution.py:245
  406.8 66.8 %collective-permute-start.19 = (bf16[256,2048]{1,0:T(8,128)(2,1)S(1)}, bf16[256,2048]{1,0:T(8,128)(2,1)}, u32[]{:S(2)}, u32[]{:S(2)}) collective-permute-start(bf16[256,2048]{1,0:T(8,128)(2,1)S(1)} %get-tuple-element.284.refs_0_.refs_3_), channel_id=1, source_target_pairs={{0,2},{1,3},{2,0},{3,1},{4,6},{5,7},{6,4},{7,5},{8,10},{9,11},{10,... | collective-permute-start | bytes 3145736 | tf_op jit(solution)/shard_map/ppermute | solution.py:245
  429.7 49.5 %collective-permute-start.20 = (bf16[256,2048]{1,0:T(8,128)(2,1)S(1)}, bf16[256,2048]{1,0:T(8,128)(2,1)}, u32[]{:S(2)}, u32[]{:S(2)}) collective-permute-start(bf16[256,2048]{1,0:T(8,128)(2,1)S(1)} %get-tuple-element.284.refs_0_.refs_3_), channel_id=1, source_target_pairs={{0,4},{1,5},{2,6},{3,7},{4,0},{5,1},{6,2},{7,3},{8,12},{9,13},{10,... | collective-permute-start | bytes 3145736 | tf_op jit(solution)/shard_map/ppermute | solution.py:245
  431.0 74.3 %collective-permute-start.22 = (bf16[256,2048]{1,0:T(8,128)(2,1)S(1)}, bf16[256,2048]{1,0:T(8,128)(2,1)}, u32[]{:S(2)}, u32[]{:S(2)}) collective-permute-start(bf16[256,2048]{1,0:T(8,128)(2,1)S(1)} %get-tuple-element.284.refs_0_.refs_3_), channel_id=1, source_target_pairs={{2,4},{3,5},{4,2},{5,3},{10,12},{11,13},{12,10},{13,11},{18,20},{1... | collective-permute-start | bytes 3145736 | tf_op jit(solution)/shard_map/ppermute | solution.py:245
  507.7 44.1 %collective-permute-start.23 = (bf16[256,2048]{1,0:T(8,128)(2,1)}, bf16[256,2048]{1,0:T(8,128)(2,1)S(1)}, u32[]{:S(2)}, u32[]{:S(2)}) collective-permute-start(bf16[256,2048]{1,0:T(8,128)(2,1)} %get-tuple-element.259), channel_id=1, source_target_pairs={{0,2},{1,3},{2,0},{3,1},{4,6},{5,7},{6,4},{7,5},{8,10},{9,11},{10,... | collective-permute-start | bytes 3145736 | tf_op jit(solution)/shard_map/ppermute | solution.py:245
  511.4 78.5 %collective-permute-start.24 = (bf16[256,2048]{1,0:T(8,128)(2,1)}, bf16[256,2048]{1,0:T(8,128)(2,1)}, u32[]{:S(2)}, u32[]{:S(2)}) collective-permute-start(bf16[256,2048]{1,0:T(8,128)(2,1)} %get-tuple-element.269), channel_id=1, source_target_pairs={{0,4},{1,5},{2,6},{3,7},{4,0},{5,1},{6,2},{7,3},{8,12},{9,13},{10,... | collective-permute-start | bytes 3145736 | tf_op jit(solution)/shard_map/ppermute | solution.py:245
  617.1 62.0 %collective-permute-start.30 = (bf16[1024,2048]{1,0:T(8,128)(2,1)}, bf16[1024,2048]{1,0:T(8,128)(2,1)}, u32[]{:S(2)}, u32[]{:S(2)}) collective-permute-start(bf16[1024,2048]{1,0:T(8,128)(2,1)} %outer_blocks.11), channel_id=1, source_target_pairs={{0,1},{1,0},{2,3},{3,2},{4,5},{5,4},{6,7},{7,6},{8,9},{9,8},{10,11... | collective-permute-start | bytes 12582920 | tf_op jit(solution)/shard_map/ppermute | solution.py:238
  617.3 61.8 %collective-permute-start.31 = (bf16[1024,2048]{1,0:T(8,128)(2,1)}, bf16[1024,2048]{1,0:T(8,128)(2,1)}, u32[]{:S(2)}, u32[]{:S(2)}) collective-permute-start(bf16[1024,2048]{1,0:T(8,128)(2,1)} %outer_blocks.12), channel_id=1, source_target_pairs={{0,1},{1,0},{2,3},{3,2},{4,5},{5,4},{6,7},{7,6},{8,9},{9,8},{10,11... | collective-permute-start | bytes 12582920 | tf_op jit(solution)/shard_map/ppermute | solution.py:238
  624.7 54.3 %collective-permute-start.29 = (bf16[256,2688]{1,0:T(8,128)(2,1)S(1)}, bf16[256,2688]{1,0:T(8,128)(2,1)S(1)}, u32[]{:S(2)}, u32[]{:S(2)}) collective-permute-start(bf16[256,2688]{1,0:T(8,128)(2,1)S(1)} %pad_maximum_fusion.2), channel_id=1, source_target_pairs={{0,2},{1,3},{6,4},{7,5},{8,10},{9,11},{14,12},{15,13},{16,18},{17,... | collective-permute-start | bytes 4128776 | tf_op jit(solution)/shard_map/ppermute | solution.py:245
  680.1 174.6 %reduce-scatter.5.cloned.1.call-start = ((), (), s32[]{:S(2)}) async-start(), calls=%async_computation.5 | async-start | bytes 10485760 | tf_op jit(solution)/shard_map/reduce_scatter | solution.py:950
  680.1 40.0 %collective-permute-start.33 = (bf16[256,2688]{1,0:T(8,128)(2,1)}, bf16[256,2688]{1,0:T(8,128)(2,1)S(1)}, u32[]{:S(2)}, u32[]{:S(2)}) collective-permute-start(bf16[256,2688]{1,0:T(8,128)(2,1)} %pad_maximum_fusion.4), channel_id=1, source_target_pairs={{0,2},{1,3},{2,0},{3,1},{4,6},{5,7},{6,4},{7,5},{8,10},{9,11},{10,... | collective-permute-start | bytes 4128776 | tf_op jit(solution)/shard_map/ppermute | solution.py:245
  680.1 40.0 %collective-permute-start.34 = (bf16[256,2688]{1,0:T(8,128)(2,1)}, bf16[256,2688]{1,0:T(8,128)(2,1)S(1)}, u32[]{:S(2)}, u32[]{:S(2)}) collective-permute-start(bf16[256,2688]{1,0:T(8,128)(2,1)} %copy-done.45), channel_id=1, source_target_pairs={{2,4},{3,5},{4,2},{5,3},{10,12},{11,13},{12,10},{13,11},{18,20},{1... | collective-permute-start | bytes 4128776 | tf_op jit(solution)/shard_map/ppermute | solution.py:245
  721.7 169.3 %all-gather.9.cloned.1.call-start = ((), (), s32[]{:S(2)}) async-start(), calls=%async_computation.6 | async-start | bytes 5242880 | tf_op jit(solution)/shard_map/all_gather | solution.py:965
  739.8 283.2 %all-gather.11.cloned.1.call-start = ((), (), s32[]{:S(2)}) async-start(), calls=%async_computation.7 | async-start | bytes 10485760 | tf_op jit(solution)/shard_map/all_gather | solution.py:996
  745.2 58.6 %collective-permute-start.37 = (bf16[256,1024]{1,0:T(8,128)(2,1)S(1)}, bf16[256,1024]{1,0:T(8,128)(2,1)S(1)}, u32[]{:S(2)}, u32[]{:S(2)}) collective-permute-start(bf16[256,1024]{1,0:T(8,128)(2,1)S(1)} %convert_element_type.555), channel_id=1, source_target_pairs={{4,0},{5,1},{6,2},{7,3},{12,8},{13,9},{14,10},{15,11},{20,16},{21,... | collective-permute-start | bytes 1572872 | tf_op jit(solution)/shard_map/ppermute | solution.py:245
  748.2 88.3 %collective-permute-start.36 = (bf16[256,2688]{1,0:T(8,128)(2,1)}, bf16[256,2688]{1,0:T(8,128)(2,1)}, u32[]{:S(2)}, u32[]{:S(2)}) collective-permute-start(bf16[256,2688]{1,0:T(8,128)(2,1)} %add_convert_fusion.1), channel_id=1, source_target_pairs={{0,4},{1,5},{2,6},{3,7},{4,0},{5,1},{6,2},{7,3},{8,12},{9,13},{10,... | collective-permute-start | bytes 4128776 | tf_op jit(solution)/shard_map/ppermute | solution.py:245
  809.9 44.9 %collective-permute-start.41 = (bf16[256,2048]{1,0:T(8,128)(2,1)}, bf16[256,2048]{1,0:T(8,128)(2,1)}, u32[]{:S(2)}, u32[]{:S(2)}) collective-permute-start(bf16[256,2048]{1,0:T(8,128)(2,1)} %get-tuple-element.460), channel_id=1, source_target_pairs={{2,4},{3,5},{4,2},{5,3},{10,12},{11,13},{12,10},{13,11},{18,20},{1... | collective-permute-start | bytes 3145736 | tf_op jit(solution)/shard_map/ppermute | solution.py:245
  858.7 48.9 %collective-permute-start.44 = (bf16[256,2048]{1,0:T(8,128)(2,1)}, bf16[256,2048]{1,0:T(8,128)(2,1)}, u32[]{:S(2)}, u32[]{:S(2)}) collective-permute-start(bf16[256,2048]{1,0:T(8,128)(2,1)} %add_convert_fusion.4), channel_id=1, source_target_pairs={{0,4},{1,5},{2,6},{3,7},{4,0},{5,1},{6,2},{7,3},{8,12},{9,13},{10,... | collective-permute-start | bytes 3145736 | tf_op jit(solution)/shard_map/ppermute | solution.py:245
  869.5 50.2 %collective-permute-start.45 = (bf16[256,1152]{1,0:T(8,128)(2,1)S(1)}, bf16[256,1152]{1,0:T(8,128)(2,1)S(1)}, u32[]{:S(2)}, u32[]{:S(2)}) collective-permute-start(bf16[256,1152]{1,0:T(8,128)(2,1)S(1)} %pad_maximum_fusion.13), channel_id=1, source_target_pairs={{0,2},{1,3},{6,4},{7,5},{8,10},{9,11},{14,12},{15,13},{16,18},{17,... | collective-permute-start | bytes 1769480 | tf_op jit(solution)/shard_map/ppermute | solution.py:245
  (137 other events, 1873.4 us)
Sparse Core Ops, SparseCore 0:
  18.5 144.2 all-gather.4
  201.1 95.2 all-gather.6
  679.2 51.5 reduce-scatter.2
  734.6 86.3 reduce-scatter.4
  822.7 61.8 all-gather.8
  886.3 130.5 all-gather.10

commit v5 on v4

--- a/solution.py
+++ b/solution.py
@@ -950,7 +950,7 @@
     wide_part = lax.psum_scatter(wide_w, "rep", scatter_dimension=0, tiled=True)
     if at.four:
         pair_sum = kv_parts[0] + at.chip_swap(kv_parts[1].astype(BF), 1).astype(F32)
-        pair_sum, out_near, down_part = tie(pair_sum, out_near, down_part)
+        pair_sum, out_near = tie(pair_sum, out_near)
         prompt_parts = [at.chip_send(pair_sum.astype(BF), [(2, 0), (3, 1)])]
     else:
         pair_sum = kv_parts[0]
@@ -962,8 +962,10 @@
         ]
     q_leaving = at.core_swap(q_other_w)
     out_far = at.collect_far(out_parts, out_near)
-    down_sum = lax.all_gather(down_part, "rep", axis=0, tiled=True)
-    prompt_parts, pair_sum, q_leaving = tie(prompt_parts, pair_sum, q_leaving)
+    prompt_parts, pair_sum, q_leaving, wide_part = tie(
+        prompt_parts, pair_sum, q_leaving, wide_part
+    )
+    wide_sum = lax.all_gather(wide_part, "rep", axis=0, tiled=True)
     q_parts = at.lane_parts([q_mine], [q_leaving])
     q_near = at.collect_near(q_parts)
     prompt_sum = pair_sum
@@ -990,10 +992,10 @@
     gain_pack = jnp.concatenate([by_owner(gain_total), by_owner(qk_total)], axis=1).astype(BF)
     gain_pack = jnp.pad(gain_pack, ((0, 0), (0, shard * 128 - gain_pack.shape[1])))
     gain_mine, gain_leaving = at.lanes(gain_pack.reshape(-1, 128))
-    out_far, q_near, kv_other_w, kv_mine, gain_mine, gain_leaving, grad_tokens, wide_part = tie(
-        out_far, q_near, kv_other_w, kv_mine, gain_mine, gain_leaving, grad_tokens, wide_part
-    )
-    wide_sum = lax.all_gather(wide_part, "rep", axis=0, tiled=True)
+    out_far, q_near, kv_other_w, kv_mine, gain_mine, gain_leaving, grad_tokens, down_part = tie(
+        out_far, q_near, kv_other_w, kv_mine, gain_mine, gain_leaving, grad_tokens, down_part
+    )
+    down_sum = lax.all_gather(down_part, "rep", axis=0, tiled=True)
     out_ready = at.collect_sum(out_parts[0], out_far).astype(BF)
     q_far = at.collect_far(q_parts, q_near)
     kv_leaving, gain_leaving, out_ready = tie(
@@ -1002,14 +1004,14 @@
     kv_w_parts = at.lane_parts([kv_mine, gain_mine], [kv_leaving, gain_leaving])
     kv_near = at.collect_near(kv_w_parts)
     out_total = at.copies_sum(out_ready)
-    q_far, kv_near, out_total, down_sum = tie(q_far, kv_near, out_total, down_sum)
+    q_far, kv_near, out_total = tie(q_far, kv_near, out_total)
     kv_far = at.collect_far(kv_w_parts, kv_near)
     q_total = at.copies_sum(at.collect_sum(q_parts[0], q_far))
     out_sum = at.copies_all(out_total)
-    kv_far, q_total, out_sum, down_sum = tie(kv_far, q_total, out_sum, down_sum)
+    kv_far, q_total, out_sum = tie(kv_far, q_total, out_sum)
     kv_total = at.copies_sum(at.collect_sum(kv_w_parts[0], kv_far))
     q_sum = at.copies_all(q_total)
-    kv_total, q_sum, down_sum = tie(kv_total, q_sum, down_sum)
+    kv_total, q_sum = tie(kv_total, q_sum)
     grad_gate_up, grad_down = join_pair(wide_sum, units), down_sum.astype(F32)
     kv_sum_w = at.copies_all(kv_total)
     gain_out = kv_sum_w[:, 2 * KVH * HD :].reshape(-1)

time: 1050 us -> 1080 us (1.029)
  waiting for transfers between devices: 400 us -> 422 us
    ppermute x34, waiting for transfers between devices: 321 us -> 297 us  [chip_send(): return lax.ppermute(array, 'fsdp', pairs)]
    all_gather x1, waiting for transfers between devices: 0.01 us -> 22 us  [body(): wide_sum = lax.all_gather(wide_part, 'rep', axis=0, tiled=True)]
    reduce_scatter x1, waiting for transfers between devices: 0.02 us -> 20 us  [body(): down_part = lax.psum_scatter(down_w, 'rep', scatter_dimension=0, tiled=True)]
    reduce_scatter x1, waiting for transfers between devices: 0.01 us -> 11.6 us  [body(): wide_part = lax.psum_scatter(wide_w, 'rep', scatter_dimension=0, tiled=True)]
  transfers between devices with their start and end apart: 73 -> 73, of which waited for: 35 -> 35; matrix products, arithmetic and copies ran while one was open for 16% -> 15% of each run, Pallas kernels for 25% -> 24%
where the time goes in v5:
time: 1080 us; the launch traced here: 1070 us
  waiting for transfers between devices  422 us (39%)
  Pallas kernels  268 us (25%)
  starting transfers between devices  158 us (15%)
  other arithmetic  104 us (10%)
  matrix products  52.6 us (5%)
  local copies, waits for them, and re-layouts  49.7 us (5%)
  between operations  16.3 us (2%)
    ppermute x34, waiting for transfers between devices, chip_send(): return lax.ppermute(array, 'fsdp', pairs)  297 us
    ppermute x34, starting transfers between devices, chip_send(): return lax.ppermute(array, 'fsdp', pairs)  132 us
    pallas_call x10, Pallas kernels, outer_blocks(): pl.pallas_call(kernel, grid=(tiles,), in_specs=specs, out_specs=pl.BlockS...  74.7 us
    ppermute x18, waiting for transfers between devices, copy_swap(): lax.ppermute(array, 'rep', [(i, i ^ mask) for i in range(self.copies)])  67 us
    pallas_call x3, Pallas kernels, ffn_block_back(): pl.pallas_call(kernel, grid=(2 * tiles,), in_specs=[whole] * count + [par...  58.7 us
    pallas_call x3, Pallas kernels, ffn_block(): pl.pallas_call(kernel, grid=(2 * tiles,), in_specs=[whole] * count + half...  53.4 us
    pallas_call x1, Pallas kernels, attend_back(): pl.pallas_call(kernel, grid=(H,), in_specs=[pl.BlockSpec(memory_space=plt...  26.2 us
    ppermute x18, starting transfers between devices, copy_swap(): lax.ppermute(array, 'rep', [(i, i ^ mask) for i in range(self.copies)])  22.1 us
  transfers between devices with their start and end apart: 73, of which 35 were waited for; matrix products, arithmetic and copies ran while one was open for 15% of the time, Pallas kernels for 24%

profile of v5, /device:TPU:0, one launch (start us, length us, event | category | flops | bytes accessed | tf_op | source)
XLA Modules:
  0.0 1070.1 jit_solution(4536687507549719172)
XLA Ops:
  25.1 19.0 %split_pair.1 = (bf16[1024,2048]{1,0:T(8,128)(2,1)}, bf16[1024,2048]{1,0:T(8,128)(2,1)}) custom-call(f32[1024,2,2048]{2,1,0:T(2,128)} %pair_ref.1), custom_call_target="tpu_custom_call" | custom-call | bytes 25165824 | tf_op jit(solution)/shard_map/split_pair/pallas_call | solution.py:605
  63.6 32.9 %collective-permute-done.3 = bf16[256,1152]{1,0:T(8,128)(2,1)S(1)} collective-permute-done((bf16[256,1152]{1,0:T(8,128)(2,1)S(1)}, bf16[256,1152]{1,0:T(8,128)(2,1)S(1)}, u32[]{:S(2)}, u32[]{:S(2)}) %collective-permute-start.3) | collective-permute-done | bytes 589856 | tf_op jit(solution)/shard_map/ppermute | solution.py:245
  119.5 23.7 %collective-permute-done.6 = bf16[256,1024]{1,0:T(8,128)(2,1)S(1)} collective-permute-done((bf16[256,1024]{1,0:T(8,128)(2,1)}, bf16[256,1024]{1,0:T(8,128)(2,1)S(1)}, u32[]{:S(2)}, u32[]{:S(2)}) %collective-permute-start.6) | collective-permute-done | bytes 524320 | tf_op jit(solution)/shard_map/ppermute | solution.py:245
  144.3 26.7 %collective-permute-start.7 = (bf16[256,1024]{1,0:T(8,128)(2,1)S(1)}, bf16[256,1024]{1,0:T(8,128)(2,1)}, u32[]{:S(2)}, u32[]{:S(2)}) collective-permute-start(bf16[256,1024]{1,0:T(8,128)(2,1)S(1)} %broadcast_select_fusion.6), channel_id=1, source_target_pairs={{0,2},{1,3},{2,0},{3,1},{4,6},{5,7},{6,4},{7,5},{8,10},{9,11},{10,... | collective-permute-start | bytes 1572872 | tf_op jit(solution)/shard_map/ppermute | solution.py:245
  171.0 11.5 %collective-permute-done.7 = bf16[256,1024]{1,0:T(8,128)(2,1)} collective-permute-done((bf16[256,1024]{1,0:T(8,128)(2,1)S(1)}, bf16[256,1024]{1,0:T(8,128)(2,1)}, u32[]{:S(2)}, u32[]{:S(2)}) %collective-permute-start.7) | collective-permute-done | bytes 524320 | tf_op jit(solution)/shard_map/ppermute | solution.py:245
  213.3 12.9 %attend.1 = (bf16[256,2048]{1,0:T(8,128)(2,1)}, bf16[256,2048]{1,0:T(8,128)(2,1)}) custom-call(s32[1]{0:T(128)} %bitcast.at_ref, f32[256,2048]{1,0:T(8,128)} %fusion.4.x_ref, f32[256,128]{1,0:T(8,128)} %get-tuple-element.539.c_ref, f32[256,128]{1,0:T(8,128)} %get-tuple-element.538.s_ref, f32[2,256]{1,0:T(2,128)} %reshape.435.g_ref, ...), custom_call_target="tpu_custom_call" | custom-call | flops 2684354560 | bytes 6815744 | tf_op jit(solution)/shard_map/attend/pallas_call | solution.py:104
  245.1 16.3 %ffn_block.3 = (f32[256,2048]{1,0:T(8,128)}, bf16[256,2048]{1,0:T(8,128)(2,1)}, bf16[256,2048]{1,0:T(8,128)(2,1)}, bf16[256,2048]{1,0:T(8,128)(2,1)}) custom-call(bf16[256,2048]{1,0:T(8,128)(2,1)} %copy-done.9, bf16[1024,2048]{1,0:T(8,128)(2,1)} %get-tuple-element.209.refs_1_.refs_2_.refs_3_.refs_4_, ...), custom_call_target="tpu_custom_call" | custom-call | flops 6442450944 | bytes 31457280 | tf_op jit(solution)/shard_map/ffn_block/pallas_call | solution.py:477
  264.0 25.4 %collective-permute-done.12.refs_0_.refs_4_ = bf16[256,2048]{1,0:T(8,128)(2,1)} collective-permute-done((bf16[256,2048]{1,0:T(8,128)(2,1)S(1)}, bf16[256,2048]{1,0:T(8,128)(2,1)}, u32[]{:S(2)}, u32[]{:S(2)}) %collective-permute-start.12) | collective-permute-done | bytes 1048608 | tf_op jit(solution)/shard_map/ppermute | solution.py:245
  296.0 21.4 %ffn_block.4 = (bf16[256,2048]{1,0:T(8,128)(2,1)}, bf16[256,2048]{1,0:T(8,128)(2,1)}, bf16[512,2048]{1,0:T(8,128)(2,1)}, bf16[512,2048]{1,0:T(8,128)(2,1)}, bf16[512,2048]{1,0:T(8,128)(2,1)}) custom-call(bf16[256,2048]{1,0:T(8,128)(2,1)} %collective-permute-done.12.refs_0_.refs_4_, bf16[256,2048]{1,0:T(8,128)(2,1)} %collective-permute-done.13.refs_1_.refs_5_, ...), custom_call_target="tpu_custom_call" | custom-call | flops 12884901888 | bytes 37748736 | tf_op jit(solution)/shard_map/ffn_block/pallas_call | solution.py:477
  326.5 15.7 %ffn_block.5 = (bf16[256,2048]{1,0:T(8,128)(2,1)}, bf16[256,2048]{1,0:T(8,128)(2,1)}, bf16[256,2048]{1,0:T(8,128)(2,1)}, bf16[256,2048]{1,0:T(8,128)(2,1)}) custom-call(bf16[256,2048]{1,0:T(8,128)(2,1)} %broadcast_select_fusion.3.refs_0_.refs_6_, bf16[1024,2048]{1,0:T(8,128)(2,1)} %get-tuple-element.209.refs_1_.refs_2_.refs_3_.refs_4_, ...), custom_call_target="tpu_custom_call" | custom-call | flops 6442450944 | bytes 31457280 | tf_op jit(solution)/shard_map/ffn_block/pallas_call | solution.py:477
  342.2 24.6 %collective-permute-done.16 = bf16[256,2048]{1,0:T(8,128)(2,1)S(1)} collective-permute-done((bf16[256,2048]{1,0:T(8,128)(2,1)}, bf16[256,2048]{1,0:T(8,128)(2,1)S(1)}, u32[]{:S(2)}, u32[]{:S(2)}) %collective-permute-start.16) | collective-permute-done | bytes 1048608 | tf_op jit(solution)/shard_map/ppermute | solution.py:245
  372.9 20.7 %collective-permute-done.18 = bf16[256,2048]{1,0:T(8,128)(2,1)} collective-permute-done((bf16[256,2048]{1,0:T(8,128)(2,1)}, bf16[256,2048]{1,0:T(8,128)(2,1)}, u32[]{:S(2)}, u32[]{:S(2)}) %collective-permute-start.18) | collective-permute-done | bytes 1048608 | tf_op jit(solution)/shard_map/ppermute | solution.py:245
  406.9 22.9 %collective-permute-start.19 = (bf16[256,2048]{1,0:T(8,128)(2,1)S(1)}, bf16[256,2048]{1,0:T(8,128)(2,1)}, u32[]{:S(2)}, u32[]{:S(2)}) collective-permute-start(bf16[256,2048]{1,0:T(8,128)(2,1)S(1)} %get-tuple-element.281.refs_0_.refs_3_), channel_id=1, source_target_pairs={{0,2},{1,3},{2,0},{3,1},{4,6},{5,7},{6,4},{7,5},{8,10},{9,11},{10,... | collective-permute-start | bytes 3145736 | tf_op jit(solution)/shard_map/ppermute | solution.py:245
  432.8 17.3 %ffn_block_back.3 = (f32[256,2048]{1,0:T(8,128)}, bf16[256,2048]{1,0:T(8,128)(2,1)}, bf16[256,2048]{1,0:T(8,128)(2,1)}) custom-call(bf16[256,2048]{1,0:T(8,128)(2,1)} %copy-done.17, bf16[256,2048]{1,0:T(8,128)(2,1)} %get-tuple-element.237.refs_1_, bf16[256,2048]{1,0:T(8,128)(2,1)} %get-tuple-element.238.refs_2_, ...), custom_call_target="tpu_custom_call" | custom-call | flops 6442450944 | bytes 32505856 | tf_op jit(solution)/shard_map/ffn_block_back/pallas_call | solution.py:537
  450.0 23.7 %collective-permute-done.19.refs_0_.refs_4_ = bf16[256,2048]{1,0:T(8,128)(2,1)} collective-permute-done((bf16[256,2048]{1,0:T(8,128)(2,1)S(1)}, bf16[256,2048]{1,0:T(8,128)(2,1)}, u32[]{:S(2)}, u32[]{:S(2)}) %collective-permute-start.19) | collective-permute-done | bytes 1048608 | tf_op jit(solution)/shard_map/ppermute | solution.py:245
  480.7 24.7 %ffn_block_back.4 = (bf16[256,2048]{1,0:T(8,128)(2,1)}, bf16[256,2048]{1,0:T(8,128)(2,1)}, bf16[512,2048]{1,0:T(8,128)(2,1)}, bf16[512,2048]{1,0:T(8,128)(2,1)}) custom-call(bf16[256,2048]{1,0:T(8,128)(2,1)} %collective-permute-done.19.refs_0_.refs_4_, bf16[256,2048]{1,0:T(8,128)(2,1)} %collective-permute-done.20.refs_1_.refs_5_, ...), custom_call_target="tpu_custom_call" | custom-call | flops 12884901888 | bytes 39845888 | tf_op jit(solution)/shard_map/ffn_block_back/pallas_call | solution.py:537
  512.8 16.7 %ffn_block_back.5 = (bf16[256,2048]{1,0:T(8,128)(2,1)}, bf16[256,2048]{1,0:T(8,128)(2,1)}, bf16[256,2048]{1,0:T(8,128)(2,1)}) custom-call(bf16[256,2048]{1,0:T(8,128)(2,1)} %broadcast_select_fusion.2.refs_0_.refs_6_, bf16[256,2048]{1,0:T(8,128)(2,1)} %get-tuple-element.258.refs_1_, bf16[256,2048]{1,0:T(8,128)(2,1)} %get-tuple-element.259.refs_2_, ...), custom_call_target="tpu_custom_call" | custom-call | flops 6442450944 | bytes 32505856 | tf_op jit(solution)/shard_map/ffn_block_back/pallas_call | solution.py:537
  529.5 22.3 %collective-permute-done.23 = bf16[256,2048]{1,0:T(8,128)(2,1)S(1)} collective-permute-done((bf16[256,2048]{1,0:T(8,128)(2,1)}, bf16[256,2048]{1,0:T(8,128)(2,1)S(1)}, u32[]{:S(2)}, u32[]{:S(2)}) %collective-permute-start.23) | collective-permute-done | bytes 1048608 | tf_op jit(solution)/shard_map/ppermute | solution.py:245
  625.8 14.4 %collective-permute-start.29 = (bf16[256,2688]{1,0:T(8,128)(2,1)}, bf16[256,2688]{1,0:T(8,128)(2,1)S(1)}, u32[]{:S(2)}, u32[]{:S(2)}) collective-permute-start(bf16[256,2688]{1,0:T(8,128)(2,1)} %pad_maximum_fusion.2), channel_id=1, source_target_pairs={{0,2},{1,3},{6,4},{7,5},{8,10},{9,11},{14,12},{15,13},{16,18},{17,... | collective-permute-start | bytes 4128776 | tf_op jit(solution)/shard_map/ppermute | solution.py:245
  643.8 10.0 outer_blocks.15
  653.8 26.2 %attend_back.1 = (bf16[256,2048]{1,0:T(8,128)(2,1)}, f32[1280,512]{1,0:T(8,128)}, f32[1280,512]{1,0:T(8,128)}, f32[8,1,256]{2,1,0:T(1,128)}) custom-call(s32[1]{0:T(128)} %bitcast.at_ref, f32[256,2048]{1,0:T(8,128)} %fusion.4.x_ref, bf16[256,2048]{1,0:T(8,128)(2,1)} %get-tuple-element.314.q_ref, f32[256,128]{1,0:T(8,128)} %get-tuple-element.539.c_ref, ...), custom_call_target="tpu_custom_call" | custom-call | flops 6710886400 | bytes 13107200 | tf_op jit(solution)/shard_map/attend_back/pallas_call | solution.py:155
  696.8 9.6 outer_blocks.16.refs_8_
  706.4 9.6 outer_blocks.17
  746.8 51.8 %collective-permute-done.37 = bf16[256,1024]{1,0:T(8,128)(2,1)S(1)} collective-permute-done((bf16[256,1024]{1,0:T(8,128)(2,1)S(1)}, bf16[256,1024]{1,0:T(8,128)(2,1)S(1)}, u32[]{:S(2)}, u32[]{:S(2)}) %collective-permute-start.37) | collective-permute-done | bytes 524320 | tf_op jit(solution)/shard_map/ppermute | solution.py:245
  799.5 11.6 %reduce-scatter.3.cloned.1.call-done = bf16[512,2048]{1,0:T(8,128)(2,1)} async-done(((bf16[2048,2048]{1,0:T(8,128)(2,1)}), bf16[512,2048]{1,0:T(8,128)(2,1)}) %reduce-scatter.3.cloned.1.call-update) | async-done | bytes 2097168 | tf_op jit(solution)/shard_map/reduce_scatter | solution.py:950
  846.9 20.0 %reduce-scatter.5.cloned.1.call-done = bf16[256,2048]{1,0:T(8,128)(2,1)} async-done(((bf16[1024,2048]{1,0:T(8,128)(2,1)}), bf16[256,2048]{1,0:T(8,128)(2,1)}) %reduce-scatter.5.cloned.1.call-update) | async-done | bytes 1048592 | tf_op jit(solution)/shard_map/reduce_scatter | solution.py:915
  883.2 9.6 collective-permute-done.48
  905.0 14.7 %collective-permute-done.44 = bf16[256,2048]{1,0:T(8,128)(2,1)S(1)} collective-permute-done((bf16[256,2048]{1,0:T(8,128)(2,1)S(1)}, bf16[256,2048]{1,0:T(8,128)(2,1)S(1)}, u32[]{:S(2)}, u32[]{:S(2)}) %collective-permute-start.44) | collective-permute-done | bytes 1048608 | tf_op jit(solution)/shard_map/ppermute | solution.py:245
  919.7 9.8 collective-permute-done.46
  956.5 13.4 %collective-permute-done.57 = bf16[64,2688]{1,0:T(8,128)(2,1)S(1)} collective-permute-done((bf16[64,2688]{1,0:T(8,128)(2,1)S(1)}, bf16[64,2688]{1,0:T(8,128)(2,1)S(1)}, u32[]{:S(2)}, u32[]{:S(2)}) %collective-permute-start.57) | collective-permute-done | bytes 344096 | tf_op jit(solution)/shard_map/ppermute | solution.py:241
  1029.7 22.0 %all-gather.9.cloned.1.call-done.first_ref.second_ref = bf16[2048,2048]{1,0:T(8,128)(2,1)} async-done(((bf16[512,2048]{1,0:T(8,128)(2,1)}), bf16[2048,2048]{1,0:T(8,128)(2,1)}) %all-gather.9.cloned.1.call-update) | async-done | bytes 8388624 | tf_op jit(solution)/shard_map/all_gather | solution.py:968
  1051.8 11.3 %join_pair.1 = f32[1024,2,2048]{2,1,0:T(2,128)} custom-call(bf16[2048,2048]{1,0:T(8,128)(2,1)} %all-gather.9.cloned.1.call-done.first_ref.second_ref, bf16[2048,2048]{1,0:T(8,128)(2,1)} %all-gather.9.cloned.1.call-done.first_ref.second_ref), custom_call_target="tpu_custom_call" | custom-call | bytes 25165824 | tf_op jit(solution)/shard_map/join_pair/pallas_call | solution.py:627
  (540 shorter events, 441.4 us)
Async XLA Ops:
  7.2 177.5 %all-gather.5.cloned.1.call-start = ((), (), s32[]{:S(2)}) async-start(), calls=%async_computation.2 | async-start | bytes 17842176 | tf_op jit(solution)/shard_map/all_gather | solution.py:680
  18.4 350.6 %all-gather.7.cloned.1.call-start = ((), (), s32[]{:S(2)}) async-start(), calls=%async_computation.3 | async-start | bytes 2162688 | tf_op jit(solution)/shard_map/all_gather | solution.py:680
  18.7 39.1 %collective-permute-start = (bf16[256,1152]{1,0:T(8,128)(2,1)S(1)}, bf16[256,1152]{1,0:T(8,128)(2,1)S(1)}, u32[]{:S(2)}, u32[]{:S(2)}) collective-permute-start(bf16[256,1152]{1,0:T(8,128)(2,1)S(1)} %pad_maximum_fusion.12.shard_ref), channel_id=1, source_target_pairs={{0,2},{1,3},{2,0},{3,1},{4,6},{5,7},{6,4},{7,5},{8,10},{9,11},{10,... | collective-permute-start | bytes 1769480 | tf_op jit(solution)/shard_map/ppermute | solution.py:245
  21.8 40.4 %collective-permute-start.1 = (bf16[256,1152]{1,0:T(8,128)(2,1)S(1)}, bf16[256,1152]{1,0:T(8,128)(2,1)S(1)}, u32[]{:S(2)}, u32[]{:S(2)}) collective-permute-start(bf16[256,1152]{1,0:T(8,128)(2,1)S(1)} %pad_maximum_fusion.12.shard_ref), channel_id=1, source_target_pairs={{0,4},{1,5},{2,6},{3,7},{4,0},{5,1},{6,2},{7,3},{8,12},{9,13},{10,... | collective-permute-start | bytes 1769480 | tf_op jit(solution)/shard_map/ppermute | solution.py:245
  24.4 39.2 %collective-permute-start.4 = (bf16[256,1152]{1,0:T(8,128)(2,1)S(1)}, bf16[256,1152]{1,0:T(8,128)(2,1)S(1)}, u32[]{:S(2)}, u32[]{:S(2)}) collective-permute-start(bf16[256,1152]{1,0:T(8,128)(2,1)S(1)} %pad_maximum_fusion.12.shard_ref), channel_id=1, source_target_pairs={{2,4},{3,5},{4,2},{5,3},{10,12},{11,13},{12,10},{13,11},{18,20},{1... | collective-permute-start | bytes 1769480 | tf_op jit(solution)/shard_map/ppermute | solution.py:245
  100.6 97.0 %collective-permute-start.10 = (bf16[1024,2048]{1,0:T(8,128)(2,1)}, bf16[1024,2048]{1,0:T(8,128)(2,1)}, u32[]{:S(2)}, u32[]{:S(2)}) collective-permute-start(bf16[1024,2048]{1,0:T(8,128)(2,1)} %convert_element_type.481.refs_5_.refs_6_.refs_7_.refs_8_), channel_id=1, source_target_pairs={{0,1},{1,0},{2,3},{3,2},{4,5},{5,4},{6,7},{7,6},{8,9},{9,8},{10,11... | collective-permute-start | bytes 12582920 | tf_op jit(solution)/shard_map/ppermute | solution.py:238
  100.9 96.7 %collective-permute-start.8 = (bf16[1024,2048]{1,0:T(8,128)(2,1)}, bf16[1024,2048]{1,0:T(8,128)(2,1)}, u32[]{:S(2)}, u32[]{:S(2)}) collective-permute-start(bf16[1024,2048]{1,0:T(8,128)(2,1)} %get-tuple-element.209.refs_1_.refs_2_.refs_3_.refs_4_), channel_id=1, source_target_pairs={{0,1},{1,0},{2,3},{3,2},{4,5},{5,4},{6,7},{7,6},{8,9},{9,8},{10,11... | collective-permute-start | bytes 12582920 | tf_op jit(solution)/shard_map/ppermute | solution.py:238
  101.1 96.5 %collective-permute-start.9 = (bf16[1024,2048]{1,0:T(8,128)(2,1)}, bf16[1024,2048]{1,0:T(8,128)(2,1)}, u32[]{:S(2)}, u32[]{:S(2)}) collective-permute-start(bf16[1024,2048]{1,0:T(8,128)(2,1)} %get-tuple-element.211.refs_3_.refs_4_.refs_5_.refs_6_), channel_id=1, source_target_pairs={{0,1},{1,0},{2,3},{3,2},{4,5},{5,4},{6,7},{7,6},{8,9},{9,8},{10,11... | collective-permute-start | bytes 12582920 | tf_op jit(solution)/shard_map/ppermute | solution.py:238
  201.0 610.1 %reduce-scatter.3.cloned.1.call-start = ((), (), s32[]{:S(2)}) async-start(), calls=%async_computation.4 | async-start | bytes 10485760 | tf_op jit(solution)/shard_map/reduce_scatter | solution.py:950
  234.7 54.7 %collective-permute-start.12 = (bf16[256,2048]{1,0:T(8,128)(2,1)S(1)}, bf16[256,2048]{1,0:T(8,128)(2,1)}, u32[]{:S(2)}, u32[]{:S(2)}) collective-permute-start(bf16[256,2048]{1,0:T(8,128)(2,1)S(1)} %multiply_convert_fusion.refs_0_.refs_3_), channel_id=1, source_target_pairs={{0,2},{1,3},{2,0},{3,1},{4,6},{5,7},{6,4},{7,5},{8,10},{9,11},{10,... | collective-permute-start | bytes 3145736 | tf_op jit(solution)/shard_map/ppermute | solution.py:245
  236.5 57.8 %collective-permute-start.13 = (bf16[256,2048]{1,0:T(8,128)(2,1)S(1)}, bf16[256,2048]{1,0:T(8,128)(2,1)}, u32[]{:S(2)}, u32[]{:S(2)}) collective-permute-start(bf16[256,2048]{1,0:T(8,128)(2,1)S(1)} %multiply_convert_fusion.refs_0_.refs_3_), channel_id=1, source_target_pairs={{0,4},{1,5},{2,6},{3,7},{4,0},{5,1},{6,2},{7,3},{8,12},{9,13},{10,... | collective-permute-start | bytes 3145736 | tf_op jit(solution)/shard_map/ppermute | solution.py:245
  243.5 73.9 %collective-permute-start.15 = (bf16[256,2048]{1,0:T(8,128)(2,1)S(1)}, bf16[256,2048]{1,0:T(8,128)(2,1)}, u32[]{:S(2)}, u32[]{:S(2)}) collective-permute-start(bf16[256,2048]{1,0:T(8,128)(2,1)S(1)} %multiply_convert_fusion.refs_0_.refs_3_), channel_id=1, source_target_pairs={{2,4},{3,5},{4,2},{5,3},{10,12},{11,13},{12,10},{13,11},{18,20},{1... | collective-permute-start | bytes 3145736 | tf_op jit(solution)/shard_map/ppermute | solution.py:245
  321.6 45.2 %collective-permute-start.16 = (bf16[256,2048]{1,0:T(8,128)(2,1)}, bf16[256,2048]{1,0:T(8,128)(2,1)S(1)}, u32[]{:S(2)}, u32[]{:S(2)}) collective-permute-start(bf16[256,2048]{1,0:T(8,128)(2,1)} %get-tuple-element.227), channel_id=1, source_target_pairs={{0,2},{1,3},{2,0},{3,1},{4,6},{5,7},{6,4},{7,5},{8,10},{9,11},{10,... | collective-permute-start | bytes 3145736 | tf_op jit(solution)/shard_map/ppermute | solution.py:245
  323.4 49.5 %collective-permute-start.17 = (bf16[256,2048]{1,0:T(8,128)(2,1)}, bf16[256,2048]{1,0:T(8,128)(2,1)}, u32[]{:S(2)}, u32[]{:S(2)}) collective-permute-start(bf16[256,2048]{1,0:T(8,128)(2,1)} %get-tuple-element.234), channel_id=1, source_target_pairs={{0,4},{1,5},{2,6},{3,7},{4,0},{5,1},{6,2},{7,3},{8,12},{9,13},{10,... | collective-permute-start | bytes 3145736 | tf_op jit(solution)/shard_map/ppermute | solution.py:245
  406.9 66.8 %collective-permute-start.19 = (bf16[256,2048]{1,0:T(8,128)(2,1)S(1)}, bf16[256,2048]{1,0:T(8,128)(2,1)}, u32[]{:S(2)}, u32[]{:S(2)}) collective-permute-start(bf16[256,2048]{1,0:T(8,128)(2,1)S(1)} %get-tuple-element.281.refs_0_.refs_3_), channel_id=1, source_target_pairs={{0,2},{1,3},{2,0},{3,1},{4,6},{5,7},{6,4},{7,5},{8,10},{9,11},{10,... | collective-permute-start | bytes 3145736 | tf_op jit(solution)/shard_map/ppermute | solution.py:245
  429.8 49.5 %collective-permute-start.20 = (bf16[256,2048]{1,0:T(8,128)(2,1)S(1)}, bf16[256,2048]{1,0:T(8,128)(2,1)}, u32[]{:S(2)}, u32[]{:S(2)}) collective-permute-start(bf16[256,2048]{1,0:T(8,128)(2,1)S(1)} %get-tuple-element.281.refs_0_.refs_3_), channel_id=1, source_target_pairs={{0,4},{1,5},{2,6},{3,7},{4,0},{5,1},{6,2},{7,3},{8,12},{9,13},{10,... | collective-permute-start | bytes 3145736 | tf_op jit(solution)/shard_map/ppermute | solution.py:245
  431.1 74.3 %collective-permute-start.22 = (bf16[256,2048]{1,0:T(8,128)(2,1)S(1)}, bf16[256,2048]{1,0:T(8,128)(2,1)}, u32[]{:S(2)}, u32[]{:S(2)}) collective-permute-start(bf16[256,2048]{1,0:T(8,128)(2,1)S(1)} %get-tuple-element.281.refs_0_.refs_3_), channel_id=1, source_target_pairs={{2,4},{3,5},{4,2},{5,3},{10,12},{11,13},{12,10},{13,11},{18,20},{1... | collective-permute-start | bytes 3145736 | tf_op jit(solution)/shard_map/ppermute | solution.py:245
  507.8 44.0 %collective-permute-start.23 = (bf16[256,2048]{1,0:T(8,128)(2,1)}, bf16[256,2048]{1,0:T(8,128)(2,1)S(1)}, u32[]{:S(2)}, u32[]{:S(2)}) collective-permute-start(bf16[256,2048]{1,0:T(8,128)(2,1)} %get-tuple-element.256), channel_id=1, source_target_pairs={{0,2},{1,3},{2,0},{3,1},{4,6},{5,7},{6,4},{7,5},{8,10},{9,11},{10,... | collective-permute-start | bytes 3145736 | tf_op jit(solution)/shard_map/ppermute | solution.py:245
  511.4 78.4 %collective-permute-start.24 = (bf16[256,2048]{1,0:T(8,128)(2,1)}, bf16[256,2048]{1,0:T(8,128)(2,1)}, u32[]{:S(2)}, u32[]{:S(2)}) collective-permute-start(bf16[256,2048]{1,0:T(8,128)(2,1)} %get-tuple-element.266), channel_id=1, source_target_pairs={{0,4},{1,5},{2,6},{3,7},{4,0},{5,1},{6,2},{7,3},{8,12},{9,13},{10,... | collective-permute-start | bytes 3145736 | tf_op jit(solution)/shard_map/ppermute | solution.py:245
  617.1 62.9 %collective-permute-start.30 = (bf16[1024,2048]{1,0:T(8,128)(2,1)}, bf16[1024,2048]{1,0:T(8,128)(2,1)}, u32[]{:S(2)}, u32[]{:S(2)}) collective-permute-start(bf16[1024,2048]{1,0:T(8,128)(2,1)} %outer_blocks.11), channel_id=1, source_target_pairs={{0,1},{1,0},{2,3},{3,2},{4,5},{5,4},{6,7},{7,6},{8,9},{9,8},{10,11... | collective-permute-start | bytes 12582920 | tf_op jit(solution)/shard_map/ppermute | solution.py:238
  617.3 62.8 %collective-permute-start.31 = (bf16[1024,2048]{1,0:T(8,128)(2,1)}, bf16[1024,2048]{1,0:T(8,128)(2,1)}, u32[]{:S(2)}, u32[]{:S(2)}) collective-permute-start(bf16[1024,2048]{1,0:T(8,128)(2,1)} %outer_blocks.12), channel_id=1, source_target_pairs={{0,1},{1,0},{2,3},{3,2},{4,5},{5,4},{6,7},{7,6},{8,9},{9,8},{10,11... | collective-permute-start | bytes 12582920 | tf_op jit(solution)/shard_map/ppermute | solution.py:238
  625.8 54.2 %collective-permute-start.29 = (bf16[256,2688]{1,0:T(8,128)(2,1)}, bf16[256,2688]{1,0:T(8,128)(2,1)S(1)}, u32[]{:S(2)}, u32[]{:S(2)}) collective-permute-start(bf16[256,2688]{1,0:T(8,128)(2,1)} %pad_maximum_fusion.2), channel_id=1, source_target_pairs={{0,2},{1,3},{6,4},{7,5},{8,10},{9,11},{14,12},{15,13},{16,18},{17,... | collective-permute-start | bytes 4128776 | tf_op jit(solution)/shard_map/ppermute | solution.py:245
  721.9 145.0 %reduce-scatter.5.cloned.1.call-start = ((), (), s32[]{:S(2)}) async-start(), calls=%async_computation.5 | async-start | bytes 5242880 | tf_op jit(solution)/shard_map/reduce_scatter | solution.py:915
  722.5 300.6 %all-gather.11.cloned.1.call-start = ((), (), s32[]{:S(2)}) async-start(), calls=%async_computation.7 | async-start | bytes 5242880 | tf_op jit(solution)/shard_map/all_gather | solution.py:998
  722.5 76.9 %collective-permute-start.38 = (bf16[1024,2048]{1,0:T(8,128)(2,1)}, bf16[1024,2048]{1,0:T(8,128)(2,1)}, u32[]{:S(2)}, u32[]{:S(2)}) collective-permute-start(bf16[1024,2048]{1,0:T(8,128)(2,1)} %outer_blocks.18), channel_id=1, source_target_pairs={{0,1},{1,0},{2,3},{3,2},{4,5},{5,4},{6,7},{7,6},{8,9},{9,8},{10,11... | collective-permute-start | bytes 12582920 | tf_op jit(solution)/shard_map/ppermute | solution.py:238
  740.5 58.1 %collective-permute-start.37 = (bf16[256,1024]{1,0:T(8,128)(2,1)S(1)}, bf16[256,1024]{1,0:T(8,128)(2,1)S(1)}, u32[]{:S(2)}, u32[]{:S(2)}) collective-permute-start(bf16[256,1024]{1,0:T(8,128)(2,1)S(1)} %convert_element_type.555), channel_id=1, source_target_pairs={{4,0},{5,1},{6,2},{7,3},{12,8},{13,9},{14,10},{15,11},{20,16},{21,... | collective-permute-start | bytes 1572872 | tf_op jit(solution)/shard_map/ppermute | solution.py:245
  743.2 103.7 %collective-permute-start.36 = (bf16[256,2688]{1,0:T(8,128)(2,1)}, bf16[256,2688]{1,0:T(8,128)(2,1)}, u32[]{:S(2)}, u32[]{:S(2)}) collective-permute-start(bf16[256,2688]{1,0:T(8,128)(2,1)} %add_convert_fusion.1), channel_id=1, source_target_pairs={{0,4},{1,5},{2,6},{3,7},{4,0},{5,1},{6,2},{7,3},{8,12},{9,13},{10,... | collective-permute-start | bytes 4128776 | tf_op jit(solution)/shard_map/ppermute | solution.py:245
  815.6 51.3 %collective-permute-start.39 = (bf16[256,2048]{1,0:T(8,128)(2,1)}, bf16[256,2048]{1,0:T(8,128)(2,1)}, u32[]{:S(2)}, u32[]{:S(2)}) collective-permute-start(bf16[256,2048]{1,0:T(8,128)(2,1)} %get-tuple-element.454), channel_id=1, source_target_pairs={{0,2},{1,3},{6,4},{7,5},{8,10},{9,11},{14,12},{15,13},{16,18},{17,... | collective-permute-start | bytes 3145736 | tf_op jit(solution)/shard_map/ppermute | solution.py:245
  820.0 46.9 %collective-permute-start.41 = (bf16[256,2048]{1,0:T(8,128)(2,1)}, bf16[256,2048]{1,0:T(8,128)(2,1)}, u32[]{:S(2)}, u32[]{:S(2)}) collective-permute-start(bf16[256,2048]{1,0:T(8,128)(2,1)} %get-tuple-element.454), channel_id=1, source_target_pairs={{2,4},{3,5},{4,2},{5,3},{10,12},{11,13},{12,10},{13,11},{18,20},{1... | collective-permute-start | bytes 3145736 | tf_op jit(solution)/shard_map/ppermute | solution.py:245
  866.9 184.8 %all-gather.9.cloned.1.call-start = ((), (), s32[]{:S(2)}) async-start(), calls=%async_computation.6 | async-start | bytes 10485760 | tf_op jit(solution)/shard_map/all_gather | solution.py:968
  870.2 49.4 %collective-permute-start.44 = (bf16[256,2048]{1,0:T(8,128)(2,1)S(1)}, bf16[256,2048]{1,0:T(8,128)(2,1)S(1)}, u32[]{:S(2)}, u32[]{:S(2)}) collective-permute-start(bf16[256,2048]{1,0:T(8,128)(2,1)S(1)} %add_convert_fusion.4), channel_id=1, source_target_pairs={{0,4},{1,5},{2,6},{3,7},{4,0},{5,1},{6,2},{7,3},{8,12},{9,13},{10,... | collective-permute-start | bytes 3145736 | tf_op jit(solution)/shard_map/ppermute | solution.py:245
  879.7 49.8 %collective-permute-start.45 = (bf16[256,1152]{1,0:T(8,128)(2,1)S(1)}, bf16[256,1152]{1,0:T(8,128)(2,1)S(1)}, u32[]{:S(2)}, u32[]{:S(2)}) collective-permute-start(bf16[256,1152]{1,0:T(8,128)(2,1)S(1)} %pad_maximum_fusion.13), channel_id=1, source_target_pairs={{0,2},{1,3},{6,4},{7,5},{8,10},{9,11},{14,12},{15,13},{16,18},{17,... | collective-permute-start | bytes 1769480 | tf_op jit(solution)/shard_map/ppermute | solution.py:245
  (139 other events, 1792.6 us)
Sparse Core Ops, SparseCore 0:
  18.5 144.2 all-gather.4
  201.1 95.3 all-gather.6
  722.0 89.0 reduce-scatter.2
  814.2 52.6 reduce-scatter.4
  868.6 66.0 all-gather.10
  936.4 115.2 all-gather.8
